TPU v7x, 128 devices: a whole 4x4x4 slice. The times are simulated.
128 devices in a mesh: row: 8 (over y_hi, x), col: 16 (over y_lo, z, core).
Axes of the slice: x: 4, y: 4 (y_hi: 2, y_lo: 2; y = y_hi * 2 + y_lo), z: 4, core: 2. Of those that a mesh axis runs over, the one named last changes fastest.
Arguments:
- right_side: float32 [16, 512, 512], P('col', 'row'), may hold values from -6 to 6
- affinity_blocks: float32 [16, 16, 8, 128, 128], P('row', 'col'), may hold values from -0.03125 to 0.03125
- block_coords: int32 [16, 16, 8, 2], P('row', 'col'), may hold values from 0 to 3
- block_counts: int32 [16, 16], P('row', 'col'), may hold values from 4 to 8, as said below
Outputs:
- ranking: float32 [16, 512, 512], P('col', 'row')
- residual: float32 [16, 512, 512], P('col', 'row')
Inputs may be any that keep to these rules, and one draw needn't show every extreme that they name: `block_counts`: some grid tile holds 8 live blocks in every draw.
All inputs are finite; a program needn't handle non-finite values.
Results may differ from a plain program's by a relative error of at most 0.0003.
Values sent between devices are 32-bit elements; how exact they have to be, the bound alone decides.
No kernel may reach another device: no remote copies, remote signals or barrier semaphores. Data moves between devices by JAX's collectives and lax.ppermute only.
A program may use at most 64 MiB of HBM per device.

v0:
```python
import jax
import jax.numpy as jnp
from jax import lax
from jax.sharding import PartitionSpec as P

ITERS = 3


diffusion = 0.8


def broadcast(value, axis, source):
    kept = jnp.where(lax.axis_index(axis) == source, value, 0).astype(value.dtype)
    return lax.psum(kept, axis)


def live_blocks(blocks, count):
    live = (jnp.arange(blocks.shape[0], dtype=jnp.int32) < count).astype(blocks.dtype)
    return blocks * live[:, None, None]


def forward_only(masked, rows, cols, column_field):
    position = jnp.arange(column_field.shape[0], dtype=jnp.int32)
    picked = jnp.take(column_field, cols, axis=0)
    product = jnp.einsum("kab,kbw->kaw", masked, picked, precision=lax.Precision.HIGHEST)
    row_onehot = (rows[None, :] == position[:, None]).astype(jnp.float32)
    return jnp.einsum("tk,kaw->taw", row_onehot, product, precision=lax.Precision.HIGHEST)


def backward_only(masked, rows, cols, row_field):
    position = jnp.arange(row_field.shape[0], dtype=jnp.int32)
    chosen = jnp.take(row_field, rows, axis=0)
    mirrored = jnp.einsum("kab,kaw->kbw", masked, chosen, precision=lax.Precision.HIGHEST)
    col_onehot = (cols[None, :] == position[:, None]).astype(jnp.float32)
    return jnp.einsum("tk,kbw->tbw", col_onehot, mirrored, precision=lax.Precision.HIGHEST)


def tile_products(masked, rows, cols, column_field, row_field):
    forward = forward_only(masked, rows, cols, column_field)
    backward = backward_only(masked, rows, cols, row_field)
    return (forward, backward)


def block_products(affinity_blocks, block_coords, block_counts, column_block, row_blocks):
    members = affinity_blocks.shape[0]
    edge = affinity_blocks.shape[-1]
    width = column_block.shape[1]
    column_field = column_block.reshape(-1, edge, width)
    forward_parts = []
    backward_total = jnp.zeros(column_field.shape, jnp.float32)
    for member in range(members):
        masked = live_blocks(affinity_blocks[member, 0], block_counts[member, 0])
        forward, backward = tile_products(
            masked,
            block_coords[member, 0, :, 0],
            block_coords[member, 0, :, 1],
            column_field,
            row_blocks[member].reshape(column_field.shape),
        )
        forward_parts.append(forward.reshape(column_block.shape))
        backward_total = backward_total + backward
    return (jnp.stack(forward_parts), backward_total.reshape(column_block.shape))


def operate(piece, affinity_blocks, block_coords, block_counts):
    rows_count = lax.axis_size("row")
    cols_count = lax.axis_size("col")
    members = cols_count // rows_count
    my_row = lax.axis_index("row")
    share = piece.shape[1]
    width = piece.shape[2]
    sliver = share // cols_count
    whole = lax.all_gather(piece, "row", axis=1, tiled=True)
    received = []
    for member in range(members):
        received.append(broadcast(whole[0], "col", my_row * members + member))
    row_blocks = jnp.stack(received)
    forward, backward = block_products(
        affinity_blocks, block_coords, block_counts, whole[0], row_blocks
    )
    back_part = lax.psum_scatter(backward[None], "row", scatter_dimension=1, tiled=True)
    spread = forward.reshape(members, rows_count, cols_count, sliver, width)
    summed = lax.psum_scatter(spread, "col", scatter_dimension=2, tiled=True)
    ordered = summed.reshape(members, rows_count, sliver, width).transpose(1, 0, 2, 3)
    ordered = ordered.reshape(rows_count * members, sliver, width)
    forward_part = lax.all_to_all(
        lax.all_to_all(ordered, "row", split_axis=0, concat_axis=0, tiled=True),
        "col",
        split_axis=0,
        concat_axis=1,
        tiled=True,
    )
    return piece - diffusion * (forward_part + back_part)


def squares(residual):
    return lax.psum(jnp.sum(residual * residual, axis=(0, 1)), ("row", "col"))


def shards(right_side, affinity_blocks, block_coords, block_counts):
    ranking = jnp.zeros_like(right_side)
    residual = right_side
    direction = right_side
    norm_now = squares(residual)
    for step in range(ITERS):
        image = operate(direction, affinity_blocks, block_coords, block_counts)
        curve = lax.psum(jnp.sum(direction * image, axis=(0, 1)), ("row", "col"))
        alpha = norm_now / curve
        ranking = ranking + alpha * direction
        residual = residual - alpha * image
        if step + 1 < ITERS:
            norm_next = squares(residual)
            direction = residual + norm_next / norm_now * direction
            norm_now = norm_next
    return (ranking, residual)


def solution(mesh):
    in_specs = (
        P("col", "row", None),
        P("row", "col", None, None, None),
        P("row", "col", None, None),
        P("row", "col"),
    )
    out_specs = (P("col", "row", None), P("col", "row", None))
    return jax.shard_map(shards, mesh=mesh, in_specs=in_specs, out_specs=out_specs, check_vma=False)
```

profile of v0, /device:TPU:0, one launch (start us, length us, event | category | flops | bytes accessed | tf_op | source)
XLA Modules:
  0.0 1282.3 jit_solution(11291299337467463532)
XLA Ops:
  9.9 50.2 %all-gather.4.cloned.1.call-done = f32[1,512,512]{2,1,0:T(8,128)} async-done(((f32[1,64,512]{2,1,0:T(8,128)}), f32[1,512,512]{2,1,0:T(8,128)}) %all-gather.4.cloned.1.call-update) | async-done | bytes 1048592 | tf_op jit(solution)/shard_map/all_gather | solution.py:73
  87.7 98.0 %all-reduce.12.cloned.1.call-done = (f32[4,128,512]{2,1,0:T(8,128)}, f32[4,128,512]{2,1,0:T(8,128)}) async-done(((f32[4,128,512]{2,1,0:T(8,128)}, f32[4,128,512]{2,1,0:T(8,128)}), (f32[4,128,512]{2,1,0:T(8,128)}, f32[4,128,512]{2,1,0:T(8,128)})) %all-reduce.12.cloned.1.call-update) | async-done | bytes 2097168 | tf_op jit(solution)/shard_map/psum | solution.py:14
  202.6 49.9 %reduce-scatter.7.cloned.1.call-done = f32[2,8,1,4,512]{4,1,3,0,2:T(8,128)} async-done(((f32[2,8,16,4,512]{4,1,3,0,2:T(8,128)}), f32[2,8,1,4,512]{4,1,3,0,2:T(8,128)}) %reduce-scatter.7.cloned.1.call-update) | async-done | bytes 131088 | tf_op jit(solution)/shard_map/reduce_scatter | solution.py:83
  253.4 14.3 %all_to_all.51 = f32[16,4,512]{2,1,0:T(4,128)S(1)} all-to-all(f32[16,4,512]{2,1,0:T(4,128)S(1)} %bitcast.97), channel_id=1, replica_groups=mesh['row'=8,'col'=16] {'row'}, dimensions={0} | all-to-all | bytes 262144 | tf_op jit(solution)/shard_map/all_to_all | solution.py:87
  267.7 9.3 all_to_all.52
  277.1 49.2 %reduce-scatter.9.cloned.1.call-done = f32[1,64,512]{2,1,0:T(8,128)} async-done(((f32[1,512,512]{2,1,0:T(8,128)}), f32[1,64,512]{2,1,0:T(8,128)}) %reduce-scatter.9.cloned.1.call-update) | async-done | bytes 131088 | tf_op jit(solution)/shard_map/reduce_scatter | solution.py:81
  327.2 64.9 %all-reduce = (f32[512]{0:T(512)S(1)}, f32[512]{0:T(512)S(1)}) all-reduce(f32[512]{0:T(512)S(1)} %get-tuple-element.4, f32[512]{0:T(512)S(1)} %get-tuple-element.3), channel_id=1, replica_groups=mesh['row'=8,'col'=16] {'row','col'}, use_global_device_ids=true, to_apply=%region_1.0 | all-reduce | flops 1024 | bytes 8192 | tf_op jit(solution)/shard_map/psum | solution.py:97
  393.1 62.0 %psum.88 = f32[512]{0:T(512)S(1)} all-reduce(f32[512]{0:T(512)S(1)} %get-tuple-element.15), channel_id=1, replica_groups=mesh['row'=8,'col'=16] {'row','col'}, use_global_device_ids=true, to_apply=%region_9.11 | all-reduce | flops 512 | bytes 4096 | tf_op jit(solution)/shard_map/psum | solution.py:97
  455.9 44.6 %all-gather.6.cloned.1.call-done = f32[1,512,512]{2,1,0:T(8,128)} async-done(((f32[1,64,512]{2,1,0:T(8,128)}), f32[1,512,512]{2,1,0:T(8,128)}) %all-gather.6.cloned.1.call-update) | async-done | bytes 1048592 | tf_op jit(solution)/shard_map/all_gather | solution.py:73
  528.3 97.7 %all-reduce.10.cloned.1.call-done = (f32[4,128,512]{2,1,0:T(8,128)}, f32[4,128,512]{2,1,0:T(8,128)}) async-done(((f32[4,128,512]{2,1,0:T(8,128)}, f32[4,128,512]{2,1,0:T(8,128)}), (f32[4,128,512]{2,1,0:T(8,128)}, f32[4,128,512]{2,1,0:T(8,128)})) %all-reduce.10.cloned.1.call-update) | async-done | bytes 2097168 | tf_op jit(solution)/shard_map/psum | solution.py:14
  631.2 3.7 fusion.32
  643.1 49.9 %reduce-scatter.11.cloned.1.call-done = f32[2,8,1,4,512]{4,1,3,0,2:T(8,128)} async-done(((f32[2,8,16,4,512]{4,1,3,0,2:T(8,128)}), f32[2,8,1,4,512]{4,1,3,0,2:T(8,128)}) %reduce-scatter.11.cloned.1.call-update) | async-done | bytes 131088 | tf_op jit(solution)/shard_map/reduce_scatter | solution.py:83
  694.0 14.4 %all_to_all.53 = f32[16,4,512]{2,1,0:T(4,128)S(1)} all-to-all(f32[16,4,512]{2,1,0:T(4,128)S(1)} %bitcast.98), channel_id=1, replica_groups=mesh['row'=8,'col'=16] {'row'}, dimensions={0} | all-to-all | bytes 262144 | tf_op jit(solution)/shard_map/all_to_all | solution.py:87
  708.4 9.3 all_to_all.54
  717.7 49.7 %reduce-scatter.13.cloned.1.call-done = f32[1,64,512]{2,1,0:T(8,128)} async-done(((f32[1,512,512]{2,1,0:T(8,128)}), f32[1,64,512]{2,1,0:T(8,128)}) %reduce-scatter.13.cloned.1.call-update) | async-done | bytes 131088 | tf_op jit(solution)/shard_map/reduce_scatter | solution.py:81
  768.3 64.9 %psum.91 = f32[512]{0:T(512)S(1)} all-reduce(f32[512]{0:T(512)S(1)} %multiply_reduce_fusion.2), channel_id=1, replica_groups=mesh['row'=8,'col'=16] {'row','col'}, use_global_device_ids=true, to_apply=%region_15.17 | all-reduce | flops 512 | bytes 4096 | tf_op jit(solution)/shard_map/psum | solution.py:107
  834.2 62.0 %psum.92 = f32[512]{0:T(512)S(1)} all-reduce(f32[512]{0:T(512)S(1)} %get-tuple-element.13), channel_id=1, replica_groups=mesh['row'=8,'col'=16] {'row','col'}, use_global_device_ids=true, to_apply=%region_17.19 | all-reduce | flops 512 | bytes 4096 | tf_op jit(solution)/shard_map/psum | solution.py:97
  897.0 44.6 %all-gather.8.cloned.1.call-done = f32[1,512,512]{2,1,0:T(8,128)} async-done(((f32[1,64,512]{2,1,0:T(8,128)}), f32[1,512,512]{2,1,0:T(8,128)}) %all-gather.8.cloned.1.call-update) | async-done | bytes 1048592 | tf_op jit(solution)/shard_map/all_gather | solution.py:73
  969.8 97.3 %all-reduce.8.cloned.1.call-done = (f32[4,128,512]{2,1,0:T(8,128)}, f32[4,128,512]{2,1,0:T(8,128)}) async-done(((f32[4,128,512]{2,1,0:T(8,128)}, f32[4,128,512]{2,1,0:T(8,128)}), (f32[4,128,512]{2,1,0:T(8,128)}, f32[4,128,512]{2,1,0:T(8,128)})) %all-reduce.8.cloned.1.call-update) | async-done | bytes 2097168 | tf_op jit(solution)/shard_map/psum | solution.py:14
  1084.4 49.5 %reduce-scatter.15.cloned.1.call-done = f32[2,8,1,4,512]{4,1,3,0,2:T(8,128)} async-done(((f32[2,8,16,4,512]{4,1,3,0,2:T(8,128)}), f32[2,8,1,4,512]{4,1,3,0,2:T(8,128)}) %reduce-scatter.15.cloned.1.call-update) | async-done | bytes 131088 | tf_op jit(solution)/shard_map/reduce_scatter | solution.py:83
  1134.9 14.3 %all_to_all.55 = f32[16,4,512]{2,1,0:T(4,128)S(1)} all-to-all(f32[16,4,512]{2,1,0:T(4,128)S(1)} %bitcast.99), channel_id=1, replica_groups=mesh['row'=8,'col'=16] {'row'}, dimensions={0} | all-to-all | bytes 262144 | tf_op jit(solution)/shard_map/all_to_all | solution.py:87
  1149.2 9.3 all_to_all.56
  1158.5 49.2 %reduce-scatter.17.cloned.1.call-done = f32[1,64,512]{2,1,0:T(8,128)} async-done(((f32[1,512,512]{2,1,0:T(8,128)}), f32[1,64,512]{2,1,0:T(8,128)}) %reduce-scatter.17.cloned.1.call-update) | async-done | bytes 131088 | tf_op jit(solution)/shard_map/reduce_scatter | solution.py:81
  1208.7 64.9 %psum.95 = f32[512]{0:T(512)S(1)} all-reduce(f32[512]{0:T(512)S(1)} %multiply_reduce_fusion), channel_id=1, replica_groups=mesh['row'=8,'col'=16] {'row','col'}, use_global_device_ids=true, to_apply=%region_23.25 | all-reduce | flops 512 | bytes 4096 | tf_op jit(solution)/shard_map/psum | solution.py:107
  (183 shorter events, 144.1 us)
Async XLA Ops:
  7.2 52.9 %all-gather.4.cloned.1.call-start = ((), (), s32[]{:S(2)}) async-start(), calls=%async_computation.12 | async-start | bytes 1179648 | tf_op jit(solution)/shard_map/all_gather | solution.py:73
  7.9 177.7 %all-reduce.12.cloned.1.call-start = ((), (), s32[]{:S(2)}) async-start(), calls=%async_computation.23 | async-start | bytes 4194304 | tf_op jit(solution)/shard_map/psum | solution.py:14
  63.1 189.4 %reduce-scatter.7.cloned.1.call-start = ((), (), s32[]{:S(2)}) async-start(), calls=%async_computation.13 | async-start | bytes 2228224 | tf_op jit(solution)/shard_map/reduce_scatter | solution.py:83
  63.8 444.2 %copy-start.22 = (pred[8]{0:T(512)(128)(4,1)}, pred[8]{0:T(512)(128)(4,1)S(1)}, u32[]{:S(2)}) copy-start(pred[8]{0:T(512)(128)(4,1)S(1)} %get-tuple-element.37) | copy-start | bytes 28
  63.8 454.0 %copy-start.20 = (pred[8]{0:T(512)(128)(4,1)}, pred[8]{0:T(512)(128)(4,1)S(1)}, u32[]{:S(2)}) copy-start(pred[8]{0:T(512)(128)(4,1)S(1)} %get-tuple-element.41) | copy-start | bytes 28
  63.8 567.3 %copy-start.18 = (pred[8]{0:T(512)(128)(4,1)}, pred[8]{0:T(512)(128)(4,1)S(1)}, u32[]{:S(2)}) copy-start(pred[8]{0:T(512)(128)(4,1)S(1)} %get-tuple-element.39) | copy-start | bytes 28
  63.8 573.3 %copy-start.16 = (pred[8]{0:T(512)(128)(4,1)}, pred[8]{0:T(512)(128)(4,1)S(1)}, u32[]{:S(2)}) copy-start(pred[8]{0:T(512)(128)(4,1)S(1)} %get-tuple-element.17) | copy-start | bytes 28
  63.9 440.0 %copy-start.36 = (s32[1024]{0:T(1024)}, s32[1024]{0:T(1024)S(1)}, u32[]{:S(2)}) copy-start(s32[1024]{0:T(1024)S(1)} %get-tuple-element.47) | copy-start | bytes 12292
  63.9 442.1 %copy-start.35 = (s32[1024]{0:T(1024)}, s32[1024]{0:T(1024)S(1)}, u32[]{:S(2)}) copy-start(s32[1024]{0:T(1024)S(1)} %get-tuple-element.48) | copy-start | bytes 12292
  63.9 447.8 %copy-start.31 = (s32[8]{0:T(128)}, s32[8]{0:T(128)S(1)}, u32[]{:S(2)}) copy-start(s32[8]{0:T(128)S(1)} %get-tuple-element.36) | copy-start | bytes 100
  63.9 455.9 %copy-start.29 = (s32[8]{0:T(128)}, s32[8]{0:T(128)S(1)}, u32[]{:S(2)}) copy-start(s32[8]{0:T(128)S(1)} %get-tuple-element.34) | copy-start | bytes 100
  63.9 571.0 %copy-start.27 = (s32[8]{0:T(128)}, s32[8]{0:T(128)S(1)}, u32[]{:S(2)}) copy-start(s32[8]{0:T(128)S(1)} %get-tuple-element.35) | copy-start | bytes 100
  63.9 575.4 %copy-start.24 = (s32[8]{0:T(128)}, s32[8]{0:T(128)S(1)}, u32[]{:S(2)}) copy-start(s32[8]{0:T(128)S(1)} %get-tuple-element.33) | copy-start | bytes 100
  87.4 238.9 %reduce-scatter.9.cloned.1.call-start = ((), (), s32[]{:S(2)}) async-start(), calls=%async_computation.14 | async-start | bytes 1179648 | tf_op jit(solution)/shard_map/reduce_scatter | solution.py:81
  87.6 538.4 %copy-start.34 = (s32[1024]{0:T(1024)}, s32[1024]{0:T(1024)S(1)}, u32[]{:S(2)}) copy-start(s32[1024]{0:T(1024)S(1)} %get-tuple-element.45) | copy-start | bytes 12292
  87.6 541.6 %copy-start.33 = (s32[1024]{0:T(1024)}, s32[1024]{0:T(1024)S(1)}, u32[]{:S(2)}) copy-start(s32[1024]{0:T(1024)S(1)} %get-tuple-element.46) | copy-start | bytes 12292
  202.5 297.9 %all-gather.6.cloned.1.call-start = ((), (), s32[]{:S(2)}) async-start(), calls=%async_computation.15 | async-start | bytes 1179648 | tf_op jit(solution)/shard_map/all_gather | solution.py:73
  455.8 170.2 %all-reduce.10.cloned.1.call-start = ((), (), s32[]{:S(2)}) async-start(), calls=%async_computation.22 | async-start | bytes 4194304 | tf_op jit(solution)/shard_map/psum | solution.py:14
  503.4 189.5 %reduce-scatter.11.cloned.1.call-start = ((), (), s32[]{:S(2)}) async-start(), calls=%async_computation.16 | async-start | bytes 2228224 | tf_op jit(solution)/shard_map/reduce_scatter | solution.py:83
  528.1 239.3 %reduce-scatter.13.cloned.1.call-start = ((), (), s32[]{:S(2)}) async-start(), calls=%async_computation.17 | async-start | bytes 1179648 | tf_op jit(solution)/shard_map/reduce_scatter | solution.py:81
  643.0 298.5 %all-gather.8.cloned.1.call-start = ((), (), s32[]{:S(2)}) async-start(), calls=%async_computation.18 | async-start | bytes 1179648 | tf_op jit(solution)/shard_map/all_gather | solution.py:73
  896.9 170.2 %all-reduce.8.cloned.1.call-start = ((), (), s32[]{:S(2)}) async-start(), calls=%async_computation.21 | async-start | bytes 4194304 | tf_op jit(solution)/shard_map/psum | solution.py:14
  944.5 189.4 %reduce-scatter.15.cloned.1.call-start = ((), (), s32[]{:S(2)}) async-start(), calls=%async_computation.19 | async-start | bytes 2228224 | tf_op jit(solution)/shard_map/reduce_scatter | solution.py:83
  969.5 238.2 %reduce-scatter.17.cloned.1.call-start = ((), (), s32[]{:S(2)}) async-start(), calls=%async_computation.20 | async-start | bytes 1179648 | tf_op jit(solution)/shard_map/reduce_scatter | solution.py:81
  (25 other events, 984.8 us)
Sparse Core Ops, SparseCore 0:
  10.3 49.7 all-gather.3
  63.2 122.3 all-reduce.11
  188.0 64.3 reduce-scatter.6
  256.0 70.2 reduce-scatter.8
  456.0 44.4 all-gather.5
  503.6 122.4 all-reduce.9
  628.5 64.3 reduce-scatter.10
  697.0 70.2 reduce-scatter.12
  897.0 44.4 all-gather.7
  944.7 122.3 all-reduce.7
  1069.5 64.3 reduce-scatter.14
  1137.4 70.2 reduce-scatter.16
where the time goes:
time: 1290 us; the launch traced here: 1280 us
  waiting for transfers between devices  731 us (57%)
  blocking collectives  390 us (30%)
  matrix products  62.8 us (5%)
  local copies, waits for them, and re-layouts  59 us (5%)
  other arithmetic  23.3 us (2%)
  between operations  15.1 us (1%)
    psum x3, waiting for transfers between devices, broadcast(): return lax.psum(kept, axis)  293 us
    psum x3, blocking collectives, squares(): return lax.psum(jnp.sum(residual * residual, axis=(0, 1)), ('row', 'col'))  189 us
    reduce_scatter x3, waiting for transfers between devices, operate(): summed = lax.psum_scatter(spread, 'col', scatter_dimension=2, tiled=True)  149 us
    reduce_scatter x3, waiting for transfers between devices, operate(): lax.psum_scatter(backward[None], 'row', scatter_dimension=1, tiled=True)  148 us
    all_gather x3, waiting for transfers between devices, operate(): whole = lax.all_gather(piece, 'row', axis=1, tiled=True)  139 us
    psum x2, blocking collectives, shards(): curve = lax.psum(jnp.sum(direction * image, axis=(0, 1)), ('row', 'col'))  130 us
    all_to_all x3, blocking collectives, operate(): lax.all_to_all(ordered, 'row', split_axis=0, concat_axis=0, tiled=True)  43 us
    all_to_all x3, blocking collectives, operate(): lax.all_to_all(lax.all_to_all(ordered, 'row', split_axis=0, concat_axis=0...  27.9 us
  transfers between devices with their start and end apart: 12, of which 12 were waited for; matrix products, arithmetic and copies ran while one was open for 10% of the time, Pallas kernels for 0%

commit v1 on v0

v1 whole, which is shorter than its diff:
```python
import functools

import jax
import jax.numpy as jnp
from jax import lax
from jax.experimental import pallas as pl
from jax.experimental.pallas import tpu as pltpu
from jax.sharding import PartitionSpec as P

ITERS = 3
DIFFUSION = 0.8
RC = ("row", "col")


def split_id(device):
    r, c = divmod(device, 16)
    yh, x = divmod(r, 4)
    yl, q = divmod(c, 8)
    return yh * 2 + yl, x, q // 2, q % 2


def device_id(y, x, z, k):
    return ((y // 2) * 4 + x) * 16 + (y % 2) * 8 + z * 2 + k


def groups_by(key):
    groups = {}
    for device in range(128):
        groups.setdefault(key(*split_id(device)), []).append(device)
    return list(groups.values())


PLANES = groups_by(lambda y, x, z, k: (y, k))
SHEETS = groups_by(lambda y, x, z, k: (x, k))


def shift_y(d):
    pairs = []
    for device in range(128):
        y, x, z, k = split_id(device)
        pairs.append((device, device_id((y + d) % 4, x, z, k)))
    return pairs


SWAP = [(device, device ^ 1) for device in range(128)]


def exchange(send, groups):
    return lax.all_to_all(send, RC, 0, 0, axis_index_groups=groups, tiled=True)


def call(body, limit=16, **kw):
    return pl.pallas_call(
        body, compiler_params=pltpu.CompilerParams(vmem_limit_bytes=limit * 2**20), **kw
    )


def assemble_body(codes, own, left, right, far0, far1, hi, lo, dense):
    step = pl.program_id(0)

    @pl.when(step == 0)
    def _():
        dense[...] = jnp.zeros_like(dense)
        y = codes[64]
        pieces = ((own, 0, 0, 16), (left, 1, 0, 16), (right, 3, 0, 16), (far0, 2, 0, 8), (far1, 2, 8, 8))
        for ref, shift, first, count in pieces:
            base = ((y - shift) & 3) * 16 + first

            def put(b, carry, ref=ref, base=base):
                code = codes[base + b]

                @pl.when(code >= 0)
                def _():
                    ro = pl.multiple_of((code >> 3) * 128, 128)
                    co = pl.multiple_of((code & 7) * 128, 128)
                    dense[pl.ds(ro, 128), pl.ds(co, 128)] += ref[b]

                return carry

            lax.fori_loop(0, count, put, 0)

    def narrow(i, carry):
        rows = pl.ds(pl.multiple_of(i * 32, 32), 32)
        value = dense[pl.ds(pl.multiple_of(step * 256 + i * 32, 32), 32), :]
        top = value.astype(jnp.bfloat16)
        hi[rows, :] = top
        lo[rows, :] = (value - top.astype(jnp.float32)).astype(jnp.bfloat16)
        return carry

    lax.fori_loop(0, 8, narrow, 0)


def whole(*shape):
    return pl.BlockSpec(shape, lambda i: (0,) * len(shape))


def assemble(codes, own, left, right, far0, far1):
    half = jax.ShapeDtypeStruct((2048, 1024), jnp.bfloat16)
    return call(
        assemble_body,
        limit=26,
        grid=(8,),
        out_shape=(half, half),
        in_specs=[pl.BlockSpec(memory_space=pltpu.SMEM)]
        + [whole(16, 128, 128)] * 3
        + [whole(8, 128, 128)] * 2,
        out_specs=(pl.BlockSpec((256, 1024), lambda i: (i, 0)),) * 2,
        scratch_shapes=[pltpu.VMEM((2048, 1024), jnp.float32)],
        name="assemble",
    )(codes, own, left, right, far0, far1)


def parted(value):
    top = value.astype(jnp.bfloat16)
    return top, (value - top.astype(jnp.float32)).astype(jnp.bfloat16)


def dot(a, b):
    return jnp.dot(a, b, preferred_element_type=jnp.float32)


def chunk(ref, j):
    return ref[:, pl.ds(j * 16, 16), :].reshape(256, 128)


def part_right(recv, right):
    for s in range(4):
        top, rest = parted(chunk(recv, 4 + s))
        right[pl.ds(s * 256, 256), :128] = top
        right[pl.ds(s * 256, 256), 128:] = rest


def forward(hi, lo, right):
    wide = dot(hi[...], right[...])
    return wide[:, :128] + wide[:, 128:] + dot(lo[...], right[:, :128])


def mate_body(recv, hi, lo, out, right):
    @pl.when(pl.program_id(0) == 0)
    def _():
        part_right(recv, right)

    out[...] = forward(hi, lo, right)


def rows_at(first):
    return pl.BlockSpec((512, 1024), lambda i: (first + i, 0))


def mate(recv, hi, lo):
    return call(
        mate_body,
        grid=(2,),
        out_shape=jax.ShapeDtypeStruct((1024, 128), jnp.float32),
        in_specs=[whole(16, 128, 128), rows_at(2), rows_at(2)],
        out_specs=pl.BlockSpec((512, 128), lambda i: (i, 0)),
        scratch_shapes=[pltpu.VMEM((1024, 256), jnp.bfloat16)],
        name="mate",
    )(recv, hi, lo)


def mirror_body(recv, other, hi0, lo0, hi1, lo1, sums, out, scalars, back):
    step = pl.program_id(0)

    @pl.when(step == 0)
    def _():
        back[...] = jnp.zeros_like(back)

    for ref, hi, lo in ((recv, hi0, lo0), (other, hi1, lo1)):
        pairs = [parted(chunk(ref, step * 2 + c).T) for c in range(2)]
        top = jnp.concatenate([pair[0] for pair in pairs], axis=1)
        rest = jnp.concatenate([pair[1] for pair in pairs], axis=1)
        wide = dot(jnp.concatenate([top, rest], axis=0), hi[...])
        back[...] += wide[:128] + wide[128:] + dot(top, lo[...])

    @pl.when(step == 1)
    def _():
        out[...] = back[...].T
        curve = jnp.zeros((8, 128), jnp.float32)
        for s in range(4):
            piece = chunk(recv, 4 + s) * out[s * 256 : (s + 1) * 256]
            curve = curve + jnp.sum(piece.reshape(32, 8, 128), axis=0)
        place = lax.broadcasted_iota(jnp.int32, (8, 128), 0)
        scalars[...] = jnp.where(place == 2, row_sum(curve) * (2 * DIFFUSION), sums[...])


def mirror(recv, other, hi, lo, sums):
    return call(
        mirror_body,
        grid=(2,),
        limit=20,
        out_shape=(
            jax.ShapeDtypeStruct((1024, 128), jnp.float32),
            jax.ShapeDtypeStruct((8, 128), jnp.float32),
        ),
        in_specs=[whole(16, 128, 128)] * 2
        + [rows_at(0), rows_at(0), rows_at(2), rows_at(2), whole(8, 128)],
        out_specs=(whole(1024, 128), whole(8, 128)),
        scratch_shapes=[pltpu.VMEM((128, 1024), jnp.float32)],
        name="mirror",
    )(recv, other, hi, lo, hi, lo, sums)


def gathered_body(recv, hi, lo, theirs, mirrored, mine, mates, out, right):
    step = pl.program_id(0)

    @pl.when(step == 0)
    def _():
        part_right(recv, right)
        for s in range(4):
            out[:, 64 + s * 16 : 80 + s * 16, :] = mirrored[s * 256 : (s + 1) * 256].reshape(16, 16, 128)

    part = forward(hi, lo, right) + theirs[...]
    for c in range(2):
        j = step * 2 + c
        piece = part[c * 256 : (c + 1) * 256]
        out[:, pl.ds(j * 16, 16), :] = piece.reshape(16, 16, 128)

    @pl.when(step == 1)
    def _():
        row = mine[...] + mates[...]
        out[:, 128:136, :] = jnp.broadcast_to(row[None], (16, 8, 128))


def gathered(recv, hi, lo, theirs, mirrored, mine, mates):
    return call(
        gathered_body,
        grid=(2,),
        out_shape=jax.ShapeDtypeStruct((16, 136, 128), jnp.float32),
        in_specs=[
            whole(16, 128, 128),
            rows_at(0),
            rows_at(0),
            pl.BlockSpec((512, 128), lambda i: (i, 0)),
            whole(1024, 128),
            whole(8, 128),
            whole(8, 128),
        ],
        out_specs=whole(16, 136, 128),
        scratch_shapes=[
            pltpu.VMEM((1024, 256), jnp.bfloat16),
        ],
        name="gathered",
    )(recv, hi, lo, theirs, mirrored, mine, mates)


def multiply(recv, sums, hi, lo):
    other = lax.ppermute(recv, RC, SWAP)
    theirs = lax.ppermute(mate(recv, hi, lo), RC, SWAP)
    mirrored, mine = mirror(recv, other, hi, lo, sums)
    mates = lax.ppermute(mine, RC, SWAP)
    return gathered(recv, hi, lo, theirs, mirrored, mine, mates)


def spread(field, send):
    for s in range(4):
        for g in range(4):
            piece = field(s, g)
            for other in range(4):
                send[g * 4 + other, s * 16 : s * 16 + 16, :] = piece
                send[other * 4 + g, 64 + s * 16 : 80 + s * 16, :] = piece


def row_sum(value):
    return jnp.sum(value, axis=0, keepdims=True)


def rows_of(*rows):
    place = lax.broadcasted_iota(jnp.int32, (8, 128), 0)
    out = jnp.zeros((8, 128), jnp.float32)
    for i, row in enumerate(rows):
        out = jnp.where(place == i, row, out)
    return out


def start_body(recv, send, sums):
    square = jnp.zeros((16, 128), jnp.float32)
    for i in range(16):
        piece = recv[i, :16]
        square = square + piece * piece
    spread(lambda s, g: recv[s * 4 + g, :16], send)
    sums[...] = rows_of(row_sum(square))


def start(recv):
    return call(
        start_body,
        out_shape=(
            jax.ShapeDtypeStruct((16, 128, 128), jnp.float32),
            jax.ShapeDtypeStruct((8, 128), jnp.float32),
        ),
        name="start",
    )(recv)


def update_body(step, *refs):
    if step == 0:
        recv, residual = refs[:2]
        outs = refs[2:]
    else:
        recv, residual, direction, image, ranking, last = refs[:6]
        outs = refs[6:]
    total = jnp.zeros((8, 128), jnp.float32)
    for i in range(16):
        total = total + recv[i, 128:136]
    now = total[0:1]
    curve = now - total[2:3]
    if step > 0:
        beta = now / last[0:1]
        curve = curve + 2.0 * beta * total[1:2] + beta * beta * last[1:2]
    alpha = now / curve
    final = step + 1 == ITERS
    square = jnp.zeros((16, 128), jnp.float32)
    cross = jnp.zeros((16, 128), jnp.float32)
    for s in range(4):
        for g in range(4):
            acc = jnp.zeros((16, 128), jnp.float32)
            for other in range(4):
                acc = acc + recv[g * 4 + other, s * 16 : s * 16 + 16]
                acc = acc + recv[other * 4 + g, 64 + s * 16 : 80 + s * 16]
            i = s * 4 + g
            rest = residual[i, :16]
            aim = rest
            made = rest - DIFFUSION * acc
            if step > 0:
                aim = aim + beta * direction[i]
                made = made + beta * image[i]
            ranked = alpha * aim
            if step > 0:
                ranked = ranked + ranking[i]
            rest = rest - alpha * made
            if final:
                outs[0][i, 0] = ranked
                outs[0][i, 1] = rest
            else:
                send, new_residual, new_direction, new_image, new_ranking = outs[:5]
                new_residual[i] = rest
                new_direction[i] = aim
                new_image[i] = made
                new_ranking[i] = ranked
                square = square + rest * rest
                cross = cross + rest * made
    if not final:
        spread(lambda s, g: new_residual[s * 4 + g], send)
        outs[5][...] = rows_of(now, curve)
        outs[6][...] = rows_of(row_sum(square), row_sum(cross))


def update(step, *operands):
    field = jax.ShapeDtypeStruct((16, 16, 128), jnp.float32)
    small = jax.ShapeDtypeStruct((8, 128), jnp.float32)
    if step + 1 == ITERS:
        shapes = [jax.ShapeDtypeStruct((16, 2, 16, 128), jnp.float32)]
    else:
        send = jax.ShapeDtypeStruct((16, 128, 128), jnp.float32)
        shapes = [send, field, field, field, field, small, small]
    return call(
        functools.partial(update_body, step), out_shape=shapes, name="update"
    )(*operands)


def shards(right_side, affinity_blocks, block_coords, block_counts):
    r = lax.axis_index("row")
    c = lax.axis_index("col")
    yh, yl, z, k = r // 4, c // 8, (c // 2) % 4, c % 2
    own = affinity_blocks.reshape(16, 128, 128)
    left = lax.ppermute(own, RC, shift_y(1))
    right = lax.ppermute(own, RC, shift_y(3))

    br = block_coords[:, 0, :, 0]
    bc = block_coords[:, 0, :, 1]
    par = jnp.arange(2, dtype=jnp.int32)[:, None] ^ k
    row128 = par * 8 + ((br // 2) * 2 + yh) * 2 + br % 2
    col128 = ((bc // 2) * 2 + yl) * 2 + bc % 2
    live = jnp.arange(8, dtype=jnp.int32)[None, :] < block_counts
    code = jnp.where(live, row128 * 8 + col128, -1).astype(jnp.float32)
    meta = jnp.pad(code.reshape(1, 16), ((0, 7), (0, 112)))

    send = right_side.reshape(4, 16, 4, 128).transpose(2, 0, 1, 3).reshape(16, 16, 128)
    send = jnp.concatenate([send, jnp.broadcast_to(meta[None], (16, 8, 128))], axis=1)
    recv = exchange(send, SHEETS)
    codes = lax.dynamic_slice(recv.reshape(4, 4, 24, 128), (0, z, 16, 0), (4, 1, 1, 16))
    codes = jnp.concatenate(
        [codes.reshape(64).astype(jnp.int32), (yh * 2 + yl)[None].astype(jnp.int32)]
    )

    send, sums = start(recv)
    state = (recv,)
    send, left, right = lax.optimization_barrier((send, left, right))
    far0 = lax.ppermute(left[:8], RC, shift_y(1))
    far1 = lax.ppermute(right[8:], RC, shift_y(3))
    got = exchange(send, PLANES)
    hi, lo = assemble(codes, own, left, right, far0, far1)
    for step in range(ITERS):
        if step:
            got = exchange(send, PLANES)
        products = exchange(multiply(got, sums, hi, lo), PLANES)
        made = update(step, products, *state)
        if step + 1 < ITERS:
            send, sums = made[0], made[6]
            state = made[1:6]
    done = exchange(made[0], SHEETS)
    done = done.reshape(4, 4, 2, 16, 128).transpose(2, 1, 3, 0, 4).reshape(2, 1, 64, 512)
    return done[0], done[1]


def solution(mesh):
    in_specs = (
        P("col", "row", None),
        P("row", "col", None, None, None),
        P("row", "col", None, None),
        P("row", "col"),
    )
    out_specs = (P("col", "row", None), P("col", "row", None))
    return jax.shard_map(
        shards, mesh=mesh, in_specs=in_specs, out_specs=out_specs, check_vma=False
    )
```

time: 1290 us -> 222 us (0.17)
  waiting for transfers between devices: 731 us -> 15.6 us
  blocking collectives: 390 us -> 166 us
  matrix products: 62.8 us -> 0 us
  local copies, waits for them, and re-layouts: 59 us -> 6.77 us
  Pallas kernels: 0 us -> 22.9 us
  other arithmetic: 23.3 us -> 0.85 us
  between operations: 15.1 us -> 0.87 us
    psum x5 -> x0, blocking collectives: 319 us -> none  [the longest x3 189 us: squares(): return lax.psum(jnp.sum(residual * residual, axis=(0, 1)), ('row', 'col'))]
    reduce_scatter x6 -> x0, waiting for transfers between devices: 297 us -> none  [the longest x3 149 us: operate(): summed = lax.psum_scatter(spread, 'col', scatter_dimension=2, tiled=True)]
    psum x3 -> x0, waiting for transfers between devices: 293 us -> none  [broadcast(): return lax.psum(kept, axis)]
    all_gather x3 -> x0, waiting for transfers between devices: 139 us -> none  [operate(): whole = lax.all_gather(piece, 'row', axis=1, tiled=True)]
    all_to_all x6 -> x8, blocking collectives: 70.9 us -> 166 us  [exchange(): return lax.all_to_all(send, RC, 0, 0, axis_index_groups=groups, tiled=True)]
    dot_general x24 -> x0, matrix products: 62.8 us -> none  [the longest x6 18.4 us: forward_only(): jnp.einsum('kab,kbw->kaw', masked, picked, precision=lax.Precision.HIGHEST)]
    gather x12 -> x0, local copies, waits for them, and re-layouts: 28.4 us -> none  [the longest x6 15.6 us: backward_only(): chosen = jnp.take(row_field, rows, axis=0)]
    pallas_call x0 -> x14, Pallas kernels: none -> 22.9 us  [the longest x3 8.29 us: mirror(): call(mirror_body, grid=(2,), limit=20, out_shape=(jax.ShapeDtypeStruct((1...]
  transfers between devices with their start and end apart: 12 -> 13, of which waited for: 12 -> 7; matrix products, arithmetic and copies ran while one was open for 10% -> 2% of each run, Pallas kernels for 0% -> 8%
where the time goes in v1:
time: 222 us
  blocking collectives  166 us (75%)
  Pallas kernels  22.9 us (10%)
  waiting for transfers between devices  15.6 us (7%)
  starting transfers between devices  8.76 us (4%)
  local copies, waits for them, and re-layouts  6.77 us (3%)
    all_to_all x8, blocking collectives, exchange(): return lax.all_to_all(send, RC, 0, 0, axis_index_groups=groups, tiled=True)  166 us
    ppermute x1, waiting for transfers between devices, shards(): far0 = lax.ppermute(left[:8], RC, shift_y(1))  11.6 us
    pallas_call x3, Pallas kernels, mirror(): call(mirror_body, grid=(2,), limit=20, out_shape=(jax.ShapeDtypeStruct((1...  8.29 us
    pallas_call x3, Pallas kernels, gathered(): call(gathered_body, grid=(2,), out_shape=jax.ShapeDtypeStruct((16, 136, 1...  4.78 us
    pallas_call x1, Pallas kernels, assemble(): call(assemble_body, limit=26, grid=(8,), out_shape=(half, half), in_specs...  4.69 us
    pallas_call x3, Pallas kernels, mate(): call(mate_body, grid=(2,), out_shape=jax.ShapeDtypeStruct((1024, 128), jn...  4.68 us
  transfers between devices with their start and end apart: 13, of which 7 were waited for; matrix products, arithmetic and copies ran while one was open for 2% of the time, Pallas kernels for 8%

profile of v1, /device:TPU:0, one launch (start us, length us, event | category | flops | bytes accessed | tf_op | source)
XLA Modules:
  0.0 221.7 jit_solution(9501719728699058052)
XLA Ops:
  0.6 1.7 collective-permute-start
  2.4 1.6 collective-permute-start.1
  6.9 26.7 %all_to_all.40.recv.refs_1_ = f32[16,24,128]{2,1,0:T(8,128)S(1)} all-to-all(f32[16,24,128]{2,1,0:T(8,128)S(1)} %pad_maximum_fusion), channel_id=1, replica_groups={{0,2,4,6,8,10,12,14,64,66,68,70,72,74,76,78},{1,3,5,7,9,11,13,15,65,67,..., dimensions={0} | all-to-all | bytes 393216 | tf_op jit(solution)/shard_map/all_to_all | solution.py:49
  33.8 21.2 %all_to_all.41.recv = f32[16,128,128]{2,1,0:T(8,128)S(1)} all-to-all(f32[16,128,128]{2,1,0:T(8,128)S(1)} %get-tuple-element.30), channel_id=1, replica_groups={{0,2,4,6,16,18,20,22,32,34,36,38,48,50,52,54},{1,3,5,7,17,19,21,23,33,3..., dimensions={0} | all-to-all | bytes 2097152 | tf_op jit(solution)/shard_map/all_to_all | solution.py:49
  57.1 2.8 %collective-permute-start.3 = (f32[8,128,128]{2,1,0:T(8,128)}, f32[8,128,128]{2,1,0:T(8,128)}, u32[]{:S(2)}, u32[]{:S(2)}) collective-permute-start(f32[8,128,128]{2,1,0:T(8,128)} %slice.23), channel_id=1, source_target_pairs={{0,72},{1,73},{2,74},{3,75},{4,76},{5,77},{6,78},{7,79},{8,0},{9,1... | collective-permute-start | bytes 1572872 | tf_op jit(solution)/shard_map/ppermute | solution.py:391
  60.1 11.6 %collective-permute-done.2.far0 = f32[8,128,128]{2,1,0:T(8,128)} collective-permute-done((f32[8,128,128]{2,1,0:T(8,128)}, f32[8,128,128]{2,1,0:T(8,128)}, u32[]{:S(2)}, u32[]{:S(2)}) %collective-permute-start.2) | collective-permute-done | bytes 524320 | tf_op jit(solution)/shard_map/ppermute | solution.py:390
  71.8 1.2 copy-done
  73.1 4.7 %assemble.1 = (bf16[2048,1024]{1,0:T(8,128)(2,1)S(1)}, bf16[2048,1024]{1,0:T(8,128)(2,1)S(1)}) custom-call(s32[65]{0:T(128)S(1)} %pad_add_fusion.codes, f32[16,128,128]{2,1,0:T(8,128)S(1)} %bitcast.16, f32[16,128,128]{2,1,0:T(8,128)S(1)} %collective-permute-done.left, f32[16,128,128]{2,1,0:T(8,128)S(1)} %collective-permute-done.1.right, ...), custom_call_target="tpu_custom_call" | custom-call | tf_op jit(solution)/shard_map/assemble/pallas_call | solution.py:99
  77.8 1.6 mate.3
  79.4 3.6 %mirror.3 = (f32[1024,128]{1,0:T(8,128)S(1)}, f32[8,128]{1,0:T(8,128)S(1)}) custom-call(f32[16,128,128]{2,1,0:T(8,128)S(1)} %all_to_all.41.recv, f32[16,128,128]{2,1,0:T(8,128)} %collective-permute-done.5.other, bf16[2048,1024]{1,0:T(8,128)(2,1)S(1)} %get-tuple-element.33.hi.hi0.hi1, bf16[2048,1024]{1,0:T(8,128)(2,1)S(1)} %get-tuple-element.34.lo.lo0.lo1, ...), custom_call_target="tpu_custom_call" | custom-call | tf_op jit(solution)/shard_map/mirror/pallas_call | solution.py:188
  84.4 1.6 gathered.3
  86.0 21.7 %all_to_all.42.refs_0_ = f32[16,136,128]{2,1,0:T(8,128)S(1)} all-to-all(f32[16,136,128]{2,1,0:T(8,128)S(1)} %gathered.3), channel_id=1, replica_groups={{0,2,4,6,16,18,20,22,32,34,36,38,48,50,52,54},{1,3,5,7,17,19,21,23,33,3..., dimensions={0} | all-to-all | bytes 2228224 | tf_op jit(solution)/shard_map/all_to_all | solution.py:49
  107.8 19.7 %all_to_all.43.recv = f32[16,128,128]{2,1,0:T(8,128)S(1)} all-to-all(f32[16,128,128]{2,1,0:T(8,128)S(1)} %get-tuple-element.38), channel_id=1, replica_groups={{0,2,4,6,16,18,20,22,32,34,36,38,48,50,52,54},{1,3,5,7,17,19,21,23,33,3..., dimensions={0} | all-to-all | bytes 2097152 | tf_op jit(solution)/shard_map/all_to_all | solution.py:49
  127.5 1.6 mate.4
  130.2 2.3 %mirror.4 = (f32[1024,128]{1,0:T(8,128)S(1)}, f32[8,128]{1,0:T(8,128)S(1)}) custom-call(f32[16,128,128]{2,1,0:T(8,128)S(1)} %all_to_all.43.recv, f32[16,128,128]{2,1,0:T(8,128)S(1)} %collective-permute-done.8.other, bf16[2048,1024]{1,0:T(8,128)(2,1)S(1)} %get-tuple-element.33.hi.hi0.hi1, bf16[2048,1024]{1,0:T(8,128)(2,1)S(1)} %get-tuple-element.34.lo.lo0.lo1, ...), custom_call_target="tpu_custom_call" | custom-call | tf_op jit(solution)/shard_map/mirror/pallas_call | solution.py:188
  133.8 1.6 gathered.4
  135.4 21.4 %all_to_all.44.refs_0_ = f32[16,136,128]{2,1,0:T(8,128)S(1)} all-to-all(f32[16,136,128]{2,1,0:T(8,128)S(1)} %gathered.4), channel_id=1, replica_groups={{0,2,4,6,16,18,20,22,32,34,36,38,48,50,52,54},{1,3,5,7,17,19,21,23,33,3..., dimensions={0} | all-to-all | bytes 2228224 | tf_op jit(solution)/shard_map/all_to_all | solution.py:49
  157.0 19.5 %all_to_all.45.recv = f32[16,128,128]{2,1,0:T(8,128)S(1)} all-to-all(f32[16,128,128]{2,1,0:T(8,128)S(1)} %get-tuple-element.47), channel_id=1, replica_groups={{0,2,4,6,16,18,20,22,32,34,36,38,48,50,52,54},{1,3,5,7,17,19,21,23,33,3..., dimensions={0} | all-to-all | bytes 2097152 | tf_op jit(solution)/shard_map/all_to_all | solution.py:49
  176.5 1.6 mate.5
  179.2 2.3 %mirror.5 = (f32[1024,128]{1,0:T(8,128)S(1)}, f32[8,128]{1,0:T(8,128)S(1)}) custom-call(f32[16,128,128]{2,1,0:T(8,128)S(1)} %all_to_all.45.recv, f32[16,128,128]{2,1,0:T(8,128)S(1)} %collective-permute-done.11.other, bf16[2048,1024]{1,0:T(8,128)(2,1)S(1)} %get-tuple-element.33.hi.hi0.hi1, bf16[2048,1024]{1,0:T(8,128)(2,1)S(1)} %get-tuple-element.34.lo.lo0.lo1, ...), custom_call_target="tpu_custom_call" | custom-call | tf_op jit(solution)/shard_map/mirror/pallas_call | solution.py:188
  181.7 1.0 collective-permute-done.12.mates
  182.8 1.6 gathered.5
  184.4 21.4 %all_to_all.46.refs_0_ = f32[16,136,128]{2,1,0:T(8,128)S(1)} all-to-all(f32[16,136,128]{2,1,0:T(8,128)S(1)} %gathered.5), channel_id=1, replica_groups={{0,2,4,6,16,18,20,22,32,34,36,38,48,50,52,54},{1,3,5,7,17,19,21,23,33,3..., dimensions={0} | all-to-all | bytes 2228224 | tf_op jit(solution)/shard_map/all_to_all | solution.py:49
  205.9 14.2 %all_to_all.47 = f32[16,2,16,128]{3,2,1,0:T(8,128)S(1)} all-to-all(f32[16,2,16,128]{3,2,1,0:T(8,128)S(1)} %update.5), channel_id=1, replica_groups={{0,2,4,6,8,10,12,14,64,66,68,70,72,74,76,78},{1,3,5,7,9,11,13,15,65,67,..., dimensions={0} | all-to-all | bytes 524288 | tf_op jit(solution)/shard_map/all_to_all | solution.py:49
  (51 shorter events, 12.5 us)
Async XLA Ops:
  0.6 33.1 %collective-permute-start = (f32[16,128,128]{2,1,0:T(8,128)}, f32[16,128,128]{2,1,0:T(8,128)S(1)}, u32[]{:S(2)}, u32[]{:S(2)}) collective-permute-start(f32[16,128,128]{2,1,0:T(8,128)} %bitcast.14), channel_id=1, source_target_pairs={{0,8},{1,9},{2,10},{3,11},{4,12},{5,13},{6,14},{7,15},{8,64},{9,65... | collective-permute-start | bytes 3145736 | tf_op jit(solution)/shard_map/ppermute | solution.py:367
  2.4 31.4 %collective-permute-start.1 = (f32[16,128,128]{2,1,0:T(8,128)}, f32[16,128,128]{2,1,0:T(8,128)S(1)}, u32[]{:S(2)}, u32[]{:S(2)}) collective-permute-start(f32[16,128,128]{2,1,0:T(8,128)} %bitcast.15), channel_id=1, source_target_pairs={{0,72},{1,73},{2,74},{3,75},{4,76},{5,77},{6,78},{7,79},{8,0},{9,1... | collective-permute-start | bytes 3145736 | tf_op jit(solution)/shard_map/ppermute | solution.py:368
  55.0 24.4 %collective-permute-start.5 = (f32[16,128,128]{2,1,0:T(8,128)S(1)}, f32[16,128,128]{2,1,0:T(8,128)}, u32[]{:S(2)}, u32[]{:S(2)}) collective-permute-start(f32[16,128,128]{2,1,0:T(8,128)S(1)} %all_to_all.41.recv), channel_id=1, source_target_pairs={{0,1},{1,0},{2,3},{3,2},{4,5},{5,4},{6,7},{7,6},{8,9},{9,8},{10,11... | collective-permute-start | bytes 3145736 | tf_op jit(solution)/shard_map/ppermute | solution.py:248
  55.9 15.9 %collective-permute-start.2 = (f32[8,128,128]{2,1,0:T(8,128)}, f32[8,128,128]{2,1,0:T(8,128)}, u32[]{:S(2)}, u32[]{:S(2)}) collective-permute-start(f32[8,128,128]{2,1,0:T(8,128)} %slice.22), channel_id=1, source_target_pairs={{0,8},{1,9},{2,10},{3,11},{4,12},{5,13},{6,14},{7,15},{8,64},{9,65... | collective-permute-start | bytes 1572872 | tf_op jit(solution)/shard_map/ppermute | solution.py:390
  57.1 14.7 %collective-permute-start.3 = (f32[8,128,128]{2,1,0:T(8,128)}, f32[8,128,128]{2,1,0:T(8,128)}, u32[]{:S(2)}, u32[]{:S(2)}) collective-permute-start(f32[8,128,128]{2,1,0:T(8,128)} %slice.23), channel_id=1, source_target_pairs={{0,72},{1,73},{2,74},{3,75},{4,76},{5,77},{6,78},{7,79},{8,0},{9,1... | collective-permute-start | bytes 1572872 | tf_op jit(solution)/shard_map/ppermute | solution.py:391
  71.8 1.2 copy-start
  79.3 4.2 %collective-permute-start.4 = (f32[1024,128]{1,0:T(8,128)S(1)}, f32[1024,128]{1,0:T(8,128)S(1)}, u32[]{:S(2)}, u32[]{:S(2)}) collective-permute-start(f32[1024,128]{1,0:T(8,128)S(1)} %mate.3), channel_id=1, source_target_pairs={{0,1},{1,0},{2,3},{3,2},{4,5},{5,4},{6,7},{7,6},{8,9},{9,8},{10,11... | collective-permute-start | bytes 1572872 | tf_op jit(solution)/shard_map/ppermute | solution.py:249
  83.0 1.4 collective-permute-start.6
  127.5 2.7 %collective-permute-start.8 = (f32[16,128,128]{2,1,0:T(8,128)S(1)}, f32[16,128,128]{2,1,0:T(8,128)S(1)}, u32[]{:S(2)}, u32[]{:S(2)}) collective-permute-start(f32[16,128,128]{2,1,0:T(8,128)S(1)} %all_to_all.43.recv), channel_id=1, source_target_pairs={{0,1},{1,0},{2,3},{3,2},{4,5},{5,4},{6,7},{7,6},{8,9},{9,8},{10,11... | collective-permute-start | bytes 3145736 | tf_op jit(solution)/shard_map/ppermute | solution.py:248
  129.1 3.7 %collective-permute-start.7 = (f32[1024,128]{1,0:T(8,128)S(1)}, f32[1024,128]{1,0:T(8,128)S(1)}, u32[]{:S(2)}, u32[]{:S(2)}) collective-permute-start(f32[1024,128]{1,0:T(8,128)S(1)} %mate.4), channel_id=1, source_target_pairs={{0,1},{1,0},{2,3},{3,2},{4,5},{5,4},{6,7},{7,6},{8,9},{9,8},{10,11... | collective-permute-start | bytes 1572872 | tf_op jit(solution)/shard_map/ppermute | solution.py:249
  132.6 1.2 collective-permute-start.9
  176.5 2.7 %collective-permute-start.11 = (f32[16,128,128]{2,1,0:T(8,128)S(1)}, f32[16,128,128]{2,1,0:T(8,128)S(1)}, u32[]{:S(2)}, u32[]{:S(2)}) collective-permute-start(f32[16,128,128]{2,1,0:T(8,128)S(1)} %all_to_all.45.recv), channel_id=1, source_target_pairs={{0,1},{1,0},{2,3},{3,2},{4,5},{5,4},{6,7},{7,6},{8,9},{9,8},{10,11... | collective-permute-start | bytes 3145736 | tf_op jit(solution)/shard_map/ppermute | solution.py:248
  178.1 3.7 %collective-permute-start.10 = (f32[1024,128]{1,0:T(8,128)S(1)}, f32[1024,128]{1,0:T(8,128)S(1)}, u32[]{:S(2)}, u32[]{:S(2)}) collective-permute-start(f32[1024,128]{1,0:T(8,128)S(1)} %mate.5), channel_id=1, source_target_pairs={{0,1},{1,0},{2,3},{3,2},{4,5},{5,4},{6,7},{7,6},{8,9},{9,8},{10,11... | collective-permute-start | bytes 1572872 | tf_op jit(solution)/shard_map/ppermute | solution.py:249
  181.5 1.2 collective-permute-start.12

commit v2 on v1

--- a/solution.py
+++ b/solution.py
@@ -55,16 +55,17 @@
     )
 
 
-def assemble_body(codes, own, left, right, far0, far1, hi, lo, dense):
+def assemble_body(codes, *refs):
+    pieces, recv, (hi, lo, share, dense) = refs[:8], refs[8], refs[9:]
     step = pl.program_id(0)
 
     @pl.when(step == 0)
     def _():
+        share[...] = recv[:, :64, :]
         dense[...] = jnp.zeros_like(dense)
         y = codes[64]
-        pieces = ((own, 0, 0, 16), (left, 1, 0, 16), (right, 3, 0, 16), (far0, 2, 0, 8), (far1, 2, 8, 8))
-        for ref, shift, first, count in pieces:
-            base = ((y - shift) & 3) * 16 + first
+        for i, ref in enumerate(pieces):
+            base = ((y - i // 2) & 3) * 16 + (i % 2) * 8
 
             def put(b, carry, ref=ref, base=base):
                 code = codes[base + b]
@@ -77,7 +78,7 @@
 
                 return carry
 
-            lax.fori_loop(0, count, put, 0)
+            lax.fori_loop(0, 8, put, 0)
 
     def narrow(i, carry):
         rows = pl.ds(pl.multiple_of(i * 32, 32), 32)
@@ -94,20 +95,21 @@
     return pl.BlockSpec(shape, lambda i: (0,) * len(shape))
 
 
-def assemble(codes, own, left, right, far0, far1):
+def assemble(codes, pieces, recv):
     half = jax.ShapeDtypeStruct((2048, 1024), jnp.bfloat16)
     return call(
         assemble_body,
         limit=26,
         grid=(8,),
-        out_shape=(half, half),
+        out_shape=(half, half, jax.ShapeDtypeStruct((16, 64, 128), jnp.float32)),
         in_specs=[pl.BlockSpec(memory_space=pltpu.SMEM)]
-        + [whole(16, 128, 128)] * 3
-        + [whole(8, 128, 128)] * 2,
-        out_specs=(pl.BlockSpec((256, 1024), lambda i: (i, 0)),) * 2,
+        + [whole(8, 128, 128)] * 8
+        + [whole(16, 128, 128)],
+        out_specs=(pl.BlockSpec((256, 1024), lambda i: (i, 0)),) * 2
+        + (whole(16, 64, 128),),
         scratch_shapes=[pltpu.VMEM((2048, 1024), jnp.float32)],
         name="assemble",
-    )(codes, own, left, right, far0, far1)
+    )(codes, *pieces, recv)
 
 
 def parted(value):
@@ -193,7 +195,7 @@
             jax.ShapeDtypeStruct((1024, 128), jnp.float32),
             jax.ShapeDtypeStruct((8, 128), jnp.float32),
         ),
-        in_specs=[whole(16, 128, 128)] * 2
+        in_specs=[whole(16, 128, 128), whole(*other.shape)]
         + [rows_at(0), rows_at(0), rows_at(2), rows_at(2), whole(8, 128)],
         out_specs=(whole(1024, 128), whole(8, 128)),
         scratch_shapes=[pltpu.VMEM((128, 1024), jnp.float32)],
@@ -244,8 +246,8 @@
     )(recv, hi, lo, theirs, mirrored, mine, mates)
 
 
-def multiply(recv, sums, hi, lo):
-    other = lax.ppermute(recv, RC, SWAP)
+def multiply(recv, share, sums, hi, lo):
+    other = lax.ppermute(share, RC, SWAP)
     theirs = lax.ppermute(mate(recv, hi, lo), RC, SWAP)
     mirrored, mine = mirror(recv, other, hi, lo, sums)
     mates = lax.ppermute(mine, RC, SWAP)
@@ -363,9 +365,10 @@
     r = lax.axis_index("row")
     c = lax.axis_index("col")
     yh, yl, z, k = r // 4, c // 8, (c // 2) % 4, c % 2
-    own = affinity_blocks.reshape(16, 128, 128)
-    left = lax.ppermute(own, RC, shift_y(1))
-    right = lax.ppermute(own, RC, shift_y(3))
+    own0 = affinity_blocks[0, 0]
+    own1 = affinity_blocks[1, 0]
+    left0 = lax.ppermute(own0, RC, shift_y(1))
+    right1 = lax.ppermute(own1, RC, shift_y(3))
 
     br = block_coords[:, 0, :, 0]
     bc = block_coords[:, 0, :, 1]
@@ -386,15 +389,19 @@
 
     send, sums = start(recv)
     state = (recv,)
-    send, left, right = lax.optimization_barrier((send, left, right))
-    far0 = lax.ppermute(left[:8], RC, shift_y(1))
-    far1 = lax.ppermute(right[8:], RC, shift_y(3))
+    send, left0, right1 = lax.optimization_barrier((send, left0, right1))
+    later0, later1, recv = lax.optimization_barrier((own0, own1, recv))
+    far0 = lax.ppermute(left0, RC, shift_y(1))
+    far1 = lax.ppermute(right1, RC, shift_y(3))
+    left1 = lax.ppermute(later1, RC, shift_y(1))
+    right0 = lax.ppermute(later0, RC, shift_y(3))
     got = exchange(send, PLANES)
-    hi, lo = assemble(codes, own, left, right, far0, far1)
+    pieces = (own0, own1, left0, left1, far0, far1, right0, right1)
+    hi, lo, share = assemble(codes, pieces, got)
     for step in range(ITERS):
         if step:
-            got = exchange(send, PLANES)
-        products = exchange(multiply(got, sums, hi, lo), PLANES)
+            got = share = exchange(send, PLANES)
+        products = exchange(multiply(got, share, sums, hi, lo), PLANES)
         made = update(step, products, *state)
         if step + 1 < ITERS:
             send, sums = made[0], made[6]

time: 222 us -> 207 us (0.932)
  blocking collectives: 166 us -> 139 us
  starting transfers between devices: 8.76 us -> 17.4 us
  waiting for transfers between devices: 15.6 us -> 21.6 us
  local copies, waits for them, and re-layouts: 6.77 us -> 3.51 us
    all_to_all x8 -> x7, blocking collectives: 166 us -> 139 us  [exchange(): return lax.all_to_all(send, RC, 0, 0, axis_index_groups=groups, tiled=True)]
    ppermute x7 -> x9, waiting for transfers between devices: 12.7 us -> 18.5 us  [the longest x1 9.52 us: shards(): left1 = lax.ppermute(later1, RC, shift_y(1))]
    all_to_all x0 -> x1, starting transfers between devices: none -> 5.31 us  [exchange(): return lax.all_to_all(send, RC, 0, 0, axis_index_groups=groups, tiled=True)]
    ppermute x7 -> x9, starting transfers between devices: 6.55 us -> 9.82 us  [the longest x1 3.24 us: shards(): right0 = lax.ppermute(later0, RC, shift_y(3))]
  transfers between devices with their start and end apart: 13 -> 16, of which waited for: 7 -> 7; matrix products, arithmetic and copies ran while one was open for 2% -> 0% of each run, Pallas kernels for 8% -> 6%
where the time goes in v2:
time: 207 us; the launch traced here: 206 us
  blocking collectives  139 us (67%)
  Pallas kernels  23 us (11%)
  waiting for transfers between devices  21.6 us (10%)
  starting transfers between devices  17.4 us (8%)
  local copies, waits for them, and re-layouts  3.51 us (2%)
    all_to_all x7, blocking collectives, exchange(): return lax.all_to_all(send, RC, 0, 0, axis_index_groups=groups, tiled=True)  139 us
    ppermute x1, waiting for transfers between devices, shards(): left1 = lax.ppermute(later1, RC, shift_y(1))  9.52 us
    ppermute x1, waiting for transfers between devices, shards(): far0 = lax.ppermute(left0, RC, shift_y(1))  7.89 us
    pallas_call x3, Pallas kernels, mirror(): call(mirror_body, grid=(2,), limit=20, out_shape=(jax.ShapeDtypeStruct((1...  7 us
    all_to_all x1, starting transfers between devices, exchange(): return lax.all_to_all(send, RC, 0, 0, axis_index_groups=groups, tiled=True)  5.31 us
    pallas_call x1, Pallas kernels, assemble(): call(assemble_body, limit=26, grid=(8,), out_shape=(half, half, jax.Shape...  5.11 us
    pallas_call x3, Pallas kernels, gathered(): call(gathered_body, grid=(2,), out_shape=jax.ShapeDtypeStruct((16, 136, 1...  4.75 us
    pallas_call x3, Pallas kernels, mate(): call(mate_body, grid=(2,), out_shape=jax.ShapeDtypeStruct((1024, 128), jn...  4.66 us
  transfers between devices with their start and end apart: 16, of which 7 were waited for; matrix products, arithmetic and copies ran while one was open for 0% of the time, Pallas kernels for 6%

profile of v2, /device:TPU:0, one launch (start us, length us, event | category | flops | bytes accessed | tf_op | source)
XLA Modules:
  0.0 206.1 jit_solution(8073387548957630264)
XLA Ops:
  0.7 1.3 slice_bitcast_fusion
  2.0 3.2 %collective-permute-start.1 = (f32[8,128,128]{2,1,0:T(8,128)S(1)}, f32[8,128,128]{2,1,0:T(8,128)S(1)}, u32[]{:S(2)}, u32[]{:S(2)}) collective-permute-start(f32[8,128,128]{2,1,0:T(8,128)S(1)} %get-tuple-element.35.refs_1_), channel_id=1, source_target_pairs={{0,72},{1,73},{2,74},{3,75},{4,76},{5,77},{6,78},{7,79},{8,0},{9,1... | collective-permute-start | bytes 1572872 | tf_op jit(solution)/shard_map/ppermute | solution.py:371
  5.8 19.4 %all_to_all.40.recv.refs_1_ = f32[16,24,128]{2,1,0:T(8,128)S(1)} all-to-all(f32[16,24,128]{2,1,0:T(8,128)S(1)} %pad_maximum_fusion), channel_id=1, replica_groups={{0,2,4,6,8,10,12,14,64,66,68,70,72,74,76,78},{1,3,5,7,9,11,13,15,65,67,..., dimensions={0} | all-to-all | bytes 393216 | tf_op jit(solution)/shard_map/all_to_all | solution.py:49
  26.3 5.3 %all-to-all-start.1 = ((f32[16,128,128]{2,1,0:T(8,128)}), f32[16,128,128]{2,1,0:T(8,128)S(1)}, u32[]{:S(2)}, u32[]{:S(2)}) async-start(f32[16,128,128]{2,1,0:T(8,128)} %get-tuple-element.33), calls=%async_computation.1 | async-start | bytes 2097152 | tf_op jit(solution)/shard_map/all_to_all | solution.py:49
  31.7 3.2 %collective-permute-start.5 = (f32[8,128,128]{2,1,0:T(8,128)S(1)}, f32[8,128,128]{2,1,0:T(8,128)}, u32[]{:S(2)}, u32[]{:S(2)}) collective-permute-start(f32[8,128,128]{2,1,0:T(8,128)S(1)} %get-tuple-element.37.refs_0_), channel_id=1, source_target_pairs={{0,72},{1,73},{2,74},{3,75},{4,76},{5,77},{6,78},{7,79},{8,0},{9,1... | collective-permute-start | bytes 1572872 | tf_op jit(solution)/shard_map/ppermute | solution.py:397
  34.9 3.2 %collective-permute-start.4 = (f32[8,128,128]{2,1,0:T(8,128)S(1)}, f32[8,128,128]{2,1,0:T(8,128)}, u32[]{:S(2)}, u32[]{:S(2)}) collective-permute-start(f32[8,128,128]{2,1,0:T(8,128)S(1)} %collective-permute-done.1.refs_7_), channel_id=1, source_target_pairs={{0,72},{1,73},{2,74},{3,75},{4,76},{5,77},{6,78},{7,79},{8,0},{9,1... | collective-permute-start | bytes 1572872 | tf_op jit(solution)/shard_map/ppermute | solution.py:395
  38.3 9.5 %collective-permute-done.2.refs_3_ = f32[8,128,128]{2,1,0:T(8,128)} collective-permute-done((f32[8,128,128]{2,1,0:T(8,128)S(1)}, f32[8,128,128]{2,1,0:T(8,128)}, u32[]{:S(2)}, u32[]{:S(2)}) %collective-permute-start.2) | collective-permute-done | bytes 524320 | tf_op jit(solution)/shard_map/ppermute | solution.py:396
  47.9 7.9 %collective-permute-done.3.refs_4_ = f32[8,128,128]{2,1,0:T(8,128)} collective-permute-done((f32[8,128,128]{2,1,0:T(8,128)S(1)}, f32[8,128,128]{2,1,0:T(8,128)}, u32[]{:S(2)}, u32[]{:S(2)}) %collective-permute-start.3) | collective-permute-done | bytes 524320 | tf_op jit(solution)/shard_map/ppermute | solution.py:394
  55.7 5.1 %assemble.1 = (bf16[2048,1024]{1,0:T(8,128)(2,1)S(1)}, bf16[2048,1024]{1,0:T(8,128)(2,1)S(1)}, f32[16,64,128]{2,1,0:T(8,128)S(1)}) custom-call(s32[65]{0:T(128)S(1)} %pad_add_fusion.codes, f32[8,128,128]{2,1,0:T(8,128)S(1)} %get-tuple-element.37.refs_0_, f32[8,128,128]{2,1,0:T(8,128)S(1)} %get-tuple-element.35.refs_1_, ...), custom_call_target="tpu_custom_call" | custom-call | tf_op jit(solution)/shard_map/assemble/pallas_call | solution.py:100
  61.0 1.6 mate.3
  63.1 2.3 %mirror.3 = (f32[1024,128]{1,0:T(8,128)S(1)}, f32[8,128]{1,0:T(8,128)S(1)}) custom-call(f32[16,128,128]{2,1,0:T(8,128)S(1)} %all-to-all-done.1.refs_8_.recv, f32[16,64,128]{2,1,0:T(8,128)S(1)} %collective-permute-done.7.other, bf16[2048,1024]{1,0:T(8,128)(2,1)S(1)} %get-tuple-element.38.hi.hi0.hi1, bf16[2048,1024]{1,0:T(8,128)(2,1)S(1)} %get-tuple-element.39.lo.lo0.lo1, ...), custom_call_target="tpu_custom_call" | custom-call | tf_op jit(solution)/shard_map/mirror/pallas_call | solution.py:190
  66.7 1.6 gathered.3
  68.3 24.9 %all_to_all.41.refs_0_ = f32[16,136,128]{2,1,0:T(8,128)S(1)} all-to-all(f32[16,136,128]{2,1,0:T(8,128)S(1)} %gathered.3), channel_id=1, replica_groups={{0,2,4,6,16,18,20,22,32,34,36,38,48,50,52,54},{1,3,5,7,17,19,21,23,33,3..., dimensions={0} | all-to-all | bytes 2228224 | tf_op jit(solution)/shard_map/all_to_all | solution.py:49
  93.3 19.5 %all_to_all.42.recv = f32[16,128,128]{2,1,0:T(8,128)S(1)} all-to-all(f32[16,128,128]{2,1,0:T(8,128)S(1)} %get-tuple-element.44), channel_id=1, replica_groups={{0,2,4,6,16,18,20,22,32,34,36,38,48,50,52,54},{1,3,5,7,17,19,21,23,33,3..., dimensions={0} | all-to-all | bytes 2097152 | tf_op jit(solution)/shard_map/all_to_all | solution.py:49
  112.8 1.6 mate.4
  115.5 2.3 %mirror.4 = (f32[1024,128]{1,0:T(8,128)S(1)}, f32[8,128]{1,0:T(8,128)S(1)}) custom-call(f32[16,128,128]{2,1,0:T(8,128)S(1)} %all_to_all.42.recv, f32[16,128,128]{2,1,0:T(8,128)S(1)} %collective-permute-done.10.other, bf16[2048,1024]{1,0:T(8,128)(2,1)S(1)} %get-tuple-element.38.hi.hi0.hi1, bf16[2048,1024]{1,0:T(8,128)(2,1)S(1)} %get-tuple-element.39.lo.lo0.lo1, ...), custom_call_target="tpu_custom_call" | custom-call | tf_op jit(solution)/shard_map/mirror/pallas_call | solution.py:190
  119.1 1.6 gathered.4
  120.7 21.4 %all_to_all.43.refs_0_ = f32[16,136,128]{2,1,0:T(8,128)S(1)} all-to-all(f32[16,136,128]{2,1,0:T(8,128)S(1)} %gathered.4), channel_id=1, replica_groups={{0,2,4,6,16,18,20,22,32,34,36,38,48,50,52,54},{1,3,5,7,17,19,21,23,33,3..., dimensions={0} | all-to-all | bytes 2228224 | tf_op jit(solution)/shard_map/all_to_all | solution.py:49
  142.3 19.5 %all_to_all.44.recv = f32[16,128,128]{2,1,0:T(8,128)S(1)} all-to-all(f32[16,128,128]{2,1,0:T(8,128)S(1)} %get-tuple-element.53), channel_id=1, replica_groups={{0,2,4,6,16,18,20,22,32,34,36,38,48,50,52,54},{1,3,5,7,17,19,21,23,33,3..., dimensions={0} | all-to-all | bytes 2097152 | tf_op jit(solution)/shard_map/all_to_all | solution.py:49
  161.8 1.5 mate.5
  164.4 2.3 %mirror.5 = (f32[1024,128]{1,0:T(8,128)S(1)}, f32[8,128]{1,0:T(8,128)S(1)}) custom-call(f32[16,128,128]{2,1,0:T(8,128)S(1)} %all_to_all.44.recv, f32[16,128,128]{2,1,0:T(8,128)S(1)} %collective-permute-done.13.other, bf16[2048,1024]{1,0:T(8,128)(2,1)S(1)} %get-tuple-element.38.hi.hi0.hi1, bf16[2048,1024]{1,0:T(8,128)(2,1)S(1)} %get-tuple-element.39.lo.lo0.lo1, ...), custom_call_target="tpu_custom_call" | custom-call | tf_op jit(solution)/shard_map/mirror/pallas_call | solution.py:190
  168.0 1.6 gathered.5
  169.6 21.4 %all_to_all.45.refs_0_ = f32[16,136,128]{2,1,0:T(8,128)S(1)} all-to-all(f32[16,136,128]{2,1,0:T(8,128)S(1)} %gathered.5), channel_id=1, replica_groups={{0,2,4,6,16,18,20,22,32,34,36,38,48,50,52,54},{1,3,5,7,17,19,21,23,33,3..., dimensions={0} | all-to-all | bytes 2228224 | tf_op jit(solution)/shard_map/all_to_all | solution.py:49
  191.1 13.4 %all_to_all.46 = f32[16,2,16,128]{3,2,1,0:T(8,128)S(1)} all-to-all(f32[16,2,16,128]{3,2,1,0:T(8,128)S(1)} %update.5), channel_id=1, replica_groups={{0,2,4,6,8,10,12,14,64,66,68,70,72,74,76,78},{1,3,5,7,9,11,13,15,65,67,..., dimensions={0} | all-to-all | bytes 524288 | tf_op jit(solution)/shard_map/all_to_all | solution.py:49
  (59 shorter events, 10.6 us)
Async XLA Ops:
  0.6 4.5 %copy-start.2 = (s32[2,1]{0,1:T(1,128)S(1)}, s32[2,1]{0,1:T(1,128)}, u32[]{:S(2)}) copy-start(s32[2,1]{0,1:T(1,128)} %param.7) | copy-start | bytes 28
  0.6 4.8 %copy-start.1 = (s32[2,1,8,2]{2,3,1,0:T(2,128)S(1)}, s32[2,1,8,2]{2,3,1,0:T(2,128)}, u32[]{:S(2)}) copy-start(s32[2,1,8,2]{2,3,1,0:T(2,128)} %param.6) | copy-start | bytes 388
  0.7 5.0 %copy-start = (f32[1,64,512]{2,1,0:T(8,128)S(1)}, f32[1,64,512]{2,1,0:T(8,128)}, u32[]{:S(2)}) copy-start(f32[1,64,512]{2,1,0:T(8,128)} %param.4) | copy-start | bytes 393220
  2.0 24.3 %collective-permute-start.1 = (f32[8,128,128]{2,1,0:T(8,128)S(1)}, f32[8,128,128]{2,1,0:T(8,128)S(1)}, u32[]{:S(2)}, u32[]{:S(2)}) collective-permute-start(f32[8,128,128]{2,1,0:T(8,128)S(1)} %get-tuple-element.35.refs_1_), channel_id=1, source_target_pairs={{0,72},{1,73},{2,74},{3,75},{4,76},{5,77},{6,78},{7,79},{8,0},{9,1... | collective-permute-start | bytes 1572872 | tf_op jit(solution)/shard_map/ppermute | solution.py:371
  5.1 21.1 %collective-permute-start = (f32[8,128,128]{2,1,0:T(8,128)S(1)}, f32[8,128,128]{2,1,0:T(8,128)S(1)}, u32[]{:S(2)}, u32[]{:S(2)}) collective-permute-start(f32[8,128,128]{2,1,0:T(8,128)S(1)} %get-tuple-element.37.refs_0_), channel_id=1, source_target_pairs={{0,8},{1,9},{2,10},{3,11},{4,12},{5,13},{6,14},{7,15},{8,64},{9,65... | collective-permute-start | bytes 1572872 | tf_op jit(solution)/shard_map/ppermute | solution.py:370
  26.3 29.5 %all-to-all-start.1 = ((f32[16,128,128]{2,1,0:T(8,128)}), f32[16,128,128]{2,1,0:T(8,128)S(1)}, u32[]{:S(2)}, u32[]{:S(2)}) async-start(f32[16,128,128]{2,1,0:T(8,128)} %get-tuple-element.33), calls=%async_computation.1 | async-start | bytes 2097152 | tf_op jit(solution)/shard_map/all_to_all | solution.py:49
  31.6 16.3 %collective-permute-start.2 = (f32[8,128,128]{2,1,0:T(8,128)S(1)}, f32[8,128,128]{2,1,0:T(8,128)}, u32[]{:S(2)}, u32[]{:S(2)}) collective-permute-start(f32[8,128,128]{2,1,0:T(8,128)S(1)} %get-tuple-element.35.refs_1_), channel_id=1, source_target_pairs={{0,8},{1,9},{2,10},{3,11},{4,12},{5,13},{6,14},{7,15},{8,64},{9,65... | collective-permute-start | bytes 1572872 | tf_op jit(solution)/shard_map/ppermute | solution.py:396
  31.7 16.2 %collective-permute-start.5 = (f32[8,128,128]{2,1,0:T(8,128)S(1)}, f32[8,128,128]{2,1,0:T(8,128)}, u32[]{:S(2)}, u32[]{:S(2)}) collective-permute-start(f32[8,128,128]{2,1,0:T(8,128)S(1)} %get-tuple-element.37.refs_0_), channel_id=1, source_target_pairs={{0,72},{1,73},{2,74},{3,75},{4,76},{5,77},{6,78},{7,79},{8,0},{9,1... | collective-permute-start | bytes 1572872 | tf_op jit(solution)/shard_map/ppermute | solution.py:397
  34.9 20.8 %collective-permute-start.3 = (f32[8,128,128]{2,1,0:T(8,128)S(1)}, f32[8,128,128]{2,1,0:T(8,128)}, u32[]{:S(2)}, u32[]{:S(2)}) collective-permute-start(f32[8,128,128]{2,1,0:T(8,128)S(1)} %collective-permute-done.refs_2_), channel_id=1, source_target_pairs={{0,8},{1,9},{2,10},{3,11},{4,12},{5,13},{6,14},{7,15},{8,64},{9,65... | collective-permute-start | bytes 1572872 | tf_op jit(solution)/shard_map/ppermute | solution.py:394
  34.9 20.8 %collective-permute-start.4 = (f32[8,128,128]{2,1,0:T(8,128)S(1)}, f32[8,128,128]{2,1,0:T(8,128)}, u32[]{:S(2)}, u32[]{:S(2)}) collective-permute-start(f32[8,128,128]{2,1,0:T(8,128)S(1)} %collective-permute-done.1.refs_7_), channel_id=1, source_target_pairs={{0,72},{1,73},{2,74},{3,75},{4,76},{5,77},{6,78},{7,79},{8,0},{9,1... | collective-permute-start | bytes 1572872 | tf_op jit(solution)/shard_map/ppermute | solution.py:395
  60.9 2.2 %collective-permute-start.7 = (f32[16,64,128]{2,1,0:T(8,128)S(1)}, f32[16,64,128]{2,1,0:T(8,128)S(1)}, u32[]{:S(2)}, u32[]{:S(2)}) collective-permute-start(f32[16,64,128]{2,1,0:T(8,128)S(1)} %get-tuple-element.40), channel_id=1, source_target_pairs={{0,1},{1,0},{2,3},{3,2},{4,5},{5,4},{6,7},{7,6},{8,9},{9,8},{10,11... | collective-permute-start | bytes 1572872 | tf_op jit(solution)/shard_map/ppermute | solution.py:250
  62.5 3.0 %collective-permute-start.6 = (f32[1024,128]{1,0:T(8,128)S(1)}, f32[1024,128]{1,0:T(8,128)S(1)}, u32[]{:S(2)}, u32[]{:S(2)}) collective-permute-start(f32[1024,128]{1,0:T(8,128)S(1)} %mate.3), channel_id=1, source_target_pairs={{0,1},{1,0},{2,3},{3,2},{4,5},{5,4},{6,7},{7,6},{8,9},{9,8},{10,11... | collective-permute-start | bytes 1572872 | tf_op jit(solution)/shard_map/ppermute | solution.py:251
  65.4 1.2 collective-permute-start.8
  112.8 2.7 %collective-permute-start.10 = (f32[16,128,128]{2,1,0:T(8,128)S(1)}, f32[16,128,128]{2,1,0:T(8,128)S(1)}, u32[]{:S(2)}, u32[]{:S(2)}) collective-permute-start(f32[16,128,128]{2,1,0:T(8,128)S(1)} %all_to_all.42.recv), channel_id=1, source_target_pairs={{0,1},{1,0},{2,3},{3,2},{4,5},{5,4},{6,7},{7,6},{8,9},{9,8},{10,11... | collective-permute-start | bytes 3145736 | tf_op jit(solution)/shard_map/ppermute | solution.py:250
  114.4 3.7 %collective-permute-start.9 = (f32[1024,128]{1,0:T(8,128)S(1)}, f32[1024,128]{1,0:T(8,128)S(1)}, u32[]{:S(2)}, u32[]{:S(2)}) collective-permute-start(f32[1024,128]{1,0:T(8,128)S(1)} %mate.4), channel_id=1, source_target_pairs={{0,1},{1,0},{2,3},{3,2},{4,5},{5,4},{6,7},{7,6},{8,9},{9,8},{10,11... | collective-permute-start | bytes 1572872 | tf_op jit(solution)/shard_map/ppermute | solution.py:251
  117.8 1.2 collective-permute-start.11
  161.8 2.7 %collective-permute-start.13 = (f32[16,128,128]{2,1,0:T(8,128)S(1)}, f32[16,128,128]{2,1,0:T(8,128)S(1)}, u32[]{:S(2)}, u32[]{:S(2)}) collective-permute-start(f32[16,128,128]{2,1,0:T(8,128)S(1)} %all_to_all.44.recv), channel_id=1, source_target_pairs={{0,1},{1,0},{2,3},{3,2},{4,5},{5,4},{6,7},{7,6},{8,9},{9,8},{10,11... | collective-permute-start | bytes 3145736 | tf_op jit(solution)/shard_map/ppermute | solution.py:250
  163.3 3.7 %collective-permute-start.12 = (f32[1024,128]{1,0:T(8,128)S(1)}, f32[1024,128]{1,0:T(8,128)S(1)}, u32[]{:S(2)}, u32[]{:S(2)}) collective-permute-start(f32[1024,128]{1,0:T(8,128)S(1)} %mate.5), channel_id=1, source_target_pairs={{0,1},{1,0},{2,3},{3,2},{4,5},{5,4},{6,7},{7,6},{8,9},{9,8},{10,11... | collective-permute-start | bytes 1572872 | tf_op jit(solution)/shard_map/ppermute | solution.py:251
  166.8 1.2 collective-permute-start.14

commit v3 on v2

--- a/solution.py
+++ b/solution.py
@@ -57,56 +57,42 @@
 
 def assemble_body(codes, *refs):
     pieces, recv, (hi, lo, share, dense) = refs[:8], refs[8], refs[9:]
-    step = pl.program_id(0)
-
-    @pl.when(step == 0)
-    def _():
-        share[...] = recv[:, :64, :]
-        dense[...] = jnp.zeros_like(dense)
-        y = codes[64]
-        for i, ref in enumerate(pieces):
-            base = ((y - i // 2) & 3) * 16 + (i % 2) * 8
-
-            def put(b, carry, ref=ref, base=base):
-                code = codes[base + b]
-
-                @pl.when(code >= 0)
-                def _():
-                    ro = pl.multiple_of((code >> 3) * 128, 128)
-                    co = pl.multiple_of((code & 7) * 128, 128)
-                    dense[pl.ds(ro, 128), pl.ds(co, 128)] += ref[b]
-
-                return carry
-
-            lax.fori_loop(0, 8, put, 0)
+    share[...] = recv[:, :64, :]
+    dense[...] = jnp.zeros_like(dense)
+    y = codes[64]
+    for i, ref in enumerate(pieces):
+        base = ((y - i // 2) & 3) * 16 + (i % 2) * 8
+        for b in range(8):
+            code = codes[base + b]
+
+            @pl.when(code >= 0)
+            def _(ref=ref, b=b, code=code):
+                ro = pl.multiple_of((code >> 3) * 128, 128)
+                co = pl.multiple_of((code & 7) * 128, 128)
+                dense[pl.ds(ro, 128), pl.ds(co, 128)] += ref[b]
 
     def narrow(i, carry):
-        rows = pl.ds(pl.multiple_of(i * 32, 32), 32)
-        value = dense[pl.ds(pl.multiple_of(step * 256 + i * 32, 32), 32), :]
+        rows = pl.ds(pl.multiple_of(i * 128, 128), 128)
+        value = dense[rows, :]
         top = value.astype(jnp.bfloat16)
         hi[rows, :] = top
         lo[rows, :] = (value - top.astype(jnp.float32)).astype(jnp.bfloat16)
         return carry
 
-    lax.fori_loop(0, 8, narrow, 0)
-
-
-def whole(*shape):
-    return pl.BlockSpec(shape, lambda i: (0,) * len(shape))
+    lax.fori_loop(0, 16, narrow, 0)
+
+
+VMEM = pl.BlockSpec(memory_space=pltpu.VMEM)
 
 
 def assemble(codes, pieces, recv):
     half = jax.ShapeDtypeStruct((2048, 1024), jnp.bfloat16)
     return call(
         assemble_body,
-        limit=26,
-        grid=(8,),
+        limit=24,
         out_shape=(half, half, jax.ShapeDtypeStruct((16, 64, 128), jnp.float32)),
-        in_specs=[pl.BlockSpec(memory_space=pltpu.SMEM)]
-        + [whole(8, 128, 128)] * 8
-        + [whole(16, 128, 128)],
-        out_specs=(pl.BlockSpec((256, 1024), lambda i: (i, 0)),) * 2
-        + (whole(16, 64, 128),),
+        in_specs=[pl.BlockSpec(memory_space=pltpu.SMEM)] + [VMEM] * 9,
+        out_specs=(VMEM,) * 3,
         scratch_shapes=[pltpu.VMEM((2048, 1024), jnp.float32)],
         name="assemble",
     )(codes, *pieces, recv)
@@ -122,7 +108,7 @@
 
 
 def chunk(ref, j):
-    return ref[:, pl.ds(j * 16, 16), :].reshape(256, 128)
+    return ref[:, j * 16 : j * 16 + 16, :].reshape(256, 128)
 
 
 def part_right(recv, right):
@@ -133,117 +119,97 @@
 
 
 def forward(hi, lo, right):
-    wide = dot(hi[...], right[...])
-    return wide[:, :128] + wide[:, 128:] + dot(lo[...], right[:, :128])
+    wide = dot(hi, right[...])
+    return wide[:, :128] + wide[:, 128:] + dot(lo, right[:, :128])
 
 
 def mate_body(recv, hi, lo, out, right):
-    @pl.when(pl.program_id(0) == 0)
-    def _():
-        part_right(recv, right)
-
-    out[...] = forward(hi, lo, right)
-
-
-def rows_at(first):
-    return pl.BlockSpec((512, 1024), lambda i: (first + i, 0))
+    part_right(recv, right)
+    for i in range(2):
+        rows = slice(1024 + i * 512, 1536 + i * 512)
+        out[i * 512 : (i + 1) * 512, :] = forward(hi[rows, :], lo[rows, :], right)
 
 
 def mate(recv, hi, lo):
     return call(
         mate_body,
-        grid=(2,),
         out_shape=jax.ShapeDtypeStruct((1024, 128), jnp.float32),
-        in_specs=[whole(16, 128, 128), rows_at(2), rows_at(2)],
-        out_specs=pl.BlockSpec((512, 128), lambda i: (i, 0)),
+        in_specs=[VMEM] * 3,
+        out_specs=VMEM,
         scratch_shapes=[pltpu.VMEM((1024, 256), jnp.bfloat16)],
         name="mate",
     )(recv, hi, lo)
 
 
-def mirror_body(recv, other, hi0, lo0, hi1, lo1, sums, out, scalars, back):
-    step = pl.program_id(0)
-
-    @pl.when(step == 0)
-    def _():
-        back[...] = jnp.zeros_like(back)
-
-    for ref, hi, lo in ((recv, hi0, lo0), (other, hi1, lo1)):
-        pairs = [parted(chunk(ref, step * 2 + c).T) for c in range(2)]
+def mirror_body(recv, other, hi, lo, sums, out, scalars, back):
+    for i in range(4):
+        ref = (recv, other)[i // 2]
+        pairs = [parted(chunk(ref, (i % 2) * 2 + c).T) for c in range(2)]
         top = jnp.concatenate([pair[0] for pair in pairs], axis=1)
         rest = jnp.concatenate([pair[1] for pair in pairs], axis=1)
-        wide = dot(jnp.concatenate([top, rest], axis=0), hi[...])
-        back[...] += wide[:128] + wide[128:] + dot(top, lo[...])
-
-    @pl.when(step == 1)
-    def _():
-        out[...] = back[...].T
-        curve = jnp.zeros((8, 128), jnp.float32)
-        for s in range(4):
-            piece = chunk(recv, 4 + s) * out[s * 256 : (s + 1) * 256]
-            curve = curve + jnp.sum(piece.reshape(32, 8, 128), axis=0)
-        place = lax.broadcasted_iota(jnp.int32, (8, 128), 0)
-        scalars[...] = jnp.where(place == 2, row_sum(curve) * (2 * DIFFUSION), sums[...])
+        rows = slice(i * 512, (i + 1) * 512)
+        wide = dot(jnp.concatenate([top, rest], axis=0), hi[rows, :])
+        part = wide[:128] + wide[128:] + dot(top, lo[rows, :])
+        back[...] = part if i == 0 else back[...] + part
+    out[...] = back[...].T
+    curve = jnp.zeros((8, 128), jnp.float32)
+    for s in range(4):
+        piece = chunk(recv, 4 + s) * out[s * 256 : (s + 1) * 256]
+        curve = curve + jnp.sum(piece.reshape(32, 8, 128), axis=0)
+    place = lax.broadcasted_iota(jnp.int32, (8, 128), 0)
+    scalars[...] = jnp.where(place == 2, row_sum(curve) * (2 * DIFFUSION), sums[...])
 
 
 def mirror(recv, other, hi, lo, sums):
     return call(
         mirror_body,
-        grid=(2,),
-        limit=20,
         out_shape=(
             jax.ShapeDtypeStruct((1024, 128), jnp.float32),
             jax.ShapeDtypeStruct((8, 128), jnp.float32),
         ),
-        in_specs=[whole(16, 128, 128), whole(*other.shape)]
-        + [rows_at(0), rows_at(0), rows_at(2), rows_at(2), whole(8, 128)],
-        out_specs=(whole(1024, 128), whole(8, 128)),
+        in_specs=[VMEM] * 5,
+        out_specs=(VMEM, VMEM),
         scratch_shapes=[pltpu.VMEM((128, 1024), jnp.float32)],
         name="mirror",
-    )(recv, other, hi, lo, hi, lo, sums)
-
-
-def gathered_body(recv, hi, lo, theirs, mirrored, mine, mates, out, right):
-    step = pl.program_id(0)
-
-    @pl.when(step == 0)
-    def _():
-        part_right(recv, right)
-        for s in range(4):
-            out[:, 64 + s * 16 : 80 + s * 16, :] = mirrored[s * 256 : (s + 1) * 256].reshape(16, 16, 128)
-
-    part = forward(hi, lo, right) + theirs[...]
-    for c in range(2):
-        j = step * 2 + c
-        piece = part[c * 256 : (c + 1) * 256]
-        out[:, pl.ds(j * 16, 16), :] = piece.reshape(16, 16, 128)
-
-    @pl.when(step == 1)
-    def _():
-        row = mine[...] + mates[...]
-        out[:, 128:136, :] = jnp.broadcast_to(row[None], (16, 8, 128))
-
-
-def gathered(recv, hi, lo, theirs, mirrored, mine, mates):
-    return call(
-        gathered_body,
-        grid=(2,),
+    )(recv, other, hi, lo, sums)
+
+
+def own_body(recv, hi, lo, after, out, right):
+    part_right(recv, right)
+    for i in range(2):
+        rows = slice(i * 512, (i + 1) * 512)
+        out[rows, :] = forward(hi[rows, :], lo[rows, :], right)
+
+
+def own_rows(recv, hi, lo, after):
+    return call(
+        own_body,
+        out_shape=jax.ShapeDtypeStruct((1024, 128), jnp.float32),
+        in_specs=[VMEM] * 4,
+        out_specs=VMEM,
+        scratch_shapes=[pltpu.VMEM((1024, 256), jnp.bfloat16)],
+        name="own_rows",
+    )(recv, hi, lo, after)
+
+
+def join_body(ours, theirs, mirrored, mine, mates, out):
+    for s in range(4):
+        rows = slice(s * 256, (s + 1) * 256)
+        part = ours[rows, :] + theirs[rows, :]
+        out[:, s * 16 : s * 16 + 16, :] = part.reshape(16, 16, 128)
+        out[:, 64 + s * 16 : 80 + s * 16, :] = mirrored[rows, :].reshape(16, 16, 128)
+    row = mine[...] + mates[...]
+    out[:, 128:136, :] = jnp.broadcast_to(row[None], (16, 8, 128))
+
+
+def join(ours, theirs, mirrored, mine, mates):
+    return call(
+        join_body,
         out_shape=jax.ShapeDtypeStruct((16, 136, 128), jnp.float32),
-        in_specs=[
-            whole(16, 128, 128),
-            rows_at(0),
-            rows_at(0),
-            pl.BlockSpec((512, 128), lambda i: (i, 0)),
-            whole(1024, 128),
-            whole(8, 128),
-            whole(8, 128),
-        ],
-        out_specs=whole(16, 136, 128),
-        scratch_shapes=[
-            pltpu.VMEM((1024, 256), jnp.bfloat16),
-        ],
-        name="gathered",
-    )(recv, hi, lo, theirs, mirrored, mine, mates)
+        in_specs=[VMEM] * 5,
+        out_specs=VMEM,
+        name="join",
+    )(ours, theirs, mirrored, mine, mates)
 
 
 def multiply(recv, share, sums, hi, lo):
@@ -251,7 +217,8 @@
     theirs = lax.ppermute(mate(recv, hi, lo), RC, SWAP)
     mirrored, mine = mirror(recv, other, hi, lo, sums)
     mates = lax.ppermute(mine, RC, SWAP)
-    return gathered(recv, hi, lo, theirs, mirrored, mine, mates)
+    ours = own_rows(recv, hi, lo, mine)
+    return join(ours, theirs, mirrored, mine, mates)
 
 
 def spread(field, send):
@@ -361,6 +328,18 @@
     )(*operands)
 
 
+def deliver_body(recv, *outs):
+    for y in range(4):
+        for z in range(4):
+            for which, out in enumerate(outs):
+                out[0, z * 16 : z * 16 + 16, y * 128 : y * 128 + 128] = recv[y * 4 + z, which]
+
+
+def deliver(recv):
+    out = jax.ShapeDtypeStruct((1, 64, 512), jnp.float32)
+    return call(deliver_body, out_shape=(out, out), name="deliver")(recv)
+
+
 def shards(right_side, affinity_blocks, block_coords, block_counts):
     r = lax.axis_index("row")
     c = lax.axis_index("col")
@@ -407,8 +386,7 @@
             send, sums = made[0], made[6]
             state = made[1:6]
     done = exchange(made[0], SHEETS)
-    done = done.reshape(4, 4, 2, 16, 128).transpose(2, 1, 3, 0, 4).reshape(2, 1, 64, 512)
-    return done[0], done[1]
+    return tuple(deliver(done))
 
 
 def solution(mesh):

time: 207 us -> 202 us (0.976)
  waiting for transfers between devices: 21.6 us -> 18.9 us
    ppermute x3, waiting for transfers between devices: 3.17 us -> 0.01 us  [multiply(): mates = lax.ppermute(mine, RC, SWAP)]
    pallas_call x10 -> x14, Pallas kernels: 21.5 us -> 19.5 us  [the longest x3 5.94 us: mirror(): call(mirror_body, out_shape=(jax.ShapeDtypeStruct((1024, 128), jnp.float3...]
  transfers between devices with their start and end apart: 16 -> 16, of which waited for: 7 -> 4; matrix products, arithmetic and copies ran while one was open for 0% -> 0% of each run, Pallas kernels for 6% -> 7%
where the time goes in v3:
time: 202 us; the launch traced here: 201 us
  blocking collectives  141 us (70%)
  Pallas kernels  21 us (10%)
  waiting for transfers between devices  18.9 us (9%)
  starting transfers between devices  17.5 us (9%)
    all_to_all x7, blocking collectives, exchange(): return lax.all_to_all(send, RC, 0, 0, axis_index_groups=groups, tiled=True)  141 us
    ppermute x1, waiting for transfers between devices, shards(): left1 = lax.ppermute(later1, RC, shift_y(1))  9.52 us
    ppermute x1, waiting for transfers between devices, shards(): far0 = lax.ppermute(left0, RC, shift_y(1))  7.89 us
    pallas_call x3, Pallas kernels, mirror(): call(mirror_body, out_shape=(jax.ShapeDtypeStruct((1024, 128), jnp.float3...  5.94 us
    all_to_all x1, starting transfers between devices, exchange(): return lax.all_to_all(send, RC, 0, 0, axis_index_groups=groups, tiled=True)  5.31 us
    pallas_call x1, Pallas kernels, assemble(): call(assemble_body, limit=24, out_shape=(half, half, jax.ShapeDtypeStruct...  4.57 us
  transfers between devices with their start and end apart: 16, of which 4 were waited for; matrix products, arithmetic and copies ran while one was open for 0% of the time, Pallas kernels for 7%

profile of v3, /device:TPU:0, one launch (start us, length us, event | category | flops | bytes accessed | tf_op | source)
XLA Modules:
  0.0 201.1 jit_solution(11529910493566933099)
XLA Ops:
  0.7 1.3 slice_bitcast_fusion
  2.0 3.2 %collective-permute-start.1 = (f32[8,128,128]{2,1,0:T(8,128)S(1)}, f32[8,128,128]{2,1,0:T(8,128)S(1)}, u32[]{:S(2)}, u32[]{:S(2)}) collective-permute-start(f32[8,128,128]{2,1,0:T(8,128)S(1)} %get-tuple-element.35.refs_1_), channel_id=1, source_target_pairs={{0,72},{1,73},{2,74},{3,75},{4,76},{5,77},{6,78},{7,79},{8,0},{9,1... | collective-permute-start | bytes 1572872 | tf_op jit(solution)/shard_map/ppermute | solution.py:350
  5.8 19.4 %all_to_all.40.recv.refs_1_ = f32[16,24,128]{2,1,0:T(8,128)S(1)} all-to-all(f32[16,24,128]{2,1,0:T(8,128)S(1)} %pad_maximum_fusion), channel_id=1, replica_groups={{0,2,4,6,8,10,12,14,64,66,68,70,72,74,76,78},{1,3,5,7,9,11,13,15,65,67,..., dimensions={0} | all-to-all | bytes 393216 | tf_op jit(solution)/shard_map/all_to_all | solution.py:49
  26.3 5.3 %all-to-all-start.1 = ((f32[16,128,128]{2,1,0:T(8,128)}), f32[16,128,128]{2,1,0:T(8,128)S(1)}, u32[]{:S(2)}, u32[]{:S(2)}) async-start(f32[16,128,128]{2,1,0:T(8,128)} %get-tuple-element.33), calls=%async_computation.1 | async-start | bytes 2097152 | tf_op jit(solution)/shard_map/all_to_all | solution.py:49
  31.7 3.2 %collective-permute-start.5 = (f32[8,128,128]{2,1,0:T(8,128)S(1)}, f32[8,128,128]{2,1,0:T(8,128)}, u32[]{:S(2)}, u32[]{:S(2)}) collective-permute-start(f32[8,128,128]{2,1,0:T(8,128)S(1)} %get-tuple-element.37.refs_0_), channel_id=1, source_target_pairs={{0,72},{1,73},{2,74},{3,75},{4,76},{5,77},{6,78},{7,79},{8,0},{9,1... | collective-permute-start | bytes 1572872 | tf_op jit(solution)/shard_map/ppermute | solution.py:376
  34.9 3.2 %collective-permute-start.4 = (f32[8,128,128]{2,1,0:T(8,128)S(1)}, f32[8,128,128]{2,1,0:T(8,128)}, u32[]{:S(2)}, u32[]{:S(2)}) collective-permute-start(f32[8,128,128]{2,1,0:T(8,128)S(1)} %collective-permute-done.1.refs_7_), channel_id=1, source_target_pairs={{0,72},{1,73},{2,74},{3,75},{4,76},{5,77},{6,78},{7,79},{8,0},{9,1... | collective-permute-start | bytes 1572872 | tf_op jit(solution)/shard_map/ppermute | solution.py:374
  38.3 9.5 %collective-permute-done.2.refs_3_ = f32[8,128,128]{2,1,0:T(8,128)} collective-permute-done((f32[8,128,128]{2,1,0:T(8,128)S(1)}, f32[8,128,128]{2,1,0:T(8,128)}, u32[]{:S(2)}, u32[]{:S(2)}) %collective-permute-start.2) | collective-permute-done | bytes 524320 | tf_op jit(solution)/shard_map/ppermute | solution.py:375
  47.9 7.9 %collective-permute-done.3.refs_4_ = f32[8,128,128]{2,1,0:T(8,128)} collective-permute-done((f32[8,128,128]{2,1,0:T(8,128)S(1)}, f32[8,128,128]{2,1,0:T(8,128)}, u32[]{:S(2)}, u32[]{:S(2)}) %collective-permute-start.3) | collective-permute-done | bytes 524320 | tf_op jit(solution)/shard_map/ppermute | solution.py:373
  55.7 4.6 %assemble.1 = (bf16[2048,1024]{1,0:T(8,128)(2,1)S(1)}, bf16[2048,1024]{1,0:T(8,128)(2,1)S(1)}, f32[16,64,128]{2,1,0:T(8,128)S(1)}) custom-call(s32[65]{0:T(128)S(1)} %pad_add_fusion.codes, f32[8,128,128]{2,1,0:T(8,128)S(1)} %get-tuple-element.37.refs_0_, f32[8,128,128]{2,1,0:T(8,128)S(1)} %get-tuple-element.35.refs_1_, ...), custom_call_target="tpu_custom_call" | custom-call | tf_op jit(solution)/shard_map/assemble/pallas_call | solution.py:90
  60.4 1.3 mate.3
  62.3 2.0 mirror.3
  64.5 1.3 own_rows.3.ours
  66.0 25.2 %all_to_all.41.refs_0_ = f32[16,136,128]{2,1,0:T(8,128)S(1)} all-to-all(f32[16,136,128]{2,1,0:T(8,128)S(1)} %join.3), channel_id=1, replica_groups={{0,2,4,6,16,18,20,22,32,34,36,38,48,50,52,54},{1,3,5,7,17,19,21,23,33,3..., dimensions={0} | all-to-all | bytes 2228224 | tf_op jit(solution)/shard_map/all_to_all | solution.py:49
  91.3 19.8 %all_to_all.42.recv = f32[16,128,128]{2,1,0:T(8,128)S(1)} all-to-all(f32[16,128,128]{2,1,0:T(8,128)S(1)} %get-tuple-element.44), channel_id=1, replica_groups={{0,2,4,6,16,18,20,22,32,34,36,38,48,50,52,54},{1,3,5,7,17,19,21,23,33,3..., dimensions={0} | all-to-all | bytes 2097152 | tf_op jit(solution)/shard_map/all_to_all | solution.py:49
  111.1 1.3 mate.4
  113.8 2.0 mirror.4
  116.0 1.3 own_rows.4.ours
  117.4 21.6 %all_to_all.43.refs_0_ = f32[16,136,128]{2,1,0:T(8,128)S(1)} all-to-all(f32[16,136,128]{2,1,0:T(8,128)S(1)} %join.4), channel_id=1, replica_groups={{0,2,4,6,16,18,20,22,32,34,36,38,48,50,52,54},{1,3,5,7,17,19,21,23,33,3..., dimensions={0} | all-to-all | bytes 2228224 | tf_op jit(solution)/shard_map/all_to_all | solution.py:49
  139.3 19.7 %all_to_all.44.recv = f32[16,128,128]{2,1,0:T(8,128)S(1)} all-to-all(f32[16,128,128]{2,1,0:T(8,128)S(1)} %get-tuple-element.53), channel_id=1, replica_groups={{0,2,4,6,16,18,20,22,32,34,36,38,48,50,52,54},{1,3,5,7,17,19,21,23,33,3..., dimensions={0} | all-to-all | bytes 2097152 | tf_op jit(solution)/shard_map/all_to_all | solution.py:49
  159.0 1.3 mate.5
  161.6 2.0 mirror.5
  163.8 1.3 own_rows.5.ours
  165.3 21.6 %all_to_all.45.refs_0_ = f32[16,136,128]{2,1,0:T(8,128)S(1)} all-to-all(f32[16,136,128]{2,1,0:T(8,128)S(1)} %join.5), channel_id=1, replica_groups={{0,2,4,6,16,18,20,22,32,34,36,38,48,50,52,54},{1,3,5,7,17,19,21,23,33,3..., dimensions={0} | all-to-all | bytes 2228224 | tf_op jit(solution)/shard_map/all_to_all | solution.py:49
  187.0 13.4 %all_to_all.46.recv = f32[16,2,16,128]{3,2,1,0:T(8,128)S(1)} all-to-all(f32[16,2,16,128]{3,2,1,0:T(8,128)S(1)} %update.5), channel_id=1, replica_groups={{0,2,4,6,8,10,12,14,64,66,68,70,72,74,76,78},{1,3,5,7,9,11,13,15,65,67,..., dimensions={0} | all-to-all | bytes 524288 | tf_op jit(solution)/shard_map/all_to_all | solution.py:49
  (58 shorter events, 7.4 us)
Async XLA Ops:
  0.6 4.5 %copy-start.2 = (s32[2,1]{0,1:T(1,128)S(1)}, s32[2,1]{0,1:T(1,128)}, u32[]{:S(2)}) copy-start(s32[2,1]{0,1:T(1,128)} %param.7) | copy-start | bytes 28
  0.6 4.8 %copy-start.1 = (s32[2,1,8,2]{2,3,1,0:T(2,128)S(1)}, s32[2,1,8,2]{2,3,1,0:T(2,128)}, u32[]{:S(2)}) copy-start(s32[2,1,8,2]{2,3,1,0:T(2,128)} %param.6) | copy-start | bytes 388
  0.7 5.0 %copy-start = (f32[1,64,512]{2,1,0:T(8,128)S(1)}, f32[1,64,512]{2,1,0:T(8,128)}, u32[]{:S(2)}) copy-start(f32[1,64,512]{2,1,0:T(8,128)} %param.4) | copy-start | bytes 393220
  2.0 24.3 %collective-permute-start.1 = (f32[8,128,128]{2,1,0:T(8,128)S(1)}, f32[8,128,128]{2,1,0:T(8,128)S(1)}, u32[]{:S(2)}, u32[]{:S(2)}) collective-permute-start(f32[8,128,128]{2,1,0:T(8,128)S(1)} %get-tuple-element.35.refs_1_), channel_id=1, source_target_pairs={{0,72},{1,73},{2,74},{3,75},{4,76},{5,77},{6,78},{7,79},{8,0},{9,1... | collective-permute-start | bytes 1572872 | tf_op jit(solution)/shard_map/ppermute | solution.py:350
  5.1 21.1 %collective-permute-start = (f32[8,128,128]{2,1,0:T(8,128)S(1)}, f32[8,128,128]{2,1,0:T(8,128)S(1)}, u32[]{:S(2)}, u32[]{:S(2)}) collective-permute-start(f32[8,128,128]{2,1,0:T(8,128)S(1)} %get-tuple-element.37.refs_0_), channel_id=1, source_target_pairs={{0,8},{1,9},{2,10},{3,11},{4,12},{5,13},{6,14},{7,15},{8,64},{9,65... | collective-permute-start | bytes 1572872 | tf_op jit(solution)/shard_map/ppermute | solution.py:349
  26.3 29.5 %all-to-all-start.1 = ((f32[16,128,128]{2,1,0:T(8,128)}), f32[16,128,128]{2,1,0:T(8,128)S(1)}, u32[]{:S(2)}, u32[]{:S(2)}) async-start(f32[16,128,128]{2,1,0:T(8,128)} %get-tuple-element.33), calls=%async_computation.1 | async-start | bytes 2097152 | tf_op jit(solution)/shard_map/all_to_all | solution.py:49
  31.6 16.3 %collective-permute-start.2 = (f32[8,128,128]{2,1,0:T(8,128)S(1)}, f32[8,128,128]{2,1,0:T(8,128)}, u32[]{:S(2)}, u32[]{:S(2)}) collective-permute-start(f32[8,128,128]{2,1,0:T(8,128)S(1)} %get-tuple-element.35.refs_1_), channel_id=1, source_target_pairs={{0,8},{1,9},{2,10},{3,11},{4,12},{5,13},{6,14},{7,15},{8,64},{9,65... | collective-permute-start | bytes 1572872 | tf_op jit(solution)/shard_map/ppermute | solution.py:375
  31.7 16.2 %collective-permute-start.5 = (f32[8,128,128]{2,1,0:T(8,128)S(1)}, f32[8,128,128]{2,1,0:T(8,128)}, u32[]{:S(2)}, u32[]{:S(2)}) collective-permute-start(f32[8,128,128]{2,1,0:T(8,128)S(1)} %get-tuple-element.37.refs_0_), channel_id=1, source_target_pairs={{0,72},{1,73},{2,74},{3,75},{4,76},{5,77},{6,78},{7,79},{8,0},{9,1... | collective-permute-start | bytes 1572872 | tf_op jit(solution)/shard_map/ppermute | solution.py:376
  34.9 20.8 %collective-permute-start.3 = (f32[8,128,128]{2,1,0:T(8,128)S(1)}, f32[8,128,128]{2,1,0:T(8,128)}, u32[]{:S(2)}, u32[]{:S(2)}) collective-permute-start(f32[8,128,128]{2,1,0:T(8,128)S(1)} %collective-permute-done.refs_2_), channel_id=1, source_target_pairs={{0,8},{1,9},{2,10},{3,11},{4,12},{5,13},{6,14},{7,15},{8,64},{9,65... | collective-permute-start | bytes 1572872 | tf_op jit(solution)/shard_map/ppermute | solution.py:373
  34.9 20.8 %collective-permute-start.4 = (f32[8,128,128]{2,1,0:T(8,128)S(1)}, f32[8,128,128]{2,1,0:T(8,128)}, u32[]{:S(2)}, u32[]{:S(2)}) collective-permute-start(f32[8,128,128]{2,1,0:T(8,128)S(1)} %collective-permute-done.1.refs_7_), channel_id=1, source_target_pairs={{0,72},{1,73},{2,74},{3,75},{4,76},{5,77},{6,78},{7,79},{8,0},{9,1... | collective-permute-start | bytes 1572872 | tf_op jit(solution)/shard_map/ppermute | solution.py:374
  60.3 2.0 collective-permute-start.6
  61.8 4.1 %collective-permute-start.7 = (f32[1024,128]{1,0:T(8,128)S(1)}, f32[1024,128]{1,0:T(8,128)S(1)}, u32[]{:S(2)}, u32[]{:S(2)}) collective-permute-start(f32[1024,128]{1,0:T(8,128)S(1)} %mate.3), channel_id=1, source_target_pairs={{0,1},{1,0},{2,3},{3,2},{4,5},{5,4},{6,7},{7,6},{8,9},{9,8},{10,11... | collective-permute-start | bytes 1572872 | tf_op jit(solution)/shard_map/ppermute | solution.py:217
  64.3 1.5 collective-permute-start.8
  111.1 2.7 %collective-permute-start.9 = (f32[16,128,128]{2,1,0:T(8,128)S(1)}, f32[16,128,128]{2,1,0:T(8,128)S(1)}, u32[]{:S(2)}, u32[]{:S(2)}) collective-permute-start(f32[16,128,128]{2,1,0:T(8,128)S(1)} %all_to_all.42.recv), channel_id=1, source_target_pairs={{0,1},{1,0},{2,3},{3,2},{4,5},{5,4},{6,7},{7,6},{8,9},{9,8},{10,11... | collective-permute-start | bytes 3145736 | tf_op jit(solution)/shard_map/ppermute | solution.py:216
  112.5 4.9 %collective-permute-start.10 = (f32[1024,128]{1,0:T(8,128)S(1)}, f32[1024,128]{1,0:T(8,128)S(1)}, u32[]{:S(2)}, u32[]{:S(2)}) collective-permute-start(f32[1024,128]{1,0:T(8,128)S(1)} %mate.4), channel_id=1, source_target_pairs={{0,1},{1,0},{2,3},{3,2},{4,5},{5,4},{6,7},{7,6},{8,9},{9,8},{10,11... | collective-permute-start | bytes 1572872 | tf_op jit(solution)/shard_map/ppermute | solution.py:217
  115.8 1.6 collective-permute-start.11
  159.0 2.7 %collective-permute-start.12 = (f32[16,128,128]{2,1,0:T(8,128)S(1)}, f32[16,128,128]{2,1,0:T(8,128)S(1)}, u32[]{:S(2)}, u32[]{:S(2)}) collective-permute-start(f32[16,128,128]{2,1,0:T(8,128)S(1)} %all_to_all.44.recv), channel_id=1, source_target_pairs={{0,1},{1,0},{2,3},{3,2},{4,5},{5,4},{6,7},{7,6},{8,9},{9,8},{10,11... | collective-permute-start | bytes 3145736 | tf_op jit(solution)/shard_map/ppermute | solution.py:216
  160.3 4.9 %collective-permute-start.13 = (f32[1024,128]{1,0:T(8,128)S(1)}, f32[1024,128]{1,0:T(8,128)S(1)}, u32[]{:S(2)}, u32[]{:S(2)}) collective-permute-start(f32[1024,128]{1,0:T(8,128)S(1)} %mate.5), channel_id=1, source_target_pairs={{0,1},{1,0},{2,3},{3,2},{4,5},{5,4},{6,7},{7,6},{8,9},{9,8},{10,11... | collective-permute-start | bytes 1572872 | tf_op jit(solution)/shard_map/ppermute | solution.py:217
  163.6 1.6 collective-permute-start.14

commit v4 on v3

--- a/solution.py
+++ b/solution.py
@@ -56,17 +56,20 @@
 
 
 def assemble_body(codes, *refs):
-    pieces, recv, (hi, lo, share, dense) = refs[:8], refs[8], refs[9:]
+    own0, own1, left0, right1, wave, back, recv, hi, lo, share, dense = refs
+    pieces = (
+        (own0, 0), (own1, 0), (left0, 0), (wave, 8), (wave, 0), (back, 0), (back, 8), (right1, 0)
+    )
     share[...] = recv[:, :64, :]
     dense[...] = jnp.zeros_like(dense)
     y = codes[64]
-    for i, ref in enumerate(pieces):
+    for i, (ref, first) in enumerate(pieces):
         base = ((y - i // 2) & 3) * 16 + (i % 2) * 8
         for b in range(8):
             code = codes[base + b]
 
             @pl.when(code >= 0)
-            def _(ref=ref, b=b, code=code):
+            def _(ref=ref, b=first + b, code=code):
                 ro = pl.multiple_of((code >> 3) * 128, 128)
                 co = pl.multiple_of((code & 7) * 128, 128)
                 dense[pl.ds(ro, 128), pl.ds(co, 128)] += ref[b]
@@ -91,7 +94,7 @@
         assemble_body,
         limit=24,
         out_shape=(half, half, jax.ShapeDtypeStruct((16, 64, 128), jnp.float32)),
-        in_specs=[pl.BlockSpec(memory_space=pltpu.SMEM)] + [VMEM] * 9,
+        in_specs=[pl.BlockSpec(memory_space=pltpu.SMEM)] + [VMEM] * 7,
         out_specs=(VMEM,) * 3,
         scratch_shapes=[pltpu.VMEM((2048, 1024), jnp.float32)],
         name="assemble",
@@ -369,13 +372,13 @@
     send, sums = start(recv)
     state = (recv,)
     send, left0, right1 = lax.optimization_barrier((send, left0, right1))
-    later0, later1, recv = lax.optimization_barrier((own0, own1, recv))
-    far0 = lax.ppermute(left0, RC, shift_y(1))
-    far1 = lax.ppermute(right1, RC, shift_y(3))
-    left1 = lax.ppermute(later1, RC, shift_y(1))
-    right0 = lax.ppermute(later0, RC, shift_y(3))
+    wave, back, recv = lax.optimization_barrier(
+        (jnp.concatenate([left0, own1]), jnp.concatenate([right1, own0]), recv)
+    )
+    wave = lax.ppermute(wave, RC, shift_y(1))
+    back = lax.ppermute(back, RC, shift_y(3))
     got = exchange(send, PLANES)
-    pieces = (own0, own1, left0, left1, far0, far1, right0, right1)
+    pieces = (own0, own1, left0, right1, wave, back)
     hi, lo, share = assemble(codes, pieces, got)
     for step in range(ITERS):
         if step:

time: 202 us -> 197 us (0.975)
  starting transfers between devices: 17.5 us -> 14.4 us
    ppermute x4 -> x2, waiting for transfers between devices: 17.4 us -> 1.35 us  [the longest x1 1.35 us: shards(): wave = lax.ppermute(wave, RC, shift_y(1))]
    all_to_all x1, waiting for transfers between devices: 0.01 us -> 14.6 us  [exchange(): return lax.all_to_all(send, RC, 0, 0, axis_index_groups=groups, tiled=True)]
    ppermute x4 -> x2, starting transfers between devices: 6.56 us -> 3.24 us  [the longest x1 3.23 us: shards(): back = lax.ppermute(back, RC, shift_y(3))]
  transfers between devices with their start and end apart: 16 -> 14, of which waited for: 4 -> 4; matrix products, arithmetic and copies ran while one was open for 0% -> 0% of each run, Pallas kernels for 7% -> 7%
where the time goes in v4:
time: 197 us; the launch traced here: 196 us
  blocking collectives  139 us (71%)
  Pallas kernels  19.8 us (10%)
  waiting for transfers between devices  17.3 us (9%)
  starting transfers between devices  14.4 us (7%)
  local copies, waits for them, and re-layouts  2.92 us (1%)
    all_to_all x7, blocking collectives, exchange(): return lax.all_to_all(send, RC, 0, 0, axis_index_groups=groups, tiled=True)  139 us
    all_to_all x1, waiting for transfers between devices, exchange(): return lax.all_to_all(send, RC, 0, 0, axis_index_groups=groups, tiled=True)  14.6 us
    pallas_call x3, Pallas kernels, mirror(): call(mirror_body, out_shape=(jax.ShapeDtypeStruct((1024, 128), jnp.float3...  5.8 us
    all_to_all x1, starting transfers between devices, exchange(): return lax.all_to_all(send, RC, 0, 0, axis_index_groups=groups, tiled=True)  5.3 us
    pallas_call x1, Pallas kernels, assemble(): call(assemble_body, limit=24, out_shape=(half, half, jax.ShapeDtypeStruct...  4.62 us
    pallas_call x3, Pallas kernels, mate(): call(mate_body, out_shape=jax.ShapeDtypeStruct((1024, 128), jnp.float32),...  3.94 us
  transfers between devices with their start and end apart: 14, of which 4 were waited for; matrix products, arithmetic and copies ran while one was open for 0% of the time, Pallas kernels for 7%

profile of v4, /device:TPU:0, one launch (start us, length us, event | category | flops | bytes accessed | tf_op | source)
XLA Modules:
  0.0 196.0 jit_solution(17856881654374613790)
XLA Ops:
  0.7 1.3 slice_bitcast_fusion
  2.0 3.2 %collective-permute-start.1 = (f32[8,128,128]{2,1,0:T(8,128)S(1)}, f32[8,128,128]{2,1,0:T(8,128)S(1)}, u32[]{:S(2)}, u32[]{:S(2)}) collective-permute-start(f32[8,128,128]{2,1,0:T(8,128)S(1)} %get-tuple-element.64.refs_1_), channel_id=1, source_target_pairs={{0,72},{1,73},{2,74},{3,75},{4,76},{5,77},{6,78},{7,79},{8,0},{9,1... | collective-permute-start | bytes 1572872 | tf_op jit(solution)/shard_map/ppermute | solution.py:353
  5.9 19.4 %all_to_all.40.recv.refs_1_ = f32[16,24,128]{2,1,0:T(8,128)S(1)} all-to-all(f32[16,24,128]{2,1,0:T(8,128)S(1)} %pad_maximum_fusion.2), channel_id=1, replica_groups={{0,2,4,6,8,10,12,14,64,66,68,70,72,74,76,78},{1,3,5,7,9,11,13,15,65,67,..., dimensions={0} | all-to-all | bytes 393216 | tf_op jit(solution)/shard_map/all_to_all | solution.py:49
  26.3 1.5 pad_maximum_fusion
  27.8 3.2 %collective-permute-start.3 = (f32[16,128,128]{2,1,0:T(8,128)}, f32[16,128,128]{2,1,0:T(8,128)}, u32[]{:S(2)}, u32[]{:S(2)}) collective-permute-start(f32[16,128,128]{2,1,0:T(8,128)} %get-tuple-element.37), channel_id=1, source_target_pairs={{0,72},{1,73},{2,74},{3,75},{4,76},{5,77},{6,78},{7,79},{8,0},{9,1... | collective-permute-start | bytes 3145736 | tf_op jit(solution)/shard_map/ppermute | solution.py:379
  31.1 5.3 %all-to-all-start.1 = ((f32[16,128,128]{2,1,0:T(8,128)}), f32[16,128,128]{2,1,0:T(8,128)S(1)}, u32[]{:S(2)}, u32[]{:S(2)}) async-start(f32[16,128,128]{2,1,0:T(8,128)} %copy-done), calls=%async_computation.1 | async-start | bytes 2097152 | tf_op jit(solution)/shard_map/all_to_all | solution.py:49
  36.6 14.6 %all-to-all-done.1.refs_6_.recv = f32[16,128,128]{2,1,0:T(8,128)S(1)} async-done(((f32[16,128,128]{2,1,0:T(8,128)}), f32[16,128,128]{2,1,0:T(8,128)S(1)}, u32[]{:S(2)}, u32[]{:S(2)}) %all-to-all-start.1) | async-done | bytes 1048608 | tf_op jit(solution)/shard_map/all_to_all | solution.py:49
  51.2 1.3 collective-permute-done.2.refs_4_
  52.5 4.6 %assemble.1 = (bf16[2048,1024]{1,0:T(8,128)(2,1)S(1)}, bf16[2048,1024]{1,0:T(8,128)(2,1)S(1)}, f32[16,64,128]{2,1,0:T(8,128)S(1)}) custom-call(s32[65]{0:T(128)S(1)} %pad_add_fusion.codes, f32[8,128,128]{2,1,0:T(8,128)S(1)} %get-tuple-element.65.refs_0_, f32[8,128,128]{2,1,0:T(8,128)S(1)} %get-tuple-element.64.refs_1_, ...), custom_call_target="tpu_custom_call" | custom-call | tf_op jit(solution)/shard_map/assemble/pallas_call | solution.py:93
  57.2 1.3 mate.3
  59.1 1.9 mirror.3
  61.3 1.3 own_rows.3.ours
  62.7 23.4 %all_to_all.41.refs_0_ = f32[16,136,128]{2,1,0:T(8,128)S(1)} all-to-all(f32[16,136,128]{2,1,0:T(8,128)S(1)} %join.3), channel_id=1, replica_groups={{0,2,4,6,16,18,20,22,32,34,36,38,48,50,52,54},{1,3,5,7,17,19,21,23,33,3..., dimensions={0} | all-to-all | bytes 2228224 | tf_op jit(solution)/shard_map/all_to_all | solution.py:49
  86.3 19.7 %all_to_all.42.recv = f32[16,128,128]{2,1,0:T(8,128)S(1)} all-to-all(f32[16,128,128]{2,1,0:T(8,128)S(1)} %get-tuple-element.44), channel_id=1, replica_groups={{0,2,4,6,16,18,20,22,32,34,36,38,48,50,52,54},{1,3,5,7,17,19,21,23,33,3..., dimensions={0} | all-to-all | bytes 2097152 | tf_op jit(solution)/shard_map/all_to_all | solution.py:49
  106.0 1.3 mate.4
  108.7 1.9 mirror.4
  110.9 1.3 own_rows.4.ours
  112.3 21.6 %all_to_all.43.refs_0_ = f32[16,136,128]{2,1,0:T(8,128)S(1)} all-to-all(f32[16,136,128]{2,1,0:T(8,128)S(1)} %join.4), channel_id=1, replica_groups={{0,2,4,6,16,18,20,22,32,34,36,38,48,50,52,54},{1,3,5,7,17,19,21,23,33,3..., dimensions={0} | all-to-all | bytes 2228224 | tf_op jit(solution)/shard_map/all_to_all | solution.py:49
  134.1 19.7 %all_to_all.44.recv = f32[16,128,128]{2,1,0:T(8,128)S(1)} all-to-all(f32[16,128,128]{2,1,0:T(8,128)S(1)} %get-tuple-element.53), channel_id=1, replica_groups={{0,2,4,6,16,18,20,22,32,34,36,38,48,50,52,54},{1,3,5,7,17,19,21,23,33,3..., dimensions={0} | all-to-all | bytes 2097152 | tf_op jit(solution)/shard_map/all_to_all | solution.py:49
  153.8 1.3 mate.5
  156.5 1.9 mirror.5
  158.6 1.3 own_rows.5.ours
  160.1 21.6 %all_to_all.45.refs_0_ = f32[16,136,128]{2,1,0:T(8,128)S(1)} all-to-all(f32[16,136,128]{2,1,0:T(8,128)S(1)} %join.5), channel_id=1, replica_groups={{0,2,4,6,16,18,20,22,32,34,36,38,48,50,52,54},{1,3,5,7,17,19,21,23,33,3..., dimensions={0} | all-to-all | bytes 2228224 | tf_op jit(solution)/shard_map/all_to_all | solution.py:49
  181.8 13.5 %all_to_all.46.recv = f32[16,2,16,128]{3,2,1,0:T(8,128)S(1)} all-to-all(f32[16,2,16,128]{3,2,1,0:T(8,128)S(1)} %update.5), channel_id=1, replica_groups={{0,2,4,6,8,10,12,14,64,66,68,70,72,74,76,78},{1,3,5,7,9,11,13,15,65,67,..., dimensions={0} | all-to-all | bytes 524288 | tf_op jit(solution)/shard_map/all_to_all | solution.py:49
  (57 shorter events, 7.3 us)
Async XLA Ops:
  0.6 4.5 %copy-start.3 = (s32[2,1]{0,1:T(1,128)S(1)}, s32[2,1]{0,1:T(1,128)}, u32[]{:S(2)}) copy-start(s32[2,1]{0,1:T(1,128)} %param.7) | copy-start | bytes 28
  0.6 4.9 %copy-start.2 = (s32[2,1,8,2]{2,3,1,0:T(2,128)S(1)}, s32[2,1,8,2]{2,3,1,0:T(2,128)}, u32[]{:S(2)}) copy-start(s32[2,1,8,2]{2,3,1,0:T(2,128)} %param.6) | copy-start | bytes 388
  0.7 5.0 %copy-start.1 = (f32[1,64,512]{2,1,0:T(8,128)S(1)}, f32[1,64,512]{2,1,0:T(8,128)}, u32[]{:S(2)}) copy-start(f32[1,64,512]{2,1,0:T(8,128)} %param.4) | copy-start | bytes 393220
  2.0 24.3 %collective-permute-start.1 = (f32[8,128,128]{2,1,0:T(8,128)S(1)}, f32[8,128,128]{2,1,0:T(8,128)S(1)}, u32[]{:S(2)}, u32[]{:S(2)}) collective-permute-start(f32[8,128,128]{2,1,0:T(8,128)S(1)} %get-tuple-element.64.refs_1_), channel_id=1, source_target_pairs={{0,72},{1,73},{2,74},{3,75},{4,76},{5,77},{6,78},{7,79},{8,0},{9,1... | collective-permute-start | bytes 1572872 | tf_op jit(solution)/shard_map/ppermute | solution.py:353
  5.2 21.1 %collective-permute-start = (f32[8,128,128]{2,1,0:T(8,128)S(1)}, f32[8,128,128]{2,1,0:T(8,128)S(1)}, u32[]{:S(2)}, u32[]{:S(2)}) collective-permute-start(f32[8,128,128]{2,1,0:T(8,128)S(1)} %get-tuple-element.65.refs_0_), channel_id=1, source_target_pairs={{0,8},{1,9},{2,10},{3,11},{4,12},{5,13},{6,14},{7,15},{8,64},{9,65... | collective-permute-start | bytes 1572872 | tf_op jit(solution)/shard_map/ppermute | solution.py:352
  25.3 1.0 copy-start
  27.8 24.7 %collective-permute-start.2 = (f32[16,128,128]{2,1,0:T(8,128)}, f32[16,128,128]{2,1,0:T(8,128)}, u32[]{:S(2)}, u32[]{:S(2)}) collective-permute-start(f32[16,128,128]{2,1,0:T(8,128)} %get-tuple-element.36), channel_id=1, source_target_pairs={{0,8},{1,9},{2,10},{3,11},{4,12},{5,13},{6,14},{7,15},{8,64},{9,65... | collective-permute-start | bytes 3145736 | tf_op jit(solution)/shard_map/ppermute | solution.py:378
  27.8 24.7 %collective-permute-start.3 = (f32[16,128,128]{2,1,0:T(8,128)}, f32[16,128,128]{2,1,0:T(8,128)}, u32[]{:S(2)}, u32[]{:S(2)}) collective-permute-start(f32[16,128,128]{2,1,0:T(8,128)} %get-tuple-element.37), channel_id=1, source_target_pairs={{0,72},{1,73},{2,74},{3,75},{4,76},{5,77},{6,78},{7,79},{8,0},{9,1... | collective-permute-start | bytes 3145736 | tf_op jit(solution)/shard_map/ppermute | solution.py:379
  31.1 20.1 %all-to-all-start.1 = ((f32[16,128,128]{2,1,0:T(8,128)}), f32[16,128,128]{2,1,0:T(8,128)S(1)}, u32[]{:S(2)}, u32[]{:S(2)}) async-start(f32[16,128,128]{2,1,0:T(8,128)} %copy-done), calls=%async_computation.1 | async-start | bytes 2097152 | tf_op jit(solution)/shard_map/all_to_all | solution.py:49
  57.1 2.0 %collective-permute-start.4 = (f32[16,64,128]{2,1,0:T(8,128)S(1)}, f32[16,64,128]{2,1,0:T(8,128)S(1)}, u32[]{:S(2)}, u32[]{:S(2)}) collective-permute-start(f32[16,64,128]{2,1,0:T(8,128)S(1)} %get-tuple-element.40), channel_id=1, source_target_pairs={{0,1},{1,0},{2,3},{3,2},{4,5},{5,4},{6,7},{7,6},{8,9},{9,8},{10,11... | collective-permute-start | bytes 1572872 | tf_op jit(solution)/shard_map/ppermute | solution.py:219
  58.6 4.0 %collective-permute-start.5 = (f32[1024,128]{1,0:T(8,128)S(1)}, f32[1024,128]{1,0:T(8,128)S(1)}, u32[]{:S(2)}, u32[]{:S(2)}) collective-permute-start(f32[1024,128]{1,0:T(8,128)S(1)} %mate.3), channel_id=1, source_target_pairs={{0,1},{1,0},{2,3},{3,2},{4,5},{5,4},{6,7},{7,6},{8,9},{9,8},{10,11... | collective-permute-start | bytes 1572872 | tf_op jit(solution)/shard_map/ppermute | solution.py:220
  61.1 1.5 collective-permute-start.6
  106.0 2.7 %collective-permute-start.7 = (f32[16,128,128]{2,1,0:T(8,128)S(1)}, f32[16,128,128]{2,1,0:T(8,128)S(1)}, u32[]{:S(2)}, u32[]{:S(2)}) collective-permute-start(f32[16,128,128]{2,1,0:T(8,128)S(1)} %all_to_all.42.recv), channel_id=1, source_target_pairs={{0,1},{1,0},{2,3},{3,2},{4,5},{5,4},{6,7},{7,6},{8,9},{9,8},{10,11... | collective-permute-start | bytes 3145736 | tf_op jit(solution)/shard_map/ppermute | solution.py:219
  107.4 4.8 %collective-permute-start.8 = (f32[1024,128]{1,0:T(8,128)S(1)}, f32[1024,128]{1,0:T(8,128)S(1)}, u32[]{:S(2)}, u32[]{:S(2)}) collective-permute-start(f32[1024,128]{1,0:T(8,128)S(1)} %mate.4), channel_id=1, source_target_pairs={{0,1},{1,0},{2,3},{3,2},{4,5},{5,4},{6,7},{7,6},{8,9},{9,8},{10,11... | collective-permute-start | bytes 1572872 | tf_op jit(solution)/shard_map/ppermute | solution.py:220
  110.6 1.5 collective-permute-start.9
  153.8 2.7 %collective-permute-start.10 = (f32[16,128,128]{2,1,0:T(8,128)S(1)}, f32[16,128,128]{2,1,0:T(8,128)S(1)}, u32[]{:S(2)}, u32[]{:S(2)}) collective-permute-start(f32[16,128,128]{2,1,0:T(8,128)S(1)} %all_to_all.44.recv), channel_id=1, source_target_pairs={{0,1},{1,0},{2,3},{3,2},{4,5},{5,4},{6,7},{7,6},{8,9},{9,8},{10,11... | collective-permute-start | bytes 3145736 | tf_op jit(solution)/shard_map/ppermute | solution.py:219
  155.2 4.8 %collective-permute-start.11 = (f32[1024,128]{1,0:T(8,128)S(1)}, f32[1024,128]{1,0:T(8,128)S(1)}, u32[]{:S(2)}, u32[]{:S(2)}) collective-permute-start(f32[1024,128]{1,0:T(8,128)S(1)} %mate.5), channel_id=1, source_target_pairs={{0,1},{1,0},{2,3},{3,2},{4,5},{5,4},{6,7},{7,6},{8,9},{9,8},{10,11... | collective-permute-start | bytes 1572872 | tf_op jit(solution)/shard_map/ppermute | solution.py:220
  158.4 1.5 collective-permute-start.12

commit v5 on v4

--- a/solution.py
+++ b/solution.py
@@ -56,15 +56,25 @@
 
 
 def assemble_body(codes, *refs):
-    own0, own1, left0, right1, wave, back, recv, hi, lo, share, dense = refs
+    own0, own1, left0, right1, wave_in, back_in, recv, hi, lo, share, dense, wave, back, sems = refs
+    copies = (
+        pltpu.make_async_copy(wave_in, wave, sems.at[0]),
+        pltpu.make_async_copy(back_in, back, sems.at[1]),
+    )
+    for copy in copies:
+        copy.start()
     pieces = (
-        (own0, 0), (own1, 0), (left0, 0), (wave, 8), (wave, 0), (back, 0), (back, 8), (right1, 0)
+        (own0, 0, 0, 0), (own1, 0, 0, 1), (left0, 0, 1, 0), (right1, 0, 3, 1),
+        (wave, 8, 1, 1), (wave, 0, 2, 0), (back, 0, 2, 1), (back, 8, 3, 0),
     )
     share[...] = recv[:, :64, :]
     dense[...] = jnp.zeros_like(dense)
     y = codes[64]
-    for i, (ref, first) in enumerate(pieces):
-        base = ((y - i // 2) & 3) * 16 + (i % 2) * 8
+    for i, (ref, first, d, h) in enumerate(pieces):
+        base = ((y - d) & 3) * 16 + h * 8
+        if i == 4:
+            for copy in copies:
+                copy.wait()
         for b in range(8):
             code = codes[base + b]
 
@@ -86,6 +96,7 @@
 
 
 VMEM = pl.BlockSpec(memory_space=pltpu.VMEM)
+HBM = pl.BlockSpec(memory_space=pltpu.HBM)
 
 
 def assemble(codes, pieces, recv):
@@ -94,9 +105,11 @@
         assemble_body,
         limit=24,
         out_shape=(half, half, jax.ShapeDtypeStruct((16, 64, 128), jnp.float32)),
-        in_specs=[pl.BlockSpec(memory_space=pltpu.SMEM)] + [VMEM] * 7,
+        in_specs=[pl.BlockSpec(memory_space=pltpu.SMEM)] + [VMEM] * 4 + [HBM] * 2 + [VMEM],
         out_specs=(VMEM,) * 3,
-        scratch_shapes=[pltpu.VMEM((2048, 1024), jnp.float32)],
+        scratch_shapes=[pltpu.VMEM((2048, 1024), jnp.float32)]
+        + [pltpu.VMEM((16, 128, 128), jnp.float32)] * 2
+        + [pltpu.SemaphoreType.DMA((2,))],
         name="assemble",
     )(codes, *pieces, recv)
 
@@ -245,24 +258,40 @@
     return out
 
 
-def start_body(recv, send, sums):
+def start_body(recv, left0, own1, right1, own0, send, sums, wave, back, work, sems):
+    pieces = ((left0, wave, 0), (own1, wave, 8), (right1, back, 0), (own0, back, 8))
+    copies = [
+        pltpu.make_async_copy(src, dst.at[pl.ds(first, 8)], sems.at[i])
+        for i, (src, dst, first) in enumerate(pieces)
+    ]
+    for copy in copies:
+        copy.start()
+    spread(lambda s, g: recv[s * 4 + g, :16], work)
+    copies.append(pltpu.make_async_copy(work, send, sems.at[4]))
+    copies[-1].start()
     square = jnp.zeros((16, 128), jnp.float32)
     for i in range(16):
         piece = recv[i, :16]
         square = square + piece * piece
-    spread(lambda s, g: recv[s * 4 + g, :16], send)
     sums[...] = rows_of(row_sum(square))
-
-
-def start(recv):
+    for copy in copies:
+        copy.wait()
+
+
+def start(*operands):
+    big = jax.ShapeDtypeStruct((16, 128, 128), jnp.float32)
+    small = jax.ShapeDtypeStruct((8, 128), jnp.float32)
     return call(
         start_body,
-        out_shape=(
-            jax.ShapeDtypeStruct((16, 128, 128), jnp.float32),
-            jax.ShapeDtypeStruct((8, 128), jnp.float32),
-        ),
+        out_shape=(big, small, big, big),
+        in_specs=[VMEM] * 5,
+        out_specs=(HBM, VMEM, HBM, HBM),
+        scratch_shapes=[
+            pltpu.VMEM((16, 128, 128), jnp.float32),
+            pltpu.SemaphoreType.DMA((5,)),
+        ],
         name="start",
-    )(recv)
+    )(*operands)
 
 
 def update_body(step, *refs):
@@ -369,12 +398,8 @@
         [codes.reshape(64).astype(jnp.int32), (yh * 2 + yl)[None].astype(jnp.int32)]
     )
 
-    send, sums = start(recv)
+    send, sums, wave, back = start(recv, left0, own1, right1, own0)
     state = (recv,)
-    send, left0, right1 = lax.optimization_barrier((send, left0, right1))
-    wave, back, recv = lax.optimization_barrier(
-        (jnp.concatenate([left0, own1]), jnp.concatenate([right1, own0]), recv)
-    )
     wave = lax.ppermute(wave, RC, shift_y(1))
     back = lax.ppermute(back, RC, shift_y(3))
     got = exchange(send, PLANES)

time: 197 us -> 196 us (level)
  no operation moved by 1% of the time
where the time goes in v5:
time: 196 us; the launch traced here: 195 us
  blocking collectives  139 us (71%)
  Pallas kernels  20.5 us (10%)
  waiting for transfers between devices  17.3 us (9%)
  starting transfers between devices  14.4 us (7%)
  local copies, waits for them, and re-layouts  2.91 us (1%)
    all_to_all x7, blocking collectives, exchange(): return lax.all_to_all(send, RC, 0, 0, axis_index_groups=groups, tiled=True)  139 us
    all_to_all x1, waiting for transfers between devices, exchange(): return lax.all_to_all(send, RC, 0, 0, axis_index_groups=groups, tiled=True)  14.6 us
    pallas_call x3, Pallas kernels, mirror(): call(mirror_body, out_shape=(jax.ShapeDtypeStruct((1024, 128), jnp.float3...  5.8 us
    all_to_all x1, starting transfers between devices, exchange(): return lax.all_to_all(send, RC, 0, 0, axis_index_groups=groups, tiled=True)  5.3 us
    pallas_call x1, Pallas kernels, assemble(): call(assemble_body, limit=24, out_shape=(half, half, jax.ShapeDtypeStruct...  4.06 us
    pallas_call x3, Pallas kernels, mate(): call(mate_body, out_shape=jax.ShapeDtypeStruct((1024, 128), jnp.float32),...  3.94 us
    pallas_call x3, Pallas kernels, own_rows(): call(own_body, out_shape=jax.ShapeDtypeStruct((1024, 128), jnp.float32),...  3.94 us
  transfers between devices with their start and end apart: 14, of which 4 were waited for; matrix products, arithmetic and copies ran while one was open for 0% of the time, Pallas kernels for 7%

profile of v5, /device:TPU:0, one launch (start us, length us, event | category | flops | bytes accessed | tf_op | source)
XLA Modules:
  0.0 195.2 jit_solution(9644410409746414404)
XLA Ops:
  0.7 1.3 slice_bitcast_fusion
  2.0 3.2 %collective-permute-start.1 = (f32[8,128,128]{2,1,0:T(8,128)S(1)}, f32[8,128,128]{2,1,0:T(8,128)S(1)}, u32[]{:S(2)}, u32[]{:S(2)}) collective-permute-start(f32[8,128,128]{2,1,0:T(8,128)S(1)} %get-tuple-element.58.own1.refs_1_), channel_id=1, source_target_pairs={{0,72},{1,73},{2,74},{3,75},{4,76},{5,77},{6,78},{7,79},{8,0},{9,1... | collective-permute-start | bytes 1572872 | tf_op jit(solution)/shard_map/ppermute | solution.py:382
  5.9 19.4 %all_to_all.40.recv.refs_1_ = f32[16,24,128]{2,1,0:T(8,128)S(1)} all-to-all(f32[16,24,128]{2,1,0:T(8,128)S(1)} %pad_maximum_fusion), channel_id=1, replica_groups={{0,2,4,6,8,10,12,14,64,66,68,70,72,74,76,78},{1,3,5,7,9,11,13,15,65,67,..., dimensions={0} | all-to-all | bytes 393216 | tf_op jit(solution)/shard_map/all_to_all | solution.py:49
  25.2 1.4 start.1
  27.6 3.2 %collective-permute-start.3 = (f32[16,128,128]{2,1,0:T(8,128)}, f32[16,128,128]{2,1,0:T(8,128)}, u32[]{:S(2)}, u32[]{:S(2)}) collective-permute-start(f32[16,128,128]{2,1,0:T(8,128)} %get-tuple-element.31), channel_id=1, source_target_pairs={{0,72},{1,73},{2,74},{3,75},{4,76},{5,77},{6,78},{7,79},{8,0},{9,1... | collective-permute-start | bytes 3145736 | tf_op jit(solution)/shard_map/ppermute | solution.py:404
  30.8 5.3 %all-to-all-start.1 = ((f32[16,128,128]{2,1,0:T(8,128)}), f32[16,128,128]{2,1,0:T(8,128)S(1)}, u32[]{:S(2)}, u32[]{:S(2)}) async-start(f32[16,128,128]{2,1,0:T(8,128)} %copy-done), calls=%async_computation.1 | async-start | bytes 2097152 | tf_op jit(solution)/shard_map/all_to_all | solution.py:49
  36.4 14.6 %all-to-all-done.1.refs_6_.recv = f32[16,128,128]{2,1,0:T(8,128)S(1)} async-done(((f32[16,128,128]{2,1,0:T(8,128)}), f32[16,128,128]{2,1,0:T(8,128)S(1)}, u32[]{:S(2)}, u32[]{:S(2)}) %all-to-all-start.1) | async-done | bytes 1048608 | tf_op jit(solution)/shard_map/all_to_all | solution.py:49
  50.9 1.3 collective-permute-done.2.refs_4_
  52.3 4.1 %assemble.1 = (bf16[2048,1024]{1,0:T(8,128)(2,1)S(1)}, bf16[2048,1024]{1,0:T(8,128)(2,1)S(1)}, f32[16,64,128]{2,1,0:T(8,128)S(1)}) custom-call(s32[65]{0:T(128)S(1)} %pad_add_fusion.codes, f32[8,128,128]{2,1,0:T(8,128)S(1)} %get-tuple-element.59.own0.refs_0_, f32[8,128,128]{2,1,0:T(8,128)S(1)} %get-tuple-element.58.own1.refs_1_, ...), custom_call_target="tpu_custom_call" | custom-call | tf_op jit(solution)/shard_map/assemble/pallas_call | solution.py:104
  56.4 1.3 mate.3
  58.3 1.9 mirror.3
  60.5 1.3 own_rows.3.ours
  61.9 23.4 %all_to_all.41.refs_0_ = f32[16,136,128]{2,1,0:T(8,128)S(1)} all-to-all(f32[16,136,128]{2,1,0:T(8,128)S(1)} %join.3), channel_id=1, replica_groups={{0,2,4,6,16,18,20,22,32,34,36,38,48,50,52,54},{1,3,5,7,17,19,21,23,33,3..., dimensions={0} | all-to-all | bytes 2228224 | tf_op jit(solution)/shard_map/all_to_all | solution.py:49
  85.5 19.7 %all_to_all.42.recv = f32[16,128,128]{2,1,0:T(8,128)S(1)} all-to-all(f32[16,128,128]{2,1,0:T(8,128)S(1)} %get-tuple-element.38), channel_id=1, replica_groups={{0,2,4,6,16,18,20,22,32,34,36,38,48,50,52,54},{1,3,5,7,17,19,21,23,33,3..., dimensions={0} | all-to-all | bytes 2097152 | tf_op jit(solution)/shard_map/all_to_all | solution.py:49
  105.2 1.3 mate.4
  107.9 1.9 mirror.4
  110.0 1.3 own_rows.4.ours
  111.5 21.6 %all_to_all.43.refs_0_ = f32[16,136,128]{2,1,0:T(8,128)S(1)} all-to-all(f32[16,136,128]{2,1,0:T(8,128)S(1)} %join.4), channel_id=1, replica_groups={{0,2,4,6,16,18,20,22,32,34,36,38,48,50,52,54},{1,3,5,7,17,19,21,23,33,3..., dimensions={0} | all-to-all | bytes 2228224 | tf_op jit(solution)/shard_map/all_to_all | solution.py:49
  133.3 19.7 %all_to_all.44.recv = f32[16,128,128]{2,1,0:T(8,128)S(1)} all-to-all(f32[16,128,128]{2,1,0:T(8,128)S(1)} %get-tuple-element.47), channel_id=1, replica_groups={{0,2,4,6,16,18,20,22,32,34,36,38,48,50,52,54},{1,3,5,7,17,19,21,23,33,3..., dimensions={0} | all-to-all | bytes 2097152 | tf_op jit(solution)/shard_map/all_to_all | solution.py:49
  153.0 1.3 mate.5
  155.7 1.9 mirror.5
  157.8 1.3 own_rows.5.ours
  159.3 21.6 %all_to_all.45.refs_0_ = f32[16,136,128]{2,1,0:T(8,128)S(1)} all-to-all(f32[16,136,128]{2,1,0:T(8,128)S(1)} %join.5), channel_id=1, replica_groups={{0,2,4,6,16,18,20,22,32,34,36,38,48,50,52,54},{1,3,5,7,17,19,21,23,33,3..., dimensions={0} | all-to-all | bytes 2228224 | tf_op jit(solution)/shard_map/all_to_all | solution.py:49
  181.0 13.5 %all_to_all.46.recv = f32[16,2,16,128]{3,2,1,0:T(8,128)S(1)} all-to-all(f32[16,2,16,128]{3,2,1,0:T(8,128)S(1)} %update.5), channel_id=1, replica_groups={{0,2,4,6,8,10,12,14,64,66,68,70,72,74,76,78},{1,3,5,7,9,11,13,15,65,67,..., dimensions={0} | all-to-all | bytes 524288 | tf_op jit(solution)/shard_map/all_to_all | solution.py:49
  (56 shorter events, 7.2 us)
Async XLA Ops:
  0.6 4.5 %copy-start.3 = (s32[2,1]{0,1:T(1,128)S(1)}, s32[2,1]{0,1:T(1,128)}, u32[]{:S(2)}) copy-start(s32[2,1]{0,1:T(1,128)} %param.7) | copy-start | bytes 28
  0.6 4.9 %copy-start.2 = (s32[2,1,8,2]{2,3,1,0:T(2,128)S(1)}, s32[2,1,8,2]{2,3,1,0:T(2,128)}, u32[]{:S(2)}) copy-start(s32[2,1,8,2]{2,3,1,0:T(2,128)} %param.6) | copy-start | bytes 388
  0.7 5.0 %copy-start.1 = (f32[1,64,512]{2,1,0:T(8,128)S(1)}, f32[1,64,512]{2,1,0:T(8,128)}, u32[]{:S(2)}) copy-start(f32[1,64,512]{2,1,0:T(8,128)} %param.4) | copy-start | bytes 393220
  2.0 23.2 %collective-permute-start.1 = (f32[8,128,128]{2,1,0:T(8,128)S(1)}, f32[8,128,128]{2,1,0:T(8,128)S(1)}, u32[]{:S(2)}, u32[]{:S(2)}) collective-permute-start(f32[8,128,128]{2,1,0:T(8,128)S(1)} %get-tuple-element.58.own1.refs_1_), channel_id=1, source_target_pairs={{0,72},{1,73},{2,74},{3,75},{4,76},{5,77},{6,78},{7,79},{8,0},{9,1... | collective-permute-start | bytes 1572872 | tf_op jit(solution)/shard_map/ppermute | solution.py:382
  5.2 20.0 %collective-permute-start = (f32[8,128,128]{2,1,0:T(8,128)S(1)}, f32[8,128,128]{2,1,0:T(8,128)S(1)}, u32[]{:S(2)}, u32[]{:S(2)}) collective-permute-start(f32[8,128,128]{2,1,0:T(8,128)S(1)} %get-tuple-element.59.own0.refs_0_), channel_id=1, source_target_pairs={{0,8},{1,9},{2,10},{3,11},{4,12},{5,13},{6,14},{7,15},{8,64},{9,65... | collective-permute-start | bytes 1572872 | tf_op jit(solution)/shard_map/ppermute | solution.py:381
  26.6 1.0 copy-start
  27.6 24.7 %collective-permute-start.2 = (f32[16,128,128]{2,1,0:T(8,128)}, f32[16,128,128]{2,1,0:T(8,128)}, u32[]{:S(2)}, u32[]{:S(2)}) collective-permute-start(f32[16,128,128]{2,1,0:T(8,128)} %get-tuple-element.30), channel_id=1, source_target_pairs={{0,8},{1,9},{2,10},{3,11},{4,12},{5,13},{6,14},{7,15},{8,64},{9,65... | collective-permute-start | bytes 3145736 | tf_op jit(solution)/shard_map/ppermute | solution.py:403
  27.6 24.7 %collective-permute-start.3 = (f32[16,128,128]{2,1,0:T(8,128)}, f32[16,128,128]{2,1,0:T(8,128)}, u32[]{:S(2)}, u32[]{:S(2)}) collective-permute-start(f32[16,128,128]{2,1,0:T(8,128)} %get-tuple-element.31), channel_id=1, source_target_pairs={{0,72},{1,73},{2,74},{3,75},{4,76},{5,77},{6,78},{7,79},{8,0},{9,1... | collective-permute-start | bytes 3145736 | tf_op jit(solution)/shard_map/ppermute | solution.py:404
  30.8 20.1 %all-to-all-start.1 = ((f32[16,128,128]{2,1,0:T(8,128)}), f32[16,128,128]{2,1,0:T(8,128)S(1)}, u32[]{:S(2)}, u32[]{:S(2)}) async-start(f32[16,128,128]{2,1,0:T(8,128)} %copy-done), calls=%async_computation.1 | async-start | bytes 2097152 | tf_op jit(solution)/shard_map/all_to_all | solution.py:49
  56.3 2.0 %collective-permute-start.4 = (f32[16,64,128]{2,1,0:T(8,128)S(1)}, f32[16,64,128]{2,1,0:T(8,128)S(1)}, u32[]{:S(2)}, u32[]{:S(2)}) collective-permute-start(f32[16,64,128]{2,1,0:T(8,128)S(1)} %get-tuple-element.34), channel_id=1, source_target_pairs={{0,1},{1,0},{2,3},{3,2},{4,5},{5,4},{6,7},{7,6},{8,9},{9,8},{10,11... | collective-permute-start | bytes 1572872 | tf_op jit(solution)/shard_map/ppermute | solution.py:232
  57.7 4.0 %collective-permute-start.5 = (f32[1024,128]{1,0:T(8,128)S(1)}, f32[1024,128]{1,0:T(8,128)S(1)}, u32[]{:S(2)}, u32[]{:S(2)}) collective-permute-start(f32[1024,128]{1,0:T(8,128)S(1)} %mate.3), channel_id=1, source_target_pairs={{0,1},{1,0},{2,3},{3,2},{4,5},{5,4},{6,7},{7,6},{8,9},{9,8},{10,11... | collective-permute-start | bytes 1572872 | tf_op jit(solution)/shard_map/ppermute | solution.py:233
  60.3 1.5 collective-permute-start.6
  105.2 2.7 %collective-permute-start.7 = (f32[16,128,128]{2,1,0:T(8,128)S(1)}, f32[16,128,128]{2,1,0:T(8,128)S(1)}, u32[]{:S(2)}, u32[]{:S(2)}) collective-permute-start(f32[16,128,128]{2,1,0:T(8,128)S(1)} %all_to_all.42.recv), channel_id=1, source_target_pairs={{0,1},{1,0},{2,3},{3,2},{4,5},{5,4},{6,7},{7,6},{8,9},{9,8},{10,11... | collective-permute-start | bytes 3145736 | tf_op jit(solution)/shard_map/ppermute | solution.py:232
  106.6 4.8 %collective-permute-start.8 = (f32[1024,128]{1,0:T(8,128)S(1)}, f32[1024,128]{1,0:T(8,128)S(1)}, u32[]{:S(2)}, u32[]{:S(2)}) collective-permute-start(f32[1024,128]{1,0:T(8,128)S(1)} %mate.4), channel_id=1, source_target_pairs={{0,1},{1,0},{2,3},{3,2},{4,5},{5,4},{6,7},{7,6},{8,9},{9,8},{10,11... | collective-permute-start | bytes 1572872 | tf_op jit(solution)/shard_map/ppermute | solution.py:233
  109.8 1.5 collective-permute-start.9
  153.0 2.7 %collective-permute-start.10 = (f32[16,128,128]{2,1,0:T(8,128)S(1)}, f32[16,128,128]{2,1,0:T(8,128)S(1)}, u32[]{:S(2)}, u32[]{:S(2)}) collective-permute-start(f32[16,128,128]{2,1,0:T(8,128)S(1)} %all_to_all.44.recv), channel_id=1, source_target_pairs={{0,1},{1,0},{2,3},{3,2},{4,5},{5,4},{6,7},{7,6},{8,9},{9,8},{10,11... | collective-permute-start | bytes 3145736 | tf_op jit(solution)/shard_map/ppermute | solution.py:232
  154.3 4.8 %collective-permute-start.11 = (f32[1024,128]{1,0:T(8,128)S(1)}, f32[1024,128]{1,0:T(8,128)S(1)}, u32[]{:S(2)}, u32[]{:S(2)}) collective-permute-start(f32[1024,128]{1,0:T(8,128)S(1)} %mate.5), channel_id=1, source_target_pairs={{0,1},{1,0},{2,3},{3,2},{4,5},{5,4},{6,7},{7,6},{8,9},{9,8},{10,11... | collective-permute-start | bytes 1572872 | tf_op jit(solution)/shard_map/ppermute | solution.py:233
  157.6 1.5 collective-permute-start.12

commit v6 on v5

--- a/solution.py
+++ b/solution.py
@@ -55,63 +55,95 @@
     )
 
 
-def assemble_body(codes, *refs):
-    own0, own1, left0, right1, wave_in, back_in, recv, hi, lo, share, dense, wave, back, sems = refs
+EARLY = ((0, 0), (0, 1), (1, 0), (3, 1))
+LATE = ((2, 0), (1, 1), (2, 1), (3, 0))
+
+
+def corners(codes, back, half):
+    y = (codes[64] - back) & 3
+    row = (half ^ codes[65]) * 1024 + (y >> 1) * 256
+    col = (y & 1) * 256
+    for j in range(2):
+        for i in range(2):
+            at = pl.ds(pl.multiple_of(row + j * 512, 256), 256)
+            by = pl.ds(pl.multiple_of(col + i * 512, 256), 256)
+            yield j, i, at, by
+
+
+def fill(codes, ref, first, back, half, hi, lo, work):
+    work[...] = jnp.zeros_like(work)
+    base = ((codes[64] - back) & 3) * 16 + half * 8
+    for b in range(8):
+        code = codes[base + b]
+
+        @pl.when(code >= 0)
+        def _(b=b, code=code):
+            row, col = code >> 3, code & 7
+            ro = pl.multiple_of((((row >> 2) & 1) * 2 + (row & 1)) * 128, 128)
+            co = pl.multiple_of(((col >> 2) * 2 + (col & 1)) * 128, 128)
+            work[pl.ds(ro, 128), pl.ds(co, 128)] += ref[first + b]
+
+    for j, i, at, by in corners(codes, back, half):
+        top, rest = parted(work[j * 256 : (j + 1) * 256, i * 256 : (i + 1) * 256])
+        hi[at, by] = top
+        lo[at, by] = rest
+
+
+def early_body(codes, own0, own1, left0, right1, recv, hi, lo, share, work):
+    share[...] = recv[:, :64, :]
+    for ref, place in zip((own0, own1, left0, right1), EARLY):
+        fill(codes, ref, 0, *place, hi, lo, work)
+
+
+def late_body(codes, wave_in, back_in, hi0, lo0, hi, lo, work, wave, back, sems):
     copies = (
         pltpu.make_async_copy(wave_in, wave, sems.at[0]),
         pltpu.make_async_copy(back_in, back, sems.at[1]),
     )
     for copy in copies:
         copy.start()
-    pieces = (
-        (own0, 0, 0, 0), (own1, 0, 0, 1), (left0, 0, 1, 0), (right1, 0, 3, 1),
-        (wave, 8, 1, 1), (wave, 0, 2, 0), (back, 0, 2, 1), (back, 8, 3, 0),
-    )
-    share[...] = recv[:, :64, :]
-    dense[...] = jnp.zeros_like(dense)
-    y = codes[64]
-    for i, (ref, first, d, h) in enumerate(pieces):
-        base = ((y - d) & 3) * 16 + h * 8
-        if i == 4:
-            for copy in copies:
-                copy.wait()
-        for b in range(8):
-            code = codes[base + b]
-
-            @pl.when(code >= 0)
-            def _(ref=ref, b=first + b, code=code):
-                ro = pl.multiple_of((code >> 3) * 128, 128)
-                co = pl.multiple_of((code & 7) * 128, 128)
-                dense[pl.ds(ro, 128), pl.ds(co, 128)] += ref[b]
-
-    def narrow(i, carry):
-        rows = pl.ds(pl.multiple_of(i * 128, 128), 128)
-        value = dense[rows, :]
-        top = value.astype(jnp.bfloat16)
-        hi[rows, :] = top
-        lo[rows, :] = (value - top.astype(jnp.float32)).astype(jnp.bfloat16)
-        return carry
-
-    lax.fori_loop(0, 16, narrow, 0)
+    for place in EARLY:
+        for _, _, at, by in corners(codes, *place):
+            hi[at, by] = hi0[at, by]
+            lo[at, by] = lo0[at, by]
+    copies[0].wait()
+    fill(codes, wave, 0, *LATE[0], hi, lo, work)
+    fill(codes, wave, 8, *LATE[1], hi, lo, work)
+    copies[1].wait()
+    fill(codes, back, 0, *LATE[2], hi, lo, work)
+    fill(codes, back, 8, *LATE[3], hi, lo, work)
 
 
 VMEM = pl.BlockSpec(memory_space=pltpu.VMEM)
 HBM = pl.BlockSpec(memory_space=pltpu.HBM)
 
 
-def assemble(codes, pieces, recv):
-    half = jax.ShapeDtypeStruct((2048, 1024), jnp.bfloat16)
-    return call(
-        assemble_body,
-        limit=24,
-        out_shape=(half, half, jax.ShapeDtypeStruct((16, 64, 128), jnp.float32)),
-        in_specs=[pl.BlockSpec(memory_space=pltpu.SMEM)] + [VMEM] * 4 + [HBM] * 2 + [VMEM],
+SMEM = pl.BlockSpec(memory_space=pltpu.SMEM)
+HALF = jax.ShapeDtypeStruct((2048, 1024), jnp.bfloat16)
+
+
+def early(codes, *operands):
+    return call(
+        early_body,
+        out_shape=(HALF, HALF, jax.ShapeDtypeStruct((16, 64, 128), jnp.float32)),
+        in_specs=[SMEM] + [VMEM] * 5,
         out_specs=(VMEM,) * 3,
-        scratch_shapes=[pltpu.VMEM((2048, 1024), jnp.float32)]
+        scratch_shapes=[pltpu.VMEM((512, 512), jnp.float32)],
+        name="early",
+    )(codes, *operands)
+
+
+def late(codes, *operands):
+    return call(
+        late_body,
+        out_shape=(HALF, HALF),
+        in_specs=[SMEM, HBM, HBM, VMEM, VMEM],
+        out_specs=(VMEM,) * 2,
+        scratch_shapes=[pltpu.VMEM((512, 512), jnp.float32)]
         + [pltpu.VMEM((16, 128, 128), jnp.float32)] * 2
         + [pltpu.SemaphoreType.DMA((2,))],
-        name="assemble",
-    )(codes, *pieces, recv)
+        name="late",
+    )(codes, *operands)
 
 
 def parted(value):
@@ -395,7 +427,7 @@
     recv = exchange(send, SHEETS)
     codes = lax.dynamic_slice(recv.reshape(4, 4, 24, 128), (0, z, 16, 0), (4, 1, 1, 16))
     codes = jnp.concatenate(
-        [codes.reshape(64).astype(jnp.int32), (yh * 2 + yl)[None].astype(jnp.int32)]
+        [codes.reshape(64).astype(jnp.int32), jnp.stack([yh * 2 + yl, k]).astype(jnp.int32)]
     )
 
     send, sums, wave, back = start(recv, left0, own1, right1, own0)
@@ -403,8 +435,8 @@
     wave = lax.ppermute(wave, RC, shift_y(1))
     back = lax.ppermute(back, RC, shift_y(3))
     got = exchange(send, PLANES)
-    pieces = (own0, own1, left0, right1, wave, back)
-    hi, lo, share = assemble(codes, pieces, got)
+    hi, lo, share = early(codes, own0, own1, left0, right1, got)
+    hi, lo = late(codes, wave, back, hi, lo)
     for step in range(ITERS):
         if step:
             got = share = exchange(send, PLANES)

time: 196 us -> 194 us (0.990)
  blocking collectives: 139 us -> 137 us
    pallas_call x1 -> x2, Pallas kernels: 4.06 us -> 5.71 us  [the longest x1 3.51 us: late(): call(late_body, out_shape=(HALF, HALF), in_specs=[SMEM, HBM, HBM, VMEM, V...]
  transfers between devices with their start and end apart: 14 -> 14, of which waited for: 4 -> 3; matrix products, arithmetic and copies ran while one was open for 0% -> 0% of each run, Pallas kernels for 7% -> 10%
where the time goes in v6:
time: 194 us
  blocking collectives  137 us (71%)
  Pallas kernels  22.2 us (11%)
  waiting for transfers between devices  16.1 us (8%)
  starting transfers between devices  14.1 us (7%)
  local copies, waits for them, and re-layouts  2.91 us (2%)
    all_to_all x7, blocking collectives, exchange(): return lax.all_to_all(send, RC, 0, 0, axis_index_groups=groups, tiled=True)  137 us
    all_to_all x1, waiting for transfers between devices, exchange(): return lax.all_to_all(send, RC, 0, 0, axis_index_groups=groups, tiled=True)  14.6 us
    pallas_call x3, Pallas kernels, mirror(): call(mirror_body, out_shape=(jax.ShapeDtypeStruct((1024, 128), jnp.float3...  5.81 us
    all_to_all x1, starting transfers between devices, exchange(): return lax.all_to_all(send, RC, 0, 0, axis_index_groups=groups, tiled=True)  5.3 us
    pallas_call x3, Pallas kernels, mate(): call(mate_body, out_shape=jax.ShapeDtypeStruct((1024, 128), jnp.float32),...  3.94 us
    pallas_call x3, Pallas kernels, own_rows(): call(own_body, out_shape=jax.ShapeDtypeStruct((1024, 128), jnp.float32),...  3.94 us
  transfers between devices with their start and end apart: 14, of which 3 were waited for; matrix products, arithmetic and copies ran while one was open for 0% of the time, Pallas kernels for 10%

profile of v6, /device:TPU:0, one launch (start us, length us, event | category | flops | bytes accessed | tf_op | source)
XLA Modules:
  0.0 193.8 jit_solution(16931988263946957892)
XLA Ops:
  0.7 1.3 slice_bitcast_fusion
  2.0 3.2 %collective-permute-start.1 = (f32[8,128,128]{2,1,0:T(8,128)S(1)}, f32[8,128,128]{2,1,0:T(8,128)S(1)}, u32[]{:S(2)}, u32[]{:S(2)}) collective-permute-start(f32[8,128,128]{2,1,0:T(8,128)S(1)} %get-tuple-element.62.own1), channel_id=1, source_target_pairs={{0,72},{1,73},{2,74},{3,75},{4,76},{5,77},{6,78},{7,79},{8,0},{9,1... | collective-permute-start | bytes 1572872 | tf_op jit(solution)/shard_map/ppermute | solution.py:414
  5.9 19.4 %all_to_all.40.recv.refs_1_ = f32[16,24,128]{2,1,0:T(8,128)S(1)} all-to-all(f32[16,24,128]{2,1,0:T(8,128)S(1)} %pad_maximum_fusion), channel_id=1, replica_groups={{0,2,4,6,8,10,12,14,64,66,68,70,72,74,76,78},{1,3,5,7,9,11,13,15,65,67,..., dimensions={0} | all-to-all | bytes 393216 | tf_op jit(solution)/shard_map/all_to_all | solution.py:49
  25.2 1.4 start.1
  27.6 3.2 %collective-permute-start.3 = (f32[16,128,128]{2,1,0:T(8,128)}, f32[16,128,128]{2,1,0:T(8,128)}, u32[]{:S(2)}, u32[]{:S(2)}) collective-permute-start(f32[16,128,128]{2,1,0:T(8,128)} %get-tuple-element.33), channel_id=1, source_target_pairs={{0,72},{1,73},{2,74},{3,75},{4,76},{5,77},{6,78},{7,79},{8,0},{9,1... | collective-permute-start | bytes 3145736 | tf_op jit(solution)/shard_map/ppermute | solution.py:436
  30.8 5.3 %all-to-all-start.1 = ((f32[16,128,128]{2,1,0:T(8,128)}), f32[16,128,128]{2,1,0:T(8,128)S(1)}, u32[]{:S(2)}, u32[]{:S(2)}) async-start(f32[16,128,128]{2,1,0:T(8,128)} %copy-done), calls=%async_computation.1 | async-start | bytes 2097152 | tf_op jit(solution)/shard_map/all_to_all | solution.py:49
  36.4 14.6 %all-to-all-done.1.recv = f32[16,128,128]{2,1,0:T(8,128)S(1)} async-done(((f32[16,128,128]{2,1,0:T(8,128)}), f32[16,128,128]{2,1,0:T(8,128)S(1)}, u32[]{:S(2)}, u32[]{:S(2)}) %all-to-all-start.1) | async-done | bytes 1048608 | tf_op jit(solution)/shard_map/all_to_all | solution.py:49
  50.9 2.2 %early.1 = (bf16[2048,1024]{1,0:T(8,128)(2,1)S(1)}, bf16[2048,1024]{1,0:T(8,128)(2,1)S(1)}, f32[16,64,128]{2,1,0:T(8,128)S(1)}) custom-call(s32[66]{0:T(128)S(1)} %pad_add_fusion.codes, f32[8,128,128]{2,1,0:T(8,128)S(1)} %get-tuple-element.63.own0, f32[8,128,128]{2,1,0:T(8,128)S(1)} %get-tuple-element.62.own1, ...), custom_call_target="tpu_custom_call" | custom-call | tf_op jit(solution)/shard_map/early/pallas_call | solution.py:126
  53.2 3.5 %late.1 = (bf16[2048,1024]{1,0:T(8,128)(2,1)S(1)}, bf16[2048,1024]{1,0:T(8,128)(2,1)S(1)}) custom-call(s32[66]{0:T(128)S(1)} %pad_add_fusion.codes, f32[16,128,128]{2,1,0:T(8,128)} %collective-permute-done.2.wave_in, f32[16,128,128]{2,1,0:T(8,128)} %collective-permute-done.3.back_in, bf16[2048,1024]{1,0:T(8,128)(2,1)S(1)} %get-tuple-element.34.hi0, ...), custom_call_target="tpu_custom_call" | custom-call | tf_op jit(solution)/shard_map/late/pallas_call | solution.py:137
  56.7 1.3 mate.3
  58.6 1.9 %mirror.3 = (f32[1024,128]{1,0:T(8,128)S(1)}, f32[8,128]{1,0:T(8,128)S(1)}) custom-call(f32[16,128,128]{2,1,0:T(8,128)S(1)} %all-to-all-done.1.recv, f32[16,64,128]{2,1,0:T(8,128)S(1)} %collective-permute-done.4.other, bf16[2048,1024]{1,0:T(8,128)(2,1)S(1)} %get-tuple-element.36.hi, bf16[2048,1024]{1,0:T(8,128)(2,1)S(1)} %get-tuple-element.37.lo, ...), custom_call_target="tpu_custom_call" | custom-call | tf_op jit(solution)/shard_map/mirror/pallas_call | solution.py:212
  60.7 1.3 own_rows.3.ours
  62.1 22.1 %all_to_all.41.refs_0_ = f32[16,136,128]{2,1,0:T(8,128)S(1)} all-to-all(f32[16,136,128]{2,1,0:T(8,128)S(1)} %join.3), channel_id=1, replica_groups={{0,2,4,6,16,18,20,22,32,34,36,38,48,50,52,54},{1,3,5,7,17,19,21,23,33,3..., dimensions={0} | all-to-all | bytes 2228224 | tf_op jit(solution)/shard_map/all_to_all | solution.py:49
  84.4 19.4 %all_to_all.42.recv = f32[16,128,128]{2,1,0:T(8,128)S(1)} all-to-all(f32[16,128,128]{2,1,0:T(8,128)S(1)} %get-tuple-element.42), channel_id=1, replica_groups={{0,2,4,6,16,18,20,22,32,34,36,38,48,50,52,54},{1,3,5,7,17,19,21,23,33,3..., dimensions={0} | all-to-all | bytes 2097152 | tf_op jit(solution)/shard_map/all_to_all | solution.py:49
  103.8 1.3 mate.4
  106.5 1.9 mirror.4
  108.6 1.3 own_rows.4.ours
  110.1 21.6 %all_to_all.43.refs_0_ = f32[16,136,128]{2,1,0:T(8,128)S(1)} all-to-all(f32[16,136,128]{2,1,0:T(8,128)S(1)} %join.4), channel_id=1, replica_groups={{0,2,4,6,16,18,20,22,32,34,36,38,48,50,52,54},{1,3,5,7,17,19,21,23,33,3..., dimensions={0} | all-to-all | bytes 2228224 | tf_op jit(solution)/shard_map/all_to_all | solution.py:49
  131.9 19.7 %all_to_all.44.recv = f32[16,128,128]{2,1,0:T(8,128)S(1)} all-to-all(f32[16,128,128]{2,1,0:T(8,128)S(1)} %get-tuple-element.51), channel_id=1, replica_groups={{0,2,4,6,16,18,20,22,32,34,36,38,48,50,52,54},{1,3,5,7,17,19,21,23,33,3..., dimensions={0} | all-to-all | bytes 2097152 | tf_op jit(solution)/shard_map/all_to_all | solution.py:49
  151.6 1.3 mate.5
  154.2 1.9 mirror.5
  156.4 1.3 own_rows.5.ours
  157.9 21.6 %all_to_all.45.refs_0_ = f32[16,136,128]{2,1,0:T(8,128)S(1)} all-to-all(f32[16,136,128]{2,1,0:T(8,128)S(1)} %join.5), channel_id=1, replica_groups={{0,2,4,6,16,18,20,22,32,34,36,38,48,50,52,54},{1,3,5,7,17,19,21,23,33,3..., dimensions={0} | all-to-all | bytes 2228224 | tf_op jit(solution)/shard_map/all_to_all | solution.py:49
  179.6 13.4 %all_to_all.46.recv = f32[16,2,16,128]{3,2,1,0:T(8,128)S(1)} all-to-all(f32[16,2,16,128]{3,2,1,0:T(8,128)S(1)} %update.5), channel_id=1, replica_groups={{0,2,4,6,8,10,12,14,64,66,68,70,72,74,76,78},{1,3,5,7,9,11,13,15,65,67,..., dimensions={0} | all-to-all | bytes 524288 | tf_op jit(solution)/shard_map/all_to_all | solution.py:49
  (57 shorter events, 7.1 us)
Async XLA Ops:
  0.6 4.5 %copy-start.3 = (s32[2,1]{0,1:T(1,128)S(1)}, s32[2,1]{0,1:T(1,128)}, u32[]{:S(2)}) copy-start(s32[2,1]{0,1:T(1,128)} %param.7) | copy-start | bytes 28
  0.6 4.9 %copy-start.2 = (s32[2,1,8,2]{2,3,1,0:T(2,128)S(1)}, s32[2,1,8,2]{2,3,1,0:T(2,128)}, u32[]{:S(2)}) copy-start(s32[2,1,8,2]{2,3,1,0:T(2,128)} %param.6) | copy-start | bytes 388
  0.7 5.0 %copy-start.1 = (f32[1,64,512]{2,1,0:T(8,128)S(1)}, f32[1,64,512]{2,1,0:T(8,128)}, u32[]{:S(2)}) copy-start(f32[1,64,512]{2,1,0:T(8,128)} %param.4) | copy-start | bytes 393220
  2.0 23.2 %collective-permute-start.1 = (f32[8,128,128]{2,1,0:T(8,128)S(1)}, f32[8,128,128]{2,1,0:T(8,128)S(1)}, u32[]{:S(2)}, u32[]{:S(2)}) collective-permute-start(f32[8,128,128]{2,1,0:T(8,128)S(1)} %get-tuple-element.62.own1), channel_id=1, source_target_pairs={{0,72},{1,73},{2,74},{3,75},{4,76},{5,77},{6,78},{7,79},{8,0},{9,1... | collective-permute-start | bytes 1572872 | tf_op jit(solution)/shard_map/ppermute | solution.py:414
  5.2 20.0 %collective-permute-start = (f32[8,128,128]{2,1,0:T(8,128)S(1)}, f32[8,128,128]{2,1,0:T(8,128)S(1)}, u32[]{:S(2)}, u32[]{:S(2)}) collective-permute-start(f32[8,128,128]{2,1,0:T(8,128)S(1)} %get-tuple-element.63.own0), channel_id=1, source_target_pairs={{0,8},{1,9},{2,10},{3,11},{4,12},{5,13},{6,14},{7,15},{8,64},{9,65... | collective-permute-start | bytes 1572872 | tf_op jit(solution)/shard_map/ppermute | solution.py:413
  26.6 1.0 copy-start
  27.6 25.6 %collective-permute-start.2 = (f32[16,128,128]{2,1,0:T(8,128)}, f32[16,128,128]{2,1,0:T(8,128)}, u32[]{:S(2)}, u32[]{:S(2)}) collective-permute-start(f32[16,128,128]{2,1,0:T(8,128)} %get-tuple-element.32), channel_id=1, source_target_pairs={{0,8},{1,9},{2,10},{3,11},{4,12},{5,13},{6,14},{7,15},{8,64},{9,65... | collective-permute-start | bytes 3145736 | tf_op jit(solution)/shard_map/ppermute | solution.py:435
  27.6 25.6 %collective-permute-start.3 = (f32[16,128,128]{2,1,0:T(8,128)}, f32[16,128,128]{2,1,0:T(8,128)}, u32[]{:S(2)}, u32[]{:S(2)}) collective-permute-start(f32[16,128,128]{2,1,0:T(8,128)} %get-tuple-element.33), channel_id=1, source_target_pairs={{0,72},{1,73},{2,74},{3,75},{4,76},{5,77},{6,78},{7,79},{8,0},{9,1... | collective-permute-start | bytes 3145736 | tf_op jit(solution)/shard_map/ppermute | solution.py:436
  30.8 20.1 %all-to-all-start.1 = ((f32[16,128,128]{2,1,0:T(8,128)}), f32[16,128,128]{2,1,0:T(8,128)S(1)}, u32[]{:S(2)}, u32[]{:S(2)}) async-start(f32[16,128,128]{2,1,0:T(8,128)} %copy-done), calls=%async_computation.1 | async-start | bytes 2097152 | tf_op jit(solution)/shard_map/all_to_all | solution.py:49
  53.1 5.5 %collective-permute-start.4 = (f32[16,64,128]{2,1,0:T(8,128)S(1)}, f32[16,64,128]{2,1,0:T(8,128)S(1)}, u32[]{:S(2)}, u32[]{:S(2)}) collective-permute-start(f32[16,64,128]{2,1,0:T(8,128)S(1)} %get-tuple-element.38), channel_id=1, source_target_pairs={{0,1},{1,0},{2,3},{3,2},{4,5},{5,4},{6,7},{7,6},{8,9},{9,8},{10,11... | collective-permute-start | bytes 1572872 | tf_op jit(solution)/shard_map/ppermute | solution.py:264
  58.1 4.0 %collective-permute-start.5 = (f32[1024,128]{1,0:T(8,128)S(1)}, f32[1024,128]{1,0:T(8,128)S(1)}, u32[]{:S(2)}, u32[]{:S(2)}) collective-permute-start(f32[1024,128]{1,0:T(8,128)S(1)} %mate.3), channel_id=1, source_target_pairs={{0,1},{1,0},{2,3},{3,2},{4,5},{5,4},{6,7},{7,6},{8,9},{9,8},{10,11... | collective-permute-start | bytes 1572872 | tf_op jit(solution)/shard_map/ppermute | solution.py:265
  60.6 1.4 collective-permute-start.6
  103.8 2.7 %collective-permute-start.7 = (f32[16,128,128]{2,1,0:T(8,128)S(1)}, f32[16,128,128]{2,1,0:T(8,128)S(1)}, u32[]{:S(2)}, u32[]{:S(2)}) collective-permute-start(f32[16,128,128]{2,1,0:T(8,128)S(1)} %all_to_all.42.recv), channel_id=1, source_target_pairs={{0,1},{1,0},{2,3},{3,2},{4,5},{5,4},{6,7},{7,6},{8,9},{9,8},{10,11... | collective-permute-start | bytes 3145736 | tf_op jit(solution)/shard_map/ppermute | solution.py:264
  105.1 4.8 %collective-permute-start.8 = (f32[1024,128]{1,0:T(8,128)S(1)}, f32[1024,128]{1,0:T(8,128)S(1)}, u32[]{:S(2)}, u32[]{:S(2)}) collective-permute-start(f32[1024,128]{1,0:T(8,128)S(1)} %mate.4), channel_id=1, source_target_pairs={{0,1},{1,0},{2,3},{3,2},{4,5},{5,4},{6,7},{7,6},{8,9},{9,8},{10,11... | collective-permute-start | bytes 1572872 | tf_op jit(solution)/shard_map/ppermute | solution.py:265
  108.4 1.5 collective-permute-start.9
  151.6 2.7 %collective-permute-start.10 = (f32[16,128,128]{2,1,0:T(8,128)S(1)}, f32[16,128,128]{2,1,0:T(8,128)S(1)}, u32[]{:S(2)}, u32[]{:S(2)}) collective-permute-start(f32[16,128,128]{2,1,0:T(8,128)S(1)} %all_to_all.44.recv), channel_id=1, source_target_pairs={{0,1},{1,0},{2,3},{3,2},{4,5},{5,4},{6,7},{7,6},{8,9},{9,8},{10,11... | collective-permute-start | bytes 3145736 | tf_op jit(solution)/shard_map/ppermute | solution.py:264
  152.9 4.8 %collective-permute-start.11 = (f32[1024,128]{1,0:T(8,128)S(1)}, f32[1024,128]{1,0:T(8,128)S(1)}, u32[]{:S(2)}, u32[]{:S(2)}) collective-permute-start(f32[1024,128]{1,0:T(8,128)S(1)} %mate.5), channel_id=1, source_target_pairs={{0,1},{1,0},{2,3},{3,2},{4,5},{5,4},{6,7},{7,6},{8,9},{9,8},{10,11... | collective-permute-start | bytes 1572872 | tf_op jit(solution)/shard_map/ppermute | solution.py:265
  156.2 1.5 collective-permute-start.12

commit v7 on v6

--- a/solution.py
+++ b/solution.py
@@ -290,7 +290,7 @@
     return out
 
 
-def start_body(recv, left0, own1, right1, own0, send, sums, wave, back, work, sems):
+def pack_body(left0, own1, right1, own0, recv, wave, back, sems):
     pieces = ((left0, wave, 0), (own1, wave, 8), (right1, back, 0), (own0, back, 8))
     copies = [
         pltpu.make_async_copy(src, dst.at[pl.ds(first, 8)], sems.at[i])
@@ -298,32 +298,41 @@
     ]
     for copy in copies:
         copy.start()
-    spread(lambda s, g: recv[s * 4 + g, :16], work)
-    copies.append(pltpu.make_async_copy(work, send, sems.at[4]))
-    copies[-1].start()
+    for copy in copies:
+        copy.wait()
+
+
+def pack(*operands):
+    big = jax.ShapeDtypeStruct((16, 128, 128), jnp.float32)
+    return call(
+        pack_body,
+        out_shape=(big, big),
+        in_specs=[VMEM] * 5,
+        out_specs=(HBM, HBM),
+        scratch_shapes=[pltpu.SemaphoreType.DMA((4,))],
+        name="pack",
+    )(*operands)
+
+
+def start_body(recv, send, sums):
+    spread(lambda s, g: recv[s * 4 + g, :16], send)
     square = jnp.zeros((16, 128), jnp.float32)
     for i in range(16):
         piece = recv[i, :16]
         square = square + piece * piece
     sums[...] = rows_of(row_sum(square))
-    for copy in copies:
-        copy.wait()
-
-
-def start(*operands):
+
+
+def start(recv):
     big = jax.ShapeDtypeStruct((16, 128, 128), jnp.float32)
     small = jax.ShapeDtypeStruct((8, 128), jnp.float32)
     return call(
         start_body,
-        out_shape=(big, small, big, big),
-        in_specs=[VMEM] * 5,
-        out_specs=(HBM, VMEM, HBM, HBM),
-        scratch_shapes=[
-            pltpu.VMEM((16, 128, 128), jnp.float32),
-            pltpu.SemaphoreType.DMA((5,)),
-        ],
+        out_shape=(big, small),
+        in_specs=[VMEM],
+        out_specs=(VMEM, VMEM),
         name="start",
-    )(*operands)
+    )(recv)
 
 
 def update_body(step, *refs):
@@ -430,7 +439,8 @@
         [codes.reshape(64).astype(jnp.int32), jnp.stack([yh * 2 + yl, k]).astype(jnp.int32)]
     )
 
-    send, sums, wave, back = start(recv, left0, own1, right1, own0)
+    wave, back = pack(left0, own1, right1, own0, recv)
+    send, sums = start(recv)
     state = (recv,)
     wave = lax.ppermute(wave, RC, shift_y(1))
     back = lax.ppermute(back, RC, shift_y(3))

time: 194 us -> 193 us (level)
  no operation moved by 1% of the time
where the time goes in v7:
time: 193 us
  blocking collectives  136 us (70%)
  Pallas kernels  22.2 us (12%)
  waiting for transfers between devices  16.1 us (8%)
  starting transfers between devices  14.1 us (7%)
  local copies, waits for them, and re-layouts  2.94 us (2%)
    all_to_all x7, blocking collectives, exchange(): return lax.all_to_all(send, RC, 0, 0, axis_index_groups=groups, tiled=True)  136 us
    all_to_all x1, waiting for transfers between devices, exchange(): return lax.all_to_all(send, RC, 0, 0, axis_index_groups=groups, tiled=True)  14.6 us
    pallas_call x3, Pallas kernels, mirror(): call(mirror_body, out_shape=(jax.ShapeDtypeStruct((1024, 128), jnp.float3...  5.82 us
    all_to_all x1, starting transfers between devices, exchange(): return lax.all_to_all(send, RC, 0, 0, axis_index_groups=groups, tiled=True)  5.3 us
    pallas_call x3, Pallas kernels, mate(): call(mate_body, out_shape=jax.ShapeDtypeStruct((1024, 128), jnp.float32),...  3.94 us
    pallas_call x3, Pallas kernels, own_rows(): call(own_body, out_shape=jax.ShapeDtypeStruct((1024, 128), jnp.float32),...  3.94 us
  transfers between devices with their start and end apart: 14, of which 3 were waited for; matrix products, arithmetic and copies ran while one was open for 0% of the time, Pallas kernels for 10%

profile of v7, /device:TPU:0, one launch (start us, length us, event | category | flops | bytes accessed | tf_op | source)
XLA Modules:
  0.0 192.8 jit_solution(11594424505356951996)
XLA Ops:
  0.7 1.3 slice_bitcast_fusion
  2.0 3.2 %collective-permute-start.1 = (f32[8,128,128]{2,1,0:T(8,128)S(1)}, f32[8,128,128]{2,1,0:T(8,128)S(1)}, u32[]{:S(2)}, u32[]{:S(2)}) collective-permute-start(f32[8,128,128]{2,1,0:T(8,128)S(1)} %get-tuple-element.62.own1), channel_id=1, source_target_pairs={{0,72},{1,73},{2,74},{3,75},{4,76},{5,77},{6,78},{7,79},{8,0},{9,1... | collective-permute-start | bytes 1572872 | tf_op jit(solution)/shard_map/ppermute | solution.py:423
  5.9 19.4 %all_to_all.40.recv.refs_1_ = f32[16,24,128]{2,1,0:T(8,128)S(1)} all-to-all(f32[16,24,128]{2,1,0:T(8,128)S(1)} %pad_maximum_fusion), channel_id=1, replica_groups={{0,2,4,6,8,10,12,14,64,66,68,70,72,74,76,78},{1,3,5,7,9,11,13,15,65,67,..., dimensions={0} | all-to-all | bytes 393216 | tf_op jit(solution)/shard_map/all_to_all | solution.py:49
  25.2 1.4 pack.1
  26.7 3.2 %collective-permute-start.3 = (f32[16,128,128]{2,1,0:T(8,128)}, f32[16,128,128]{2,1,0:T(8,128)}, u32[]{:S(2)}, u32[]{:S(2)}) collective-permute-start(f32[16,128,128]{2,1,0:T(8,128)} %get-tuple-element.33), channel_id=1, source_target_pairs={{0,72},{1,73},{2,74},{3,75},{4,76},{5,77},{6,78},{7,79},{8,0},{9,1... | collective-permute-start | bytes 3145736 | tf_op jit(solution)/shard_map/ppermute | solution.py:446
  31.0 5.3 %all-to-all-start.1 = ((f32[16,128,128]{2,1,0:T(8,128)}), f32[16,128,128]{2,1,0:T(8,128)S(1)}, u32[]{:S(2)}, u32[]{:S(2)}) async-start(f32[16,128,128]{2,1,0:T(8,128)} %copy-done), calls=%async_computation.1 | async-start | bytes 2097152 | tf_op jit(solution)/shard_map/all_to_all | solution.py:49
  36.5 14.6 %all-to-all-done.1.recv = f32[16,128,128]{2,1,0:T(8,128)S(1)} async-done(((f32[16,128,128]{2,1,0:T(8,128)}), f32[16,128,128]{2,1,0:T(8,128)S(1)}, u32[]{:S(2)}, u32[]{:S(2)}) %all-to-all-start.1) | async-done | bytes 1048608 | tf_op jit(solution)/shard_map/all_to_all | solution.py:49
  51.1 2.1 %early.1 = (bf16[2048,1024]{1,0:T(8,128)(2,1)S(1)}, bf16[2048,1024]{1,0:T(8,128)(2,1)S(1)}, f32[16,64,128]{2,1,0:T(8,128)S(1)}) custom-call(s32[66]{0:T(128)S(1)} %pad_add_fusion.codes, f32[8,128,128]{2,1,0:T(8,128)S(1)} %get-tuple-element.63.own0, f32[8,128,128]{2,1,0:T(8,128)S(1)} %get-tuple-element.62.own1, ...), custom_call_target="tpu_custom_call" | custom-call | tf_op jit(solution)/shard_map/early/pallas_call | solution.py:126
  53.3 3.5 %late.1 = (bf16[2048,1024]{1,0:T(8,128)(2,1)S(1)}, bf16[2048,1024]{1,0:T(8,128)(2,1)S(1)}) custom-call(s32[66]{0:T(128)S(1)} %pad_add_fusion.codes, f32[16,128,128]{2,1,0:T(8,128)} %collective-permute-done.2.wave_in, f32[16,128,128]{2,1,0:T(8,128)} %collective-permute-done.3.back_in, bf16[2048,1024]{1,0:T(8,128)(2,1)S(1)} %get-tuple-element.34.hi0, ...), custom_call_target="tpu_custom_call" | custom-call | tf_op jit(solution)/shard_map/late/pallas_call | solution.py:137
  56.8 1.3 mate.3
  58.6 1.9 %mirror.3 = (f32[1024,128]{1,0:T(8,128)S(1)}, f32[8,128]{1,0:T(8,128)S(1)}) custom-call(f32[16,128,128]{2,1,0:T(8,128)S(1)} %all-to-all-done.1.recv, f32[16,64,128]{2,1,0:T(8,128)S(1)} %collective-permute-done.4.other, bf16[2048,1024]{1,0:T(8,128)(2,1)S(1)} %get-tuple-element.36.hi, bf16[2048,1024]{1,0:T(8,128)(2,1)S(1)} %get-tuple-element.37.lo, ...), custom_call_target="tpu_custom_call" | custom-call | tf_op jit(solution)/shard_map/mirror/pallas_call | solution.py:212
  60.7 1.3 own_rows.3.ours
  62.2 21.7 %all_to_all.41.refs_0_ = f32[16,136,128]{2,1,0:T(8,128)S(1)} all-to-all(f32[16,136,128]{2,1,0:T(8,128)S(1)} %join.3), channel_id=1, replica_groups={{0,2,4,6,16,18,20,22,32,34,36,38,48,50,52,54},{1,3,5,7,17,19,21,23,33,3..., dimensions={0} | all-to-all | bytes 2228224 | tf_op jit(solution)/shard_map/all_to_all | solution.py:49
  84.1 19.8 %all_to_all.42.recv = f32[16,128,128]{2,1,0:T(8,128)S(1)} all-to-all(f32[16,128,128]{2,1,0:T(8,128)S(1)} %get-tuple-element.42), channel_id=1, replica_groups={{0,2,4,6,16,18,20,22,32,34,36,38,48,50,52,54},{1,3,5,7,17,19,21,23,33,3..., dimensions={0} | all-to-all | bytes 2097152 | tf_op jit(solution)/shard_map/all_to_all | solution.py:49
  103.9 1.3 mate.4
  106.5 1.9 %mirror.4 = (f32[1024,128]{1,0:T(8,128)S(1)}, f32[8,128]{1,0:T(8,128)S(1)}) custom-call(f32[16,128,128]{2,1,0:T(8,128)S(1)} %all_to_all.42.recv, f32[16,128,128]{2,1,0:T(8,128)S(1)} %collective-permute-done.7.other, bf16[2048,1024]{1,0:T(8,128)(2,1)S(1)} %get-tuple-element.36.hi, bf16[2048,1024]{1,0:T(8,128)(2,1)S(1)} %get-tuple-element.37.lo, ...), custom_call_target="tpu_custom_call" | custom-call | tf_op jit(solution)/shard_map/mirror/pallas_call | solution.py:212
  108.7 1.3 own_rows.4.ours
  110.1 21.6 %all_to_all.43.refs_0_ = f32[16,136,128]{2,1,0:T(8,128)S(1)} all-to-all(f32[16,136,128]{2,1,0:T(8,128)S(1)} %join.4), channel_id=1, replica_groups={{0,2,4,6,16,18,20,22,32,34,36,38,48,50,52,54},{1,3,5,7,17,19,21,23,33,3..., dimensions={0} | all-to-all | bytes 2228224 | tf_op jit(solution)/shard_map/all_to_all | solution.py:49
  131.9 19.7 %all_to_all.44.recv = f32[16,128,128]{2,1,0:T(8,128)S(1)} all-to-all(f32[16,128,128]{2,1,0:T(8,128)S(1)} %get-tuple-element.51), channel_id=1, replica_groups={{0,2,4,6,16,18,20,22,32,34,36,38,48,50,52,54},{1,3,5,7,17,19,21,23,33,3..., dimensions={0} | all-to-all | bytes 2097152 | tf_op jit(solution)/shard_map/all_to_all | solution.py:49
  151.7 1.3 mate.5
  154.3 1.9 %mirror.5 = (f32[1024,128]{1,0:T(8,128)S(1)}, f32[8,128]{1,0:T(8,128)S(1)}) custom-call(f32[16,128,128]{2,1,0:T(8,128)S(1)} %all_to_all.44.recv, f32[16,128,128]{2,1,0:T(8,128)S(1)} %collective-permute-done.10.other, bf16[2048,1024]{1,0:T(8,128)(2,1)S(1)} %get-tuple-element.36.hi, bf16[2048,1024]{1,0:T(8,128)(2,1)S(1)} %get-tuple-element.37.lo, ...), custom_call_target="tpu_custom_call" | custom-call | tf_op jit(solution)/shard_map/mirror/pallas_call | solution.py:212
  156.5 1.3 own_rows.5.ours
  157.9 21.6 %all_to_all.45.refs_0_ = f32[16,136,128]{2,1,0:T(8,128)S(1)} all-to-all(f32[16,136,128]{2,1,0:T(8,128)S(1)} %join.5), channel_id=1, replica_groups={{0,2,4,6,16,18,20,22,32,34,36,38,48,50,52,54},{1,3,5,7,17,19,21,23,33,3..., dimensions={0} | all-to-all | bytes 2228224 | tf_op jit(solution)/shard_map/all_to_all | solution.py:49
  179.7 12.4 %all_to_all.46.recv = f32[16,2,16,128]{3,2,1,0:T(8,128)S(1)} all-to-all(f32[16,2,16,128]{3,2,1,0:T(8,128)S(1)} %update.5), channel_id=1, replica_groups={{0,2,4,6,8,10,12,14,64,66,68,70,72,74,76,78},{1,3,5,7,9,11,13,15,65,67,..., dimensions={0} | all-to-all | bytes 524288 | tf_op jit(solution)/shard_map/all_to_all | solution.py:49
  (58 shorter events, 7.3 us)
Async XLA Ops:
  0.6 4.5 %copy-start.3 = (s32[2,1]{0,1:T(1,128)S(1)}, s32[2,1]{0,1:T(1,128)}, u32[]{:S(2)}) copy-start(s32[2,1]{0,1:T(1,128)} %param.7) | copy-start | bytes 28
  0.6 4.9 %copy-start.2 = (s32[2,1,8,2]{2,3,1,0:T(2,128)S(1)}, s32[2,1,8,2]{2,3,1,0:T(2,128)}, u32[]{:S(2)}) copy-start(s32[2,1,8,2]{2,3,1,0:T(2,128)} %param.6) | copy-start | bytes 388
  0.7 5.0 %copy-start.1 = (f32[1,64,512]{2,1,0:T(8,128)S(1)}, f32[1,64,512]{2,1,0:T(8,128)}, u32[]{:S(2)}) copy-start(f32[1,64,512]{2,1,0:T(8,128)} %param.4) | copy-start | bytes 393220
  2.0 23.2 %collective-permute-start.1 = (f32[8,128,128]{2,1,0:T(8,128)S(1)}, f32[8,128,128]{2,1,0:T(8,128)S(1)}, u32[]{:S(2)}, u32[]{:S(2)}) collective-permute-start(f32[8,128,128]{2,1,0:T(8,128)S(1)} %get-tuple-element.62.own1), channel_id=1, source_target_pairs={{0,72},{1,73},{2,74},{3,75},{4,76},{5,77},{6,78},{7,79},{8,0},{9,1... | collective-permute-start | bytes 1572872 | tf_op jit(solution)/shard_map/ppermute | solution.py:423
  5.2 20.0 %collective-permute-start = (f32[8,128,128]{2,1,0:T(8,128)S(1)}, f32[8,128,128]{2,1,0:T(8,128)S(1)}, u32[]{:S(2)}, u32[]{:S(2)}) collective-permute-start(f32[8,128,128]{2,1,0:T(8,128)S(1)} %get-tuple-element.63.own0), channel_id=1, source_target_pairs={{0,8},{1,9},{2,10},{3,11},{4,12},{5,13},{6,14},{7,15},{8,64},{9,65... | collective-permute-start | bytes 1572872 | tf_op jit(solution)/shard_map/ppermute | solution.py:422
  26.6 26.7 %collective-permute-start.2 = (f32[16,128,128]{2,1,0:T(8,128)}, f32[16,128,128]{2,1,0:T(8,128)}, u32[]{:S(2)}, u32[]{:S(2)}) collective-permute-start(f32[16,128,128]{2,1,0:T(8,128)} %get-tuple-element.32), channel_id=1, source_target_pairs={{0,8},{1,9},{2,10},{3,11},{4,12},{5,13},{6,14},{7,15},{8,64},{9,65... | collective-permute-start | bytes 3145736 | tf_op jit(solution)/shard_map/ppermute | solution.py:445
  26.7 26.6 %collective-permute-start.3 = (f32[16,128,128]{2,1,0:T(8,128)}, f32[16,128,128]{2,1,0:T(8,128)}, u32[]{:S(2)}, u32[]{:S(2)}) collective-permute-start(f32[16,128,128]{2,1,0:T(8,128)} %get-tuple-element.33), channel_id=1, source_target_pairs={{0,72},{1,73},{2,74},{3,75},{4,76},{5,77},{6,78},{7,79},{8,0},{9,1... | collective-permute-start | bytes 3145736 | tf_op jit(solution)/shard_map/ppermute | solution.py:446
  30.0 1.0 copy-start
  31.0 20.1 %all-to-all-start.1 = ((f32[16,128,128]{2,1,0:T(8,128)}), f32[16,128,128]{2,1,0:T(8,128)S(1)}, u32[]{:S(2)}, u32[]{:S(2)}) async-start(f32[16,128,128]{2,1,0:T(8,128)} %copy-done), calls=%async_computation.1 | async-start | bytes 2097152 | tf_op jit(solution)/shard_map/all_to_all | solution.py:49
  53.2 5.5 %collective-permute-start.4 = (f32[16,64,128]{2,1,0:T(8,128)S(1)}, f32[16,64,128]{2,1,0:T(8,128)S(1)}, u32[]{:S(2)}, u32[]{:S(2)}) collective-permute-start(f32[16,64,128]{2,1,0:T(8,128)S(1)} %get-tuple-element.38), channel_id=1, source_target_pairs={{0,1},{1,0},{2,3},{3,2},{4,5},{5,4},{6,7},{7,6},{8,9},{9,8},{10,11... | collective-permute-start | bytes 1572872 | tf_op jit(solution)/shard_map/ppermute | solution.py:264
  58.1 4.0 %collective-permute-start.5 = (f32[1024,128]{1,0:T(8,128)S(1)}, f32[1024,128]{1,0:T(8,128)S(1)}, u32[]{:S(2)}, u32[]{:S(2)}) collective-permute-start(f32[1024,128]{1,0:T(8,128)S(1)} %mate.3), channel_id=1, source_target_pairs={{0,1},{1,0},{2,3},{3,2},{4,5},{5,4},{6,7},{7,6},{8,9},{9,8},{10,11... | collective-permute-start | bytes 1572872 | tf_op jit(solution)/shard_map/ppermute | solution.py:265
  60.6 1.5 collective-permute-start.6
  103.9 2.7 %collective-permute-start.7 = (f32[16,128,128]{2,1,0:T(8,128)S(1)}, f32[16,128,128]{2,1,0:T(8,128)S(1)}, u32[]{:S(2)}, u32[]{:S(2)}) collective-permute-start(f32[16,128,128]{2,1,0:T(8,128)S(1)} %all_to_all.42.recv), channel_id=1, source_target_pairs={{0,1},{1,0},{2,3},{3,2},{4,5},{5,4},{6,7},{7,6},{8,9},{9,8},{10,11... | collective-permute-start | bytes 3145736 | tf_op jit(solution)/shard_map/ppermute | solution.py:264
  105.2 4.8 %collective-permute-start.8 = (f32[1024,128]{1,0:T(8,128)S(1)}, f32[1024,128]{1,0:T(8,128)S(1)}, u32[]{:S(2)}, u32[]{:S(2)}) collective-permute-start(f32[1024,128]{1,0:T(8,128)S(1)} %mate.4), channel_id=1, source_target_pairs={{0,1},{1,0},{2,3},{3,2},{4,5},{5,4},{6,7},{7,6},{8,9},{9,8},{10,11... | collective-permute-start | bytes 1572872 | tf_op jit(solution)/shard_map/ppermute | solution.py:265
  108.5 1.5 collective-permute-start.9
  151.7 2.7 %collective-permute-start.10 = (f32[16,128,128]{2,1,0:T(8,128)S(1)}, f32[16,128,128]{2,1,0:T(8,128)S(1)}, u32[]{:S(2)}, u32[]{:S(2)}) collective-permute-start(f32[16,128,128]{2,1,0:T(8,128)S(1)} %all_to_all.44.recv), channel_id=1, source_target_pairs={{0,1},{1,0},{2,3},{3,2},{4,5},{5,4},{6,7},{7,6},{8,9},{9,8},{10,11... | collective-permute-start | bytes 3145736 | tf_op jit(solution)/shard_map/ppermute | solution.py:264
  153.0 4.8 %collective-permute-start.11 = (f32[1024,128]{1,0:T(8,128)S(1)}, f32[1024,128]{1,0:T(8,128)S(1)}, u32[]{:S(2)}, u32[]{:S(2)}) collective-permute-start(f32[1024,128]{1,0:T(8,128)S(1)} %mate.5), channel_id=1, source_target_pairs={{0,1},{1,0},{2,3},{3,2},{4,5},{5,4},{6,7},{7,6},{8,9},{9,8},{10,11... | collective-permute-start | bytes 1572872 | tf_op jit(solution)/shard_map/ppermute | solution.py:265
  156.3 1.5 collective-permute-start.12

commit v8 on v7

--- a/solution.py
+++ b/solution.py
@@ -189,7 +189,7 @@
     )(recv, hi, lo)
 
 
-def mirror_body(recv, other, hi, lo, sums, out, scalars, back):
+def mirror_body(recv, other, hi, lo, sums, after, out, scalars, back):
     for i in range(4):
         ref = (recv, other)[i // 2]
         pairs = [parted(chunk(ref, (i % 2) * 2 + c).T) for c in range(2)]
@@ -208,31 +208,30 @@
     scalars[...] = jnp.where(place == 2, row_sum(curve) * (2 * DIFFUSION), sums[...])
 
 
-def mirror(recv, other, hi, lo, sums):
+def mirror(recv, other, hi, lo, sums, after):
     return call(
         mirror_body,
         out_shape=(
             jax.ShapeDtypeStruct((1024, 128), jnp.float32),
             jax.ShapeDtypeStruct((8, 128), jnp.float32),
         ),
-        in_specs=[VMEM] * 5,
+        in_specs=[VMEM] * 6,
         out_specs=(VMEM, VMEM),
         scratch_shapes=[pltpu.VMEM((128, 1024), jnp.float32)],
         name="mirror",
-    )(recv, other, hi, lo, sums)
-
-
-def own_body(recv, hi, lo, after, out, right):
+    )(recv, other, hi, lo, sums, after)
+
+
+def own_body(first, recv, hi, lo, after, out, right):
     part_right(recv, right)
-    for i in range(2):
-        rows = slice(i * 512, (i + 1) * 512)
-        out[rows, :] = forward(hi[rows, :], lo[rows, :], right)
-
-
-def own_rows(recv, hi, lo, after):
-    return call(
-        own_body,
-        out_shape=jax.ShapeDtypeStruct((1024, 128), jnp.float32),
+    rows = slice(first, first + 512)
+    out[...] = forward(hi[rows, :], lo[rows, :], right)
+
+
+def own_rows(first, recv, hi, lo, after):
+    return call(
+        functools.partial(own_body, first),
+        out_shape=jax.ShapeDtypeStruct((512, 128), jnp.float32),
         in_specs=[VMEM] * 4,
         out_specs=VMEM,
         scratch_shapes=[pltpu.VMEM((1024, 256), jnp.bfloat16)],
@@ -240,33 +239,36 @@
     )(recv, hi, lo, after)
 
 
-def join_body(ours, theirs, mirrored, mine, mates, out):
+def join_body(ours0, ours1, theirs, mirrored, mine, mates, out):
     for s in range(4):
         rows = slice(s * 256, (s + 1) * 256)
-        part = ours[rows, :] + theirs[rows, :]
+        ours = (ours0, ours1)[s // 2]
+        part = ours[(s % 2) * 256 : (s % 2) * 256 + 256, :] + theirs[rows, :]
         out[:, s * 16 : s * 16 + 16, :] = part.reshape(16, 16, 128)
         out[:, 64 + s * 16 : 80 + s * 16, :] = mirrored[rows, :].reshape(16, 16, 128)
     row = mine[...] + mates[...]
     out[:, 128:136, :] = jnp.broadcast_to(row[None], (16, 8, 128))
 
 
-def join(ours, theirs, mirrored, mine, mates):
+def join(ours0, ours1, theirs, mirrored, mine, mates):
     return call(
         join_body,
         out_shape=jax.ShapeDtypeStruct((16, 136, 128), jnp.float32),
-        in_specs=[VMEM] * 5,
+        in_specs=[VMEM] * 6,
         out_specs=VMEM,
         name="join",
-    )(ours, theirs, mirrored, mine, mates)
+    )(ours0, ours1, theirs, mirrored, mine, mates)
 
 
 def multiply(recv, share, sums, hi, lo):
     other = lax.ppermute(share, RC, SWAP)
-    theirs = lax.ppermute(mate(recv, hi, lo), RC, SWAP)
-    mirrored, mine = mirror(recv, other, hi, lo, sums)
+    part = mate(recv, hi, lo)
+    theirs = lax.ppermute(part, RC, SWAP)
+    ours0 = own_rows(0, recv, hi, lo, part)
+    mirrored, mine = mirror(recv, other, hi, lo, sums, ours0)
     mates = lax.ppermute(mine, RC, SWAP)
-    ours = own_rows(recv, hi, lo, mine)
-    return join(ours, theirs, mirrored, mine, mates)
+    ours1 = own_rows(512, recv, hi, lo, mine)
+    return join(ours0, ours1, theirs, mirrored, mine, mates)
 
 
 def spread(field, send):
@@ -288,6 +290,29 @@
     for i, row in enumerate(rows):
         out = jnp.where(place == i, row, out)
     return out
+
+
+def halves_body(blocks, own0, own1, sems):
+    copies = [
+        pltpu.make_async_copy(blocks.at[i, 0], out, sems.at[i])
+        for i, out in enumerate((own0, own1))
+    ]
+    for copy in copies:
+        copy.start()
+    for copy in copies:
+        copy.wait()
+
+
+def halves(blocks):
+    half = jax.ShapeDtypeStruct((8, 128, 128), jnp.float32)
+    return call(
+        halves_body,
+        out_shape=(half, half),
+        in_specs=[HBM],
+        out_specs=(VMEM, VMEM),
+        scratch_shapes=[pltpu.SemaphoreType.DMA((2,))],
+        name="halves",
+    )(blocks)
 
 
 def pack_body(left0, own1, right1, own0, recv, wave, back, sems):
@@ -417,8 +442,7 @@
     r = lax.axis_index("row")
     c = lax.axis_index("col")
     yh, yl, z, k = r // 4, c // 8, (c // 2) % 4, c % 2
-    own0 = affinity_blocks[0, 0]
-    own1 = affinity_blocks[1, 0]
+    own0, own1 = halves(affinity_blocks)
     left0 = lax.ppermute(own0, RC, shift_y(1))
     right1 = lax.ppermute(own1, RC, shift_y(3))
 

time: 193 us -> 192 us (level)
  blocking collectives: 136 us -> 134 us
    all_to_all x7, blocking collectives: 136 us -> 134 us  [exchange(): return lax.all_to_all(send, RC, 0, 0, axis_index_groups=groups, tiled=True)]
    pallas_call x3 -> x7, Pallas kernels: 3.94 us -> 4.67 us  [the longest x6 4.58 us: own_rows(): call(functools.partial(own_body, first), out_shape=jax.ShapeDtypeStruct((...]
  transfers between devices with their start and end apart: 14 -> 14, of which waited for: 3 -> 4; matrix products, arithmetic and copies ran while one was open for 0% -> 0% of each run, Pallas kernels for 10% -> 10%
where the time goes in v8:
time: 192 us
  blocking collectives  134 us (70%)
  Pallas kernels  22.9 us (12%)
  waiting for transfers between devices  16.2 us (8%)
  starting transfers between devices  14.4 us (8%)
  local copies, waits for them, and re-layouts  2.82 us (1%)
    all_to_all x7, blocking collectives, exchange(): return lax.all_to_all(send, RC, 0, 0, axis_index_groups=groups, tiled=True)  134 us
    all_to_all x1, waiting for transfers between devices, exchange(): return lax.all_to_all(send, RC, 0, 0, axis_index_groups=groups, tiled=True)  15.2 us
    pallas_call x3, Pallas kernels, mirror(): call(mirror_body, out_shape=(jax.ShapeDtypeStruct((1024, 128), jnp.float3...  5.82 us
    all_to_all x1, starting transfers between devices, exchange(): return lax.all_to_all(send, RC, 0, 0, axis_index_groups=groups, tiled=True)  5.44 us
    pallas_call x6, Pallas kernels, own_rows(): call(functools.partial(own_body, first), out_shape=jax.ShapeDtypeStruct((...  4.58 us
    pallas_call x3, Pallas kernels, mate(): call(mate_body, out_shape=jax.ShapeDtypeStruct((1024, 128), jnp.float32),...  3.94 us
  transfers between devices with their start and end apart: 14, of which 4 were waited for; matrix products, arithmetic and copies ran while one was open for 0% of the time, Pallas kernels for 10%

profile of v8, /device:TPU:0, one launch (start us, length us, event | category | flops | bytes accessed | tf_op | source)
XLA Modules:
  0.0 191.7 jit_solution(16674062438801786095)
XLA Ops:
  0.6 1.2 copy-done
  2.0 1.7 collective-permute-start
  3.7 1.6 collective-permute-start.1
  6.0 17.6 %all_to_all.40.recv.refs_1_ = f32[16,24,128]{2,1,0:T(8,128)S(1)} all-to-all(f32[16,24,128]{2,1,0:T(8,128)S(1)} %pad_maximum_fusion), channel_id=1, replica_groups={{0,2,4,6,8,10,12,14,64,66,68,70,72,74,76,78},{1,3,5,7,9,11,13,15,65,67,..., dimensions={0} | all-to-all | bytes 393216 | tf_op jit(solution)/shard_map/all_to_all | solution.py:49
  23.6 1.4 pack.1
  24.9 1.1 collective-permute-start.2
  26.0 2.2 %collective-permute-start.3 = (f32[16,128,128]{2,1,0:T(8,128)}, f32[16,128,128]{2,1,0:T(8,128)}, u32[]{:S(2)}, u32[]{:S(2)}) collective-permute-start(f32[16,128,128]{2,1,0:T(8,128)} %get-tuple-element.37), channel_id=1, source_target_pairs={{0,72},{1,73},{2,74},{3,75},{4,76},{5,77},{6,78},{7,79},{8,0},{9,1... | collective-permute-start | bytes 3145736 | tf_op jit(solution)/shard_map/ppermute | solution.py:470
  28.3 1.0 copy-done.1
  29.3 5.4 %all-to-all-start.1 = ((f32[16,128,128]{2,1,0:T(8,128)}), f32[16,128,128]{2,1,0:T(8,128)S(1)}, u32[]{:S(2)}, u32[]{:S(2)}) async-start(f32[16,128,128]{2,1,0:T(8,128)} %copy-done.1), calls=%async_computation.1 | async-start | bytes 2097152 | tf_op jit(solution)/shard_map/all_to_all | solution.py:49
  35.0 15.2 %all-to-all-done.1.recv = f32[16,128,128]{2,1,0:T(8,128)S(1)} async-done(((f32[16,128,128]{2,1,0:T(8,128)}), f32[16,128,128]{2,1,0:T(8,128)S(1)}, u32[]{:S(2)}, u32[]{:S(2)}) %all-to-all-start.1) | async-done | bytes 1048608 | tf_op jit(solution)/shard_map/all_to_all | solution.py:49
  50.2 2.2 %early.1 = (bf16[2048,1024]{1,0:T(8,128)(2,1)S(1)}, bf16[2048,1024]{1,0:T(8,128)(2,1)S(1)}, f32[16,64,128]{2,1,0:T(8,128)S(1)}) custom-call(s32[66]{0:T(128)S(1)} %pad_add_fusion.codes, f32[8,128,128]{2,1,0:T(8,128)S(1)} %get-tuple-element.34.own0, f32[8,128,128]{2,1,0:T(8,128)S(1)} %get-tuple-element.35.own1, ...), custom_call_target="tpu_custom_call" | custom-call | tf_op jit(solution)/shard_map/early/pallas_call | solution.py:126
  52.5 3.4 %late.1 = (bf16[2048,1024]{1,0:T(8,128)(2,1)S(1)}, bf16[2048,1024]{1,0:T(8,128)(2,1)S(1)}) custom-call(s32[66]{0:T(128)S(1)} %pad_add_fusion.codes, f32[16,128,128]{2,1,0:T(8,128)} %collective-permute-done.2.wave_in, f32[16,128,128]{2,1,0:T(8,128)} %collective-permute-done.3.back_in, bf16[2048,1024]{1,0:T(8,128)(2,1)S(1)} %get-tuple-element.38.hi0, ...), custom_call_target="tpu_custom_call" | custom-call | tf_op jit(solution)/shard_map/late/pallas_call | solution.py:137
  55.9 1.3 mate.3.after
  58.6 2.0 %mirror.3 = (f32[1024,128]{1,0:T(8,128)S(1)}, f32[8,128]{1,0:T(8,128)S(1)}) custom-call(f32[16,128,128]{2,1,0:T(8,128)S(1)} %all-to-all-done.1.recv, f32[16,64,128]{2,1,0:T(8,128)S(1)} %collective-permute-done.4.other, bf16[2048,1024]{1,0:T(8,128)(2,1)S(1)} %get-tuple-element.40.hi, bf16[2048,1024]{1,0:T(8,128)(2,1)S(1)} %get-tuple-element.41.lo, ...), custom_call_target="tpu_custom_call" | custom-call | tf_op jit(solution)/shard_map/mirror/pallas_call | solution.py:212
  61.9 21.5 %all_to_all.41.refs_0_ = f32[16,136,128]{2,1,0:T(8,128)S(1)} all-to-all(f32[16,136,128]{2,1,0:T(8,128)S(1)} %join.3), channel_id=1, replica_groups={{0,2,4,6,16,18,20,22,32,34,36,38,48,50,52,54},{1,3,5,7,17,19,21,23,33,3..., dimensions={0} | all-to-all | bytes 2228224 | tf_op jit(solution)/shard_map/all_to_all | solution.py:49
  83.6 19.5 %all_to_all.42.recv = f32[16,128,128]{2,1,0:T(8,128)S(1)} all-to-all(f32[16,128,128]{2,1,0:T(8,128)S(1)} %get-tuple-element.46), channel_id=1, replica_groups={{0,2,4,6,16,18,20,22,32,34,36,38,48,50,52,54},{1,3,5,7,17,19,21,23,33,3..., dimensions={0} | all-to-all | bytes 2097152 | tf_op jit(solution)/shard_map/all_to_all | solution.py:49
  103.1 1.3 mate.4.after
  105.8 1.9 %mirror.4 = (f32[1024,128]{1,0:T(8,128)S(1)}, f32[8,128]{1,0:T(8,128)S(1)}) custom-call(f32[16,128,128]{2,1,0:T(8,128)S(1)} %all_to_all.42.recv, f32[16,128,128]{2,1,0:T(8,128)S(1)} %collective-permute-done.7.other, bf16[2048,1024]{1,0:T(8,128)(2,1)S(1)} %get-tuple-element.40.hi, bf16[2048,1024]{1,0:T(8,128)(2,1)S(1)} %get-tuple-element.41.lo, ...), custom_call_target="tpu_custom_call" | custom-call | tf_op jit(solution)/shard_map/mirror/pallas_call | solution.py:212
  109.1 21.4 %all_to_all.43.refs_0_ = f32[16,136,128]{2,1,0:T(8,128)S(1)} all-to-all(f32[16,136,128]{2,1,0:T(8,128)S(1)} %join.4), channel_id=1, replica_groups={{0,2,4,6,16,18,20,22,32,34,36,38,48,50,52,54},{1,3,5,7,17,19,21,23,33,3..., dimensions={0} | all-to-all | bytes 2228224 | tf_op jit(solution)/shard_map/all_to_all | solution.py:49
  130.7 19.5 %all_to_all.44.recv = f32[16,128,128]{2,1,0:T(8,128)S(1)} all-to-all(f32[16,128,128]{2,1,0:T(8,128)S(1)} %get-tuple-element.55), channel_id=1, replica_groups={{0,2,4,6,16,18,20,22,32,34,36,38,48,50,52,54},{1,3,5,7,17,19,21,23,33,3..., dimensions={0} | all-to-all | bytes 2097152 | tf_op jit(solution)/shard_map/all_to_all | solution.py:49
  150.2 1.3 mate.5.after
  152.9 1.9 %mirror.5 = (f32[1024,128]{1,0:T(8,128)S(1)}, f32[8,128]{1,0:T(8,128)S(1)}) custom-call(f32[16,128,128]{2,1,0:T(8,128)S(1)} %all_to_all.44.recv, f32[16,128,128]{2,1,0:T(8,128)S(1)} %collective-permute-done.10.other, bf16[2048,1024]{1,0:T(8,128)(2,1)S(1)} %get-tuple-element.40.hi, bf16[2048,1024]{1,0:T(8,128)(2,1)S(1)} %get-tuple-element.41.lo, ...), custom_call_target="tpu_custom_call" | custom-call | tf_op jit(solution)/shard_map/mirror/pallas_call | solution.py:212
  156.2 21.4 %all_to_all.45.refs_0_ = f32[16,136,128]{2,1,0:T(8,128)S(1)} all-to-all(f32[16,136,128]{2,1,0:T(8,128)S(1)} %join.5), channel_id=1, replica_groups={{0,2,4,6,16,18,20,22,32,34,36,38,48,50,52,54},{1,3,5,7,17,19,21,23,33,3..., dimensions={0} | all-to-all | bytes 2228224 | tf_op jit(solution)/shard_map/all_to_all | solution.py:49
  177.7 13.3 %all_to_all.46.recv = f32[16,2,16,128]{3,2,1,0:T(8,128)S(1)} all-to-all(f32[16,2,16,128]{3,2,1,0:T(8,128)S(1)} %update.5), channel_id=1, replica_groups={{0,2,4,6,8,10,12,14,64,66,68,70,72,74,76,78},{1,3,5,7,9,11,13,15,65,67,..., dimensions={0} | all-to-all | bytes 524288 | tf_op jit(solution)/shard_map/all_to_all | solution.py:49
  (63 shorter events, 10.3 us)
Async XLA Ops:
  0.6 1.2 copy-start
  1.9 3.4 %copy-start.4 = (s32[2,1]{0,1:T(1,128)S(1)}, s32[2,1]{0,1:T(1,128)}, u32[]{:S(2)}) copy-start(s32[2,1]{0,1:T(1,128)} %param.7) | copy-start | bytes 28
  1.9 3.7 %copy-start.3 = (s32[2,1,8,2]{2,3,1,0:T(2,128)S(1)}, s32[2,1,8,2]{2,3,1,0:T(2,128)}, u32[]{:S(2)}) copy-start(s32[2,1,8,2]{2,3,1,0:T(2,128)} %param.6) | copy-start | bytes 388
  1.9 3.9 %copy-start.2 = (f32[1,64,512]{2,1,0:T(8,128)S(1)}, f32[1,64,512]{2,1,0:T(8,128)}, u32[]{:S(2)}) copy-start(f32[1,64,512]{2,1,0:T(8,128)} %param.4) | copy-start | bytes 393220
  2.0 21.6 %collective-permute-start = (f32[8,128,128]{2,1,0:T(8,128)S(1)}, f32[8,128,128]{2,1,0:T(8,128)S(1)}, u32[]{:S(2)}, u32[]{:S(2)}) collective-permute-start(f32[8,128,128]{2,1,0:T(8,128)S(1)} %get-tuple-element.34.own0), channel_id=1, source_target_pairs={{0,8},{1,9},{2,10},{3,11},{4,12},{5,13},{6,14},{7,15},{8,64},{9,65... | collective-permute-start | bytes 1572872 | tf_op jit(solution)/shard_map/ppermute | solution.py:446
  3.7 19.9 %collective-permute-start.1 = (f32[8,128,128]{2,1,0:T(8,128)S(1)}, f32[8,128,128]{2,1,0:T(8,128)S(1)}, u32[]{:S(2)}, u32[]{:S(2)}) collective-permute-start(f32[8,128,128]{2,1,0:T(8,128)S(1)} %get-tuple-element.35.own1), channel_id=1, source_target_pairs={{0,72},{1,73},{2,74},{3,75},{4,76},{5,77},{6,78},{7,79},{8,0},{9,1... | collective-permute-start | bytes 1572872 | tf_op jit(solution)/shard_map/ppermute | solution.py:447
  24.9 27.5 %collective-permute-start.2 = (f32[16,128,128]{2,1,0:T(8,128)}, f32[16,128,128]{2,1,0:T(8,128)}, u32[]{:S(2)}, u32[]{:S(2)}) collective-permute-start(f32[16,128,128]{2,1,0:T(8,128)} %get-tuple-element.36), channel_id=1, source_target_pairs={{0,8},{1,9},{2,10},{3,11},{4,12},{5,13},{6,14},{7,15},{8,64},{9,65... | collective-permute-start | bytes 3145736 | tf_op jit(solution)/shard_map/ppermute | solution.py:469
  26.0 26.5 %collective-permute-start.3 = (f32[16,128,128]{2,1,0:T(8,128)}, f32[16,128,128]{2,1,0:T(8,128)}, u32[]{:S(2)}, u32[]{:S(2)}) collective-permute-start(f32[16,128,128]{2,1,0:T(8,128)} %get-tuple-element.37), channel_id=1, source_target_pairs={{0,72},{1,73},{2,74},{3,75},{4,76},{5,77},{6,78},{7,79},{8,0},{9,1... | collective-permute-start | bytes 3145736 | tf_op jit(solution)/shard_map/ppermute | solution.py:470
  28.3 1.0 copy-start.1
  29.3 20.9 %all-to-all-start.1 = ((f32[16,128,128]{2,1,0:T(8,128)}), f32[16,128,128]{2,1,0:T(8,128)S(1)}, u32[]{:S(2)}, u32[]{:S(2)}) async-start(f32[16,128,128]{2,1,0:T(8,128)} %copy-done.1), calls=%async_computation.1 | async-start | bytes 2097152 | tf_op jit(solution)/shard_map/all_to_all | solution.py:49
  52.4 6.3 %collective-permute-start.4 = (f32[16,64,128]{2,1,0:T(8,128)S(1)}, f32[16,64,128]{2,1,0:T(8,128)S(1)}, u32[]{:S(2)}, u32[]{:S(2)}) collective-permute-start(f32[16,64,128]{2,1,0:T(8,128)S(1)} %get-tuple-element.42), channel_id=1, source_target_pairs={{0,1},{1,0},{2,3},{3,2},{4,5},{5,4},{6,7},{7,6},{8,9},{9,8},{10,11... | collective-permute-start | bytes 1572872 | tf_op jit(solution)/shard_map/ppermute | solution.py:264
  57.3 4.6 %collective-permute-start.5 = (f32[1024,128]{1,0:T(8,128)S(1)}, f32[1024,128]{1,0:T(8,128)S(1)}, u32[]{:S(2)}, u32[]{:S(2)}) collective-permute-start(f32[1024,128]{1,0:T(8,128)S(1)} %mate.3.after), channel_id=1, source_target_pairs={{0,1},{1,0},{2,3},{3,2},{4,5},{5,4},{6,7},{7,6},{8,9},{9,8},{10,11... | collective-permute-start | bytes 1572872 | tf_op jit(solution)/shard_map/ppermute | solution.py:266
  60.6 1.2 collective-permute-start.6
  103.1 2.7 %collective-permute-start.7 = (f32[16,128,128]{2,1,0:T(8,128)S(1)}, f32[16,128,128]{2,1,0:T(8,128)S(1)}, u32[]{:S(2)}, u32[]{:S(2)}) collective-permute-start(f32[16,128,128]{2,1,0:T(8,128)S(1)} %all_to_all.42.recv), channel_id=1, source_target_pairs={{0,1},{1,0},{2,3},{3,2},{4,5},{5,4},{6,7},{7,6},{8,9},{9,8},{10,11... | collective-permute-start | bytes 3145736 | tf_op jit(solution)/shard_map/ppermute | solution.py:264
  104.5 4.3 %collective-permute-start.8 = (f32[1024,128]{1,0:T(8,128)S(1)}, f32[1024,128]{1,0:T(8,128)S(1)}, u32[]{:S(2)}, u32[]{:S(2)}) collective-permute-start(f32[1024,128]{1,0:T(8,128)S(1)} %mate.4.after), channel_id=1, source_target_pairs={{0,1},{1,0},{2,3},{3,2},{4,5},{5,4},{6,7},{7,6},{8,9},{9,8},{10,11... | collective-permute-start | bytes 1572872 | tf_op jit(solution)/shard_map/ppermute | solution.py:266
  107.8 1.2 collective-permute-start.9
  150.2 2.7 %collective-permute-start.10 = (f32[16,128,128]{2,1,0:T(8,128)S(1)}, f32[16,128,128]{2,1,0:T(8,128)S(1)}, u32[]{:S(2)}, u32[]{:S(2)}) collective-permute-start(f32[16,128,128]{2,1,0:T(8,128)S(1)} %all_to_all.44.recv), channel_id=1, source_target_pairs={{0,1},{1,0},{2,3},{3,2},{4,5},{5,4},{6,7},{7,6},{8,9},{9,8},{10,11... | collective-permute-start | bytes 3145736 | tf_op jit(solution)/shard_map/ppermute | solution.py:264
  151.5 4.3 %collective-permute-start.11 = (f32[1024,128]{1,0:T(8,128)S(1)}, f32[1024,128]{1,0:T(8,128)S(1)}, u32[]{:S(2)}, u32[]{:S(2)}) collective-permute-start(f32[1024,128]{1,0:T(8,128)S(1)} %mate.5.after), channel_id=1, source_target_pairs={{0,1},{1,0},{2,3},{3,2},{4,5},{5,4},{6,7},{7,6},{8,9},{9,8},{10,11... | collective-permute-start | bytes 1572872 | tf_op jit(solution)/shard_map/ppermute | solution.py:266
  154.8 1.2 collective-permute-start.12

commit v9 on v8

--- a/solution.py
+++ b/solution.py
@@ -315,11 +315,10 @@
     )(blocks)
 
 
-def pack_body(left0, own1, right1, own0, recv, wave, back, sems):
-    pieces = ((left0, wave, 0), (own1, wave, 8), (right1, back, 0), (own0, back, 8))
+def pack_body(passed, kept, recv, wave, sems):
     copies = [
-        pltpu.make_async_copy(src, dst.at[pl.ds(first, 8)], sems.at[i])
-        for i, (src, dst, first) in enumerate(pieces)
+        pltpu.make_async_copy(src, wave.at[pl.ds(first, 8)], sems.at[i])
+        for i, (src, first) in enumerate(((passed, 0), (kept, 8)))
     ]
     for copy in copies:
         copy.start()
@@ -328,13 +327,12 @@
 
 
 def pack(*operands):
-    big = jax.ShapeDtypeStruct((16, 128, 128), jnp.float32)
     return call(
         pack_body,
-        out_shape=(big, big),
-        in_specs=[VMEM] * 5,
-        out_specs=(HBM, HBM),
-        scratch_shapes=[pltpu.SemaphoreType.DMA((4,))],
+        out_shape=jax.ShapeDtypeStruct((16, 128, 128), jnp.float32),
+        in_specs=[VMEM] * 3,
+        out_specs=HBM,
+        scratch_shapes=[pltpu.SemaphoreType.DMA((2,))],
         name="pack",
     )(*operands)
 
@@ -463,7 +461,8 @@
         [codes.reshape(64).astype(jnp.int32), jnp.stack([yh * 2 + yl, k]).astype(jnp.int32)]
     )
 
-    wave, back = pack(left0, own1, right1, own0, recv)
+    wave = pack(left0, own1, recv)
+    back = pack(right1, own0, recv)
     send, sums = start(recv)
     state = (recv,)
     wave = lax.ppermute(wave, RC, shift_y(1))

time: 192 us -> 193 us (level)
  transfers between devices with their start and end apart: 14 -> 14, of which waited for: 4 -> 4; matrix products, arithmetic and copies ran while one was open for 0% -> 0% of each run, Pallas kernels for 10% -> 11%
where the time goes in v9:
time: 193 us; the launch traced here: 192 us
  blocking collectives  134 us (69%)
  Pallas kernels  23.5 us (12%)
  waiting for transfers between devices  16.2 us (8%)
  starting transfers between devices  14.4 us (7%)
  local copies, waits for them, and re-layouts  2.82 us (1%)
    all_to_all x7, blocking collectives, exchange(): return lax.all_to_all(send, RC, 0, 0, axis_index_groups=groups, tiled=True)  134 us
    all_to_all x1, waiting for transfers between devices, exchange(): return lax.all_to_all(send, RC, 0, 0, axis_index_groups=groups, tiled=True)  15.2 us
    pallas_call x3, Pallas kernels, mirror(): call(mirror_body, out_shape=(jax.ShapeDtypeStruct((1024, 128), jnp.float3...  5.82 us
    all_to_all x1, starting transfers between devices, exchange(): return lax.all_to_all(send, RC, 0, 0, axis_index_groups=groups, tiled=True)  5.44 us
    pallas_call x6, Pallas kernels, own_rows(): call(functools.partial(own_body, first), out_shape=jax.ShapeDtypeStruct((...  4.58 us
    pallas_call x3, Pallas kernels, mate(): call(mate_body, out_shape=jax.ShapeDtypeStruct((1024, 128), jnp.float32),...  3.94 us
  transfers between devices with their start and end apart: 14, of which 4 were waited for; matrix products, arithmetic and copies ran while one was open for 0% of the time, Pallas kernels for 11%

profile of v9, /device:TPU:0, one launch (start us, length us, event | category | flops | bytes accessed | tf_op | source)
XLA Modules:
  0.0 192.3 jit_solution(774223895053317092)
XLA Ops:
  0.6 1.2 copy-done
  2.0 1.7 collective-permute-start
  3.7 1.6 collective-permute-start.2
  6.0 17.6 %all_to_all.40.recv.refs_1_ = f32[16,24,128]{2,1,0:T(8,128)S(1)} all-to-all(f32[16,24,128]{2,1,0:T(8,128)S(1)} %pad_maximum_fusion), channel_id=1, replica_groups={{0,2,4,6,8,10,12,14,64,66,68,70,72,74,76,78},{1,3,5,7,9,11,13,15,65,67,..., dimensions={0} | all-to-all | bytes 393216 | tf_op jit(solution)/shard_map/all_to_all | solution.py:49
  24.5 1.1 collective-permute-start.1
  25.6 1.0 pack.3
  26.6 2.3 %collective-permute-start.3 = (f32[16,128,128]{2,1,0:T(8,128)}, f32[16,128,128]{2,1,0:T(8,128)}, u32[]{:S(2)}, u32[]{:S(2)}) collective-permute-start(f32[16,128,128]{2,1,0:T(8,128)} %pack.3), channel_id=1, source_target_pairs={{0,72},{1,73},{2,74},{3,75},{4,76},{5,77},{6,78},{7,79},{8,0},{9,1... | collective-permute-start | bytes 3145736 | tf_op jit(solution)/shard_map/ppermute | solution.py:469
  29.0 1.0 copy-done.1
  30.0 5.4 %all-to-all-start.1 = ((f32[16,128,128]{2,1,0:T(8,128)}), f32[16,128,128]{2,1,0:T(8,128)S(1)}, u32[]{:S(2)}, u32[]{:S(2)}) async-start(f32[16,128,128]{2,1,0:T(8,128)} %copy-done.1), calls=%async_computation.1 | async-start | bytes 2097152 | tf_op jit(solution)/shard_map/all_to_all | solution.py:49
  35.7 15.2 %all-to-all-done.1.recv = f32[16,128,128]{2,1,0:T(8,128)S(1)} async-done(((f32[16,128,128]{2,1,0:T(8,128)}), f32[16,128,128]{2,1,0:T(8,128)S(1)}, u32[]{:S(2)}, u32[]{:S(2)}) %all-to-all-start.1) | async-done | bytes 1048608 | tf_op jit(solution)/shard_map/all_to_all | solution.py:49
  50.9 2.1 %early.1 = (bf16[2048,1024]{1,0:T(8,128)(2,1)S(1)}, bf16[2048,1024]{1,0:T(8,128)(2,1)S(1)}, f32[16,64,128]{2,1,0:T(8,128)S(1)}) custom-call(s32[66]{0:T(128)S(1)} %pad_add_fusion.codes, f32[8,128,128]{2,1,0:T(8,128)S(1)} %get-tuple-element.32.kept.own0, f32[8,128,128]{2,1,0:T(8,128)S(1)} %get-tuple-element.33.kept.own1, ...), custom_call_target="tpu_custom_call" | custom-call | tf_op jit(solution)/shard_map/early/pallas_call | solution.py:126
  53.2 3.5 %late.1 = (bf16[2048,1024]{1,0:T(8,128)(2,1)S(1)}, bf16[2048,1024]{1,0:T(8,128)(2,1)S(1)}) custom-call(s32[66]{0:T(128)S(1)} %pad_add_fusion.codes, f32[16,128,128]{2,1,0:T(8,128)} %collective-permute-done.1.wave_in, f32[16,128,128]{2,1,0:T(8,128)} %collective-permute-done.3.back_in, bf16[2048,1024]{1,0:T(8,128)(2,1)S(1)} %get-tuple-element.34.hi0, ...), custom_call_target="tpu_custom_call" | custom-call | tf_op jit(solution)/shard_map/late/pallas_call | solution.py:137
  56.6 1.3 mate.3.after
  59.3 2.0 %mirror.3 = (f32[1024,128]{1,0:T(8,128)S(1)}, f32[8,128]{1,0:T(8,128)S(1)}) custom-call(f32[16,128,128]{2,1,0:T(8,128)S(1)} %all-to-all-done.1.recv, f32[16,64,128]{2,1,0:T(8,128)S(1)} %collective-permute-done.4.other, bf16[2048,1024]{1,0:T(8,128)(2,1)S(1)} %get-tuple-element.36.hi, bf16[2048,1024]{1,0:T(8,128)(2,1)S(1)} %get-tuple-element.37.lo, ...), custom_call_target="tpu_custom_call" | custom-call | tf_op jit(solution)/shard_map/mirror/pallas_call | solution.py:212
  62.6 21.5 %all_to_all.41.refs_0_ = f32[16,136,128]{2,1,0:T(8,128)S(1)} all-to-all(f32[16,136,128]{2,1,0:T(8,128)S(1)} %join.3), channel_id=1, replica_groups={{0,2,4,6,16,18,20,22,32,34,36,38,48,50,52,54},{1,3,5,7,17,19,21,23,33,3..., dimensions={0} | all-to-all | bytes 2228224 | tf_op jit(solution)/shard_map/all_to_all | solution.py:49
  84.3 19.5 %all_to_all.42.recv = f32[16,128,128]{2,1,0:T(8,128)S(1)} all-to-all(f32[16,128,128]{2,1,0:T(8,128)S(1)} %get-tuple-element.42), channel_id=1, replica_groups={{0,2,4,6,16,18,20,22,32,34,36,38,48,50,52,54},{1,3,5,7,17,19,21,23,33,3..., dimensions={0} | all-to-all | bytes 2097152 | tf_op jit(solution)/shard_map/all_to_all | solution.py:49
  103.8 1.3 mate.4.after
  106.5 1.9 %mirror.4 = (f32[1024,128]{1,0:T(8,128)S(1)}, f32[8,128]{1,0:T(8,128)S(1)}) custom-call(f32[16,128,128]{2,1,0:T(8,128)S(1)} %all_to_all.42.recv, f32[16,128,128]{2,1,0:T(8,128)S(1)} %collective-permute-done.7.other, bf16[2048,1024]{1,0:T(8,128)(2,1)S(1)} %get-tuple-element.36.hi, bf16[2048,1024]{1,0:T(8,128)(2,1)S(1)} %get-tuple-element.37.lo, ...), custom_call_target="tpu_custom_call" | custom-call | tf_op jit(solution)/shard_map/mirror/pallas_call | solution.py:212
  109.8 21.4 %all_to_all.43.refs_0_ = f32[16,136,128]{2,1,0:T(8,128)S(1)} all-to-all(f32[16,136,128]{2,1,0:T(8,128)S(1)} %join.4), channel_id=1, replica_groups={{0,2,4,6,16,18,20,22,32,34,36,38,48,50,52,54},{1,3,5,7,17,19,21,23,33,3..., dimensions={0} | all-to-all | bytes 2228224 | tf_op jit(solution)/shard_map/all_to_all | solution.py:49
  131.4 19.5 %all_to_all.44.recv = f32[16,128,128]{2,1,0:T(8,128)S(1)} all-to-all(f32[16,128,128]{2,1,0:T(8,128)S(1)} %get-tuple-element.51), channel_id=1, replica_groups={{0,2,4,6,16,18,20,22,32,34,36,38,48,50,52,54},{1,3,5,7,17,19,21,23,33,3..., dimensions={0} | all-to-all | bytes 2097152 | tf_op jit(solution)/shard_map/all_to_all | solution.py:49
  150.9 1.3 mate.5.after
  153.6 1.9 %mirror.5 = (f32[1024,128]{1,0:T(8,128)S(1)}, f32[8,128]{1,0:T(8,128)S(1)}) custom-call(f32[16,128,128]{2,1,0:T(8,128)S(1)} %all_to_all.44.recv, f32[16,128,128]{2,1,0:T(8,128)S(1)} %collective-permute-done.10.other, bf16[2048,1024]{1,0:T(8,128)(2,1)S(1)} %get-tuple-element.36.hi, bf16[2048,1024]{1,0:T(8,128)(2,1)S(1)} %get-tuple-element.37.lo, ...), custom_call_target="tpu_custom_call" | custom-call | tf_op jit(solution)/shard_map/mirror/pallas_call | solution.py:212
  156.9 21.4 %all_to_all.45.refs_0_ = f32[16,136,128]{2,1,0:T(8,128)S(1)} all-to-all(f32[16,136,128]{2,1,0:T(8,128)S(1)} %join.5), channel_id=1, replica_groups={{0,2,4,6,16,18,20,22,32,34,36,38,48,50,52,54},{1,3,5,7,17,19,21,23,33,3..., dimensions={0} | all-to-all | bytes 2228224 | tf_op jit(solution)/shard_map/all_to_all | solution.py:49
  178.4 13.2 %all_to_all.46.recv = f32[16,2,16,128]{3,2,1,0:T(8,128)S(1)} all-to-all(f32[16,2,16,128]{3,2,1,0:T(8,128)S(1)} %update.5), channel_id=1, replica_groups={{0,2,4,6,8,10,12,14,64,66,68,70,72,74,76,78},{1,3,5,7,9,11,13,15,65,67,..., dimensions={0} | all-to-all | bytes 524288 | tf_op jit(solution)/shard_map/all_to_all | solution.py:49
  (64 shorter events, 11.2 us)
Async XLA Ops:
  0.6 1.2 copy-start
  1.9 3.4 %copy-start.4 = (s32[2,1]{0,1:T(1,128)S(1)}, s32[2,1]{0,1:T(1,128)}, u32[]{:S(2)}) copy-start(s32[2,1]{0,1:T(1,128)} %param.7) | copy-start | bytes 28
  1.9 3.7 %copy-start.3 = (s32[2,1,8,2]{2,3,1,0:T(2,128)S(1)}, s32[2,1,8,2]{2,3,1,0:T(2,128)}, u32[]{:S(2)}) copy-start(s32[2,1,8,2]{2,3,1,0:T(2,128)} %param.6) | copy-start | bytes 388
  1.9 3.9 %copy-start.2 = (f32[1,64,512]{2,1,0:T(8,128)S(1)}, f32[1,64,512]{2,1,0:T(8,128)}, u32[]{:S(2)}) copy-start(f32[1,64,512]{2,1,0:T(8,128)} %param.4) | copy-start | bytes 393220
  2.0 21.6 %collective-permute-start = (f32[8,128,128]{2,1,0:T(8,128)S(1)}, f32[8,128,128]{2,1,0:T(8,128)S(1)}, u32[]{:S(2)}, u32[]{:S(2)}) collective-permute-start(f32[8,128,128]{2,1,0:T(8,128)S(1)} %get-tuple-element.32.kept.own0), channel_id=1, source_target_pairs={{0,8},{1,9},{2,10},{3,11},{4,12},{5,13},{6,14},{7,15},{8,64},{9,65... | collective-permute-start | bytes 1572872 | tf_op jit(solution)/shard_map/ppermute | solution.py:444
  3.7 21.9 %collective-permute-start.2 = (f32[8,128,128]{2,1,0:T(8,128)S(1)}, f32[8,128,128]{2,1,0:T(8,128)S(1)}, u32[]{:S(2)}, u32[]{:S(2)}) collective-permute-start(f32[8,128,128]{2,1,0:T(8,128)S(1)} %get-tuple-element.33.kept.own1), channel_id=1, source_target_pairs={{0,72},{1,73},{2,74},{3,75},{4,76},{5,77},{6,78},{7,79},{8,0},{9,1... | collective-permute-start | bytes 1572872 | tf_op jit(solution)/shard_map/ppermute | solution.py:445
  24.5 28.6 %collective-permute-start.1 = (f32[16,128,128]{2,1,0:T(8,128)}, f32[16,128,128]{2,1,0:T(8,128)}, u32[]{:S(2)}, u32[]{:S(2)}) collective-permute-start(f32[16,128,128]{2,1,0:T(8,128)} %pack.2), channel_id=1, source_target_pairs={{0,8},{1,9},{2,10},{3,11},{4,12},{5,13},{6,14},{7,15},{8,64},{9,65... | collective-permute-start | bytes 3145736 | tf_op jit(solution)/shard_map/ppermute | solution.py:468
  26.6 26.5 %collective-permute-start.3 = (f32[16,128,128]{2,1,0:T(8,128)}, f32[16,128,128]{2,1,0:T(8,128)}, u32[]{:S(2)}, u32[]{:S(2)}) collective-permute-start(f32[16,128,128]{2,1,0:T(8,128)} %pack.3), channel_id=1, source_target_pairs={{0,72},{1,73},{2,74},{3,75},{4,76},{5,77},{6,78},{7,79},{8,0},{9,1... | collective-permute-start | bytes 3145736 | tf_op jit(solution)/shard_map/ppermute | solution.py:469
  29.0 1.0 copy-start.1
  30.0 20.9 %all-to-all-start.1 = ((f32[16,128,128]{2,1,0:T(8,128)}), f32[16,128,128]{2,1,0:T(8,128)S(1)}, u32[]{:S(2)}, u32[]{:S(2)}) async-start(f32[16,128,128]{2,1,0:T(8,128)} %copy-done.1), calls=%async_computation.1 | async-start | bytes 2097152 | tf_op jit(solution)/shard_map/all_to_all | solution.py:49
  53.1 6.3 %collective-permute-start.4 = (f32[16,64,128]{2,1,0:T(8,128)S(1)}, f32[16,64,128]{2,1,0:T(8,128)S(1)}, u32[]{:S(2)}, u32[]{:S(2)}) collective-permute-start(f32[16,64,128]{2,1,0:T(8,128)S(1)} %get-tuple-element.38), channel_id=1, source_target_pairs={{0,1},{1,0},{2,3},{3,2},{4,5},{5,4},{6,7},{7,6},{8,9},{9,8},{10,11... | collective-permute-start | bytes 1572872 | tf_op jit(solution)/shard_map/ppermute | solution.py:264
  58.0 4.6 %collective-permute-start.5 = (f32[1024,128]{1,0:T(8,128)S(1)}, f32[1024,128]{1,0:T(8,128)S(1)}, u32[]{:S(2)}, u32[]{:S(2)}) collective-permute-start(f32[1024,128]{1,0:T(8,128)S(1)} %mate.3.after), channel_id=1, source_target_pairs={{0,1},{1,0},{2,3},{3,2},{4,5},{5,4},{6,7},{7,6},{8,9},{9,8},{10,11... | collective-permute-start | bytes 1572872 | tf_op jit(solution)/shard_map/ppermute | solution.py:266
  61.3 1.2 collective-permute-start.6
  103.8 2.7 %collective-permute-start.7 = (f32[16,128,128]{2,1,0:T(8,128)S(1)}, f32[16,128,128]{2,1,0:T(8,128)S(1)}, u32[]{:S(2)}, u32[]{:S(2)}) collective-permute-start(f32[16,128,128]{2,1,0:T(8,128)S(1)} %all_to_all.42.recv), channel_id=1, source_target_pairs={{0,1},{1,0},{2,3},{3,2},{4,5},{5,4},{6,7},{7,6},{8,9},{9,8},{10,11... | collective-permute-start | bytes 3145736 | tf_op jit(solution)/shard_map/ppermute | solution.py:264
  105.2 4.3 %collective-permute-start.8 = (f32[1024,128]{1,0:T(8,128)S(1)}, f32[1024,128]{1,0:T(8,128)S(1)}, u32[]{:S(2)}, u32[]{:S(2)}) collective-permute-start(f32[1024,128]{1,0:T(8,128)S(1)} %mate.4.after), channel_id=1, source_target_pairs={{0,1},{1,0},{2,3},{3,2},{4,5},{5,4},{6,7},{7,6},{8,9},{9,8},{10,11... | collective-permute-start | bytes 1572872 | tf_op jit(solution)/shard_map/ppermute | solution.py:266
  108.5 1.2 collective-permute-start.9
  150.9 2.7 %collective-permute-start.10 = (f32[16,128,128]{2,1,0:T(8,128)S(1)}, f32[16,128,128]{2,1,0:T(8,128)S(1)}, u32[]{:S(2)}, u32[]{:S(2)}) collective-permute-start(f32[16,128,128]{2,1,0:T(8,128)S(1)} %all_to_all.44.recv), channel_id=1, source_target_pairs={{0,1},{1,0},{2,3},{3,2},{4,5},{5,4},{6,7},{7,6},{8,9},{9,8},{10,11... | collective-permute-start | bytes 3145736 | tf_op jit(solution)/shard_map/ppermute | solution.py:264
  152.2 4.3 %collective-permute-start.11 = (f32[1024,128]{1,0:T(8,128)S(1)}, f32[1024,128]{1,0:T(8,128)S(1)}, u32[]{:S(2)}, u32[]{:S(2)}) collective-permute-start(f32[1024,128]{1,0:T(8,128)S(1)} %mate.5.after), channel_id=1, source_target_pairs={{0,1},{1,0},{2,3},{3,2},{4,5},{5,4},{6,7},{7,6},{8,9},{9,8},{10,11... | collective-permute-start | bytes 1572872 | tf_op jit(solution)/shard_map/ppermute | solution.py:266
  155.5 1.2 collective-permute-start.12

commit v10 on v8

--- a/solution.py
+++ b/solution.py
@@ -49,7 +49,7 @@
     return lax.all_to_all(send, RC, 0, 0, axis_index_groups=groups, tiled=True)
 
 
-def call(body, limit=16, **kw):
+def call(body, limit=10, **kw):
     return pl.pallas_call(
         body, compiler_params=pltpu.CompilerParams(vmem_limit_bytes=limit * 2**20), **kw
     )

time: 192 us -> 192 us (level)
  no operation moved by 1% of the time
where the time goes in v10:
time: 192 us
  blocking collectives  134 us (70%)
  Pallas kernels  22.9 us (12%)
  waiting for transfers between devices  16.1 us (8%)
  starting transfers between devices  14.3 us (7%)
  local copies, waits for them, and re-layouts  2.82 us (1%)
    all_to_all x7, blocking collectives, exchange(): return lax.all_to_all(send, RC, 0, 0, axis_index_groups=groups, tiled=True)  134 us
    all_to_all x1, waiting for transfers between devices, exchange(): return lax.all_to_all(send, RC, 0, 0, axis_index_groups=groups, tiled=True)  15.2 us
    pallas_call x3, Pallas kernels, mirror(): call(mirror_body, out_shape=(jax.ShapeDtypeStruct((1024, 128), jnp.float3...  5.82 us
    all_to_all x1, starting transfers between devices, exchange(): return lax.all_to_all(send, RC, 0, 0, axis_index_groups=groups, tiled=True)  5.44 us
    pallas_call x6, Pallas kernels, own_rows(): call(functools.partial(own_body, first), out_shape=jax.ShapeDtypeStruct((...  4.58 us
    pallas_call x3, Pallas kernels, mate(): call(mate_body, out_shape=jax.ShapeDtypeStruct((1024, 128), jnp.float32),...  3.94 us
  transfers between devices with their start and end apart: 14, of which 4 were waited for; matrix products, arithmetic and copies ran while one was open for 0% of the time, Pallas kernels for 10%

profile of v10, /device:TPU:0, one launch (start us, length us, event | category | flops | bytes accessed | tf_op | source)
XLA Modules:
  0.0 191.7 jit_solution(12429478385476679846)
XLA Ops:
  0.6 1.2 copy-done
  2.0 1.7 collective-permute-start
  3.7 1.6 collective-permute-start.1
  6.0 17.6 %all_to_all.40.recv.refs_1_ = f32[16,24,128]{2,1,0:T(8,128)S(1)} all-to-all(f32[16,24,128]{2,1,0:T(8,128)S(1)} %pad_maximum_fusion), channel_id=1, replica_groups={{0,2,4,6,8,10,12,14,64,66,68,70,72,74,76,78},{1,3,5,7,9,11,13,15,65,67,..., dimensions={0} | all-to-all | bytes 393216 | tf_op jit(solution)/shard_map/all_to_all | solution.py:49
  23.6 1.4 pack.1
  24.9 1.1 collective-permute-start.2
  26.0 2.2 %collective-permute-start.3 = (f32[16,128,128]{2,1,0:T(8,128)}, f32[16,128,128]{2,1,0:T(8,128)}, u32[]{:S(2)}, u32[]{:S(2)}) collective-permute-start(f32[16,128,128]{2,1,0:T(8,128)} %get-tuple-element.37), channel_id=1, source_target_pairs={{0,72},{1,73},{2,74},{3,75},{4,76},{5,77},{6,78},{7,79},{8,0},{9,1... | collective-permute-start | bytes 3145736 | tf_op jit(solution)/shard_map/ppermute | solution.py:470
  28.3 1.0 copy-done.1
  29.3 5.4 %all-to-all-start.1 = ((f32[16,128,128]{2,1,0:T(8,128)}), f32[16,128,128]{2,1,0:T(8,128)S(1)}, u32[]{:S(2)}, u32[]{:S(2)}) async-start(f32[16,128,128]{2,1,0:T(8,128)} %copy-done.1), calls=%async_computation.1 | async-start | bytes 2097152 | tf_op jit(solution)/shard_map/all_to_all | solution.py:49
  35.0 15.2 %all-to-all-done.1.recv = f32[16,128,128]{2,1,0:T(8,128)S(1)} async-done(((f32[16,128,128]{2,1,0:T(8,128)}), f32[16,128,128]{2,1,0:T(8,128)S(1)}, u32[]{:S(2)}, u32[]{:S(2)}) %all-to-all-start.1) | async-done | bytes 1048608 | tf_op jit(solution)/shard_map/all_to_all | solution.py:49
  50.2 2.1 %early.1 = (bf16[2048,1024]{1,0:T(8,128)(2,1)S(1)}, bf16[2048,1024]{1,0:T(8,128)(2,1)S(1)}, f32[16,64,128]{2,1,0:T(8,128)S(1)}) custom-call(s32[66]{0:T(128)S(1)} %pad_add_fusion.codes, f32[8,128,128]{2,1,0:T(8,128)S(1)} %get-tuple-element.34.own0, f32[8,128,128]{2,1,0:T(8,128)S(1)} %get-tuple-element.35.own1, ...), custom_call_target="tpu_custom_call" | custom-call | tf_op jit(solution)/shard_map/early/pallas_call | solution.py:126
  52.5 3.5 %late.1 = (bf16[2048,1024]{1,0:T(8,128)(2,1)S(1)}, bf16[2048,1024]{1,0:T(8,128)(2,1)S(1)}) custom-call(s32[66]{0:T(128)S(1)} %pad_add_fusion.codes, f32[16,128,128]{2,1,0:T(8,128)} %collective-permute-done.2.wave_in, f32[16,128,128]{2,1,0:T(8,128)} %collective-permute-done.3.back_in, bf16[2048,1024]{1,0:T(8,128)(2,1)S(1)} %get-tuple-element.38.hi0, ...), custom_call_target="tpu_custom_call" | custom-call | tf_op jit(solution)/shard_map/late/pallas_call | solution.py:137
  56.0 1.3 mate.3.after
  58.6 2.0 %mirror.3 = (f32[1024,128]{1,0:T(8,128)S(1)}, f32[8,128]{1,0:T(8,128)S(1)}) custom-call(f32[16,128,128]{2,1,0:T(8,128)S(1)} %all-to-all-done.1.recv, f32[16,64,128]{2,1,0:T(8,128)S(1)} %collective-permute-done.4.other, bf16[2048,1024]{1,0:T(8,128)(2,1)S(1)} %get-tuple-element.40.hi, bf16[2048,1024]{1,0:T(8,128)(2,1)S(1)} %get-tuple-element.41.lo, ...), custom_call_target="tpu_custom_call" | custom-call | tf_op jit(solution)/shard_map/mirror/pallas_call | solution.py:212
  61.9 21.5 %all_to_all.41.refs_0_ = f32[16,136,128]{2,1,0:T(8,128)S(1)} all-to-all(f32[16,136,128]{2,1,0:T(8,128)S(1)} %join.3), channel_id=1, replica_groups={{0,2,4,6,16,18,20,22,32,34,36,38,48,50,52,54},{1,3,5,7,17,19,21,23,33,3..., dimensions={0} | all-to-all | bytes 2228224 | tf_op jit(solution)/shard_map/all_to_all | solution.py:49
  83.6 19.5 %all_to_all.42.recv = f32[16,128,128]{2,1,0:T(8,128)S(1)} all-to-all(f32[16,128,128]{2,1,0:T(8,128)S(1)} %get-tuple-element.46), channel_id=1, replica_groups={{0,2,4,6,16,18,20,22,32,34,36,38,48,50,52,54},{1,3,5,7,17,19,21,23,33,3..., dimensions={0} | all-to-all | bytes 2097152 | tf_op jit(solution)/shard_map/all_to_all | solution.py:49
  103.1 1.3 mate.4.after
  105.8 1.9 %mirror.4 = (f32[1024,128]{1,0:T(8,128)S(1)}, f32[8,128]{1,0:T(8,128)S(1)}) custom-call(f32[16,128,128]{2,1,0:T(8,128)S(1)} %all_to_all.42.recv, f32[16,128,128]{2,1,0:T(8,128)S(1)} %collective-permute-done.7.other, bf16[2048,1024]{1,0:T(8,128)(2,1)S(1)} %get-tuple-element.40.hi, bf16[2048,1024]{1,0:T(8,128)(2,1)S(1)} %get-tuple-element.41.lo, ...), custom_call_target="tpu_custom_call" | custom-call | tf_op jit(solution)/shard_map/mirror/pallas_call | solution.py:212
  109.1 21.4 %all_to_all.43.refs_0_ = f32[16,136,128]{2,1,0:T(8,128)S(1)} all-to-all(f32[16,136,128]{2,1,0:T(8,128)S(1)} %join.4), channel_id=1, replica_groups={{0,2,4,6,16,18,20,22,32,34,36,38,48,50,52,54},{1,3,5,7,17,19,21,23,33,3..., dimensions={0} | all-to-all | bytes 2228224 | tf_op jit(solution)/shard_map/all_to_all | solution.py:49
  130.7 19.5 %all_to_all.44.recv = f32[16,128,128]{2,1,0:T(8,128)S(1)} all-to-all(f32[16,128,128]{2,1,0:T(8,128)S(1)} %get-tuple-element.55), channel_id=1, replica_groups={{0,2,4,6,16,18,20,22,32,34,36,38,48,50,52,54},{1,3,5,7,17,19,21,23,33,3..., dimensions={0} | all-to-all | bytes 2097152 | tf_op jit(solution)/shard_map/all_to_all | solution.py:49
  150.2 1.3 mate.5.after
  152.9 1.9 %mirror.5 = (f32[1024,128]{1,0:T(8,128)S(1)}, f32[8,128]{1,0:T(8,128)S(1)}) custom-call(f32[16,128,128]{2,1,0:T(8,128)S(1)} %all_to_all.44.recv, f32[16,128,128]{2,1,0:T(8,128)S(1)} %collective-permute-done.10.other, bf16[2048,1024]{1,0:T(8,128)(2,1)S(1)} %get-tuple-element.40.hi, bf16[2048,1024]{1,0:T(8,128)(2,1)S(1)} %get-tuple-element.41.lo, ...), custom_call_target="tpu_custom_call" | custom-call | tf_op jit(solution)/shard_map/mirror/pallas_call | solution.py:212
  156.2 21.4 %all_to_all.45.refs_0_ = f32[16,136,128]{2,1,0:T(8,128)S(1)} all-to-all(f32[16,136,128]{2,1,0:T(8,128)S(1)} %join.5), channel_id=1, replica_groups={{0,2,4,6,16,18,20,22,32,34,36,38,48,50,52,54},{1,3,5,7,17,19,21,23,33,3..., dimensions={0} | all-to-all | bytes 2228224 | tf_op jit(solution)/shard_map/all_to_all | solution.py:49
  177.7 13.3 %all_to_all.46.recv = f32[16,2,16,128]{3,2,1,0:T(8,128)S(1)} all-to-all(f32[16,2,16,128]{3,2,1,0:T(8,128)S(1)} %update.5), channel_id=1, replica_groups={{0,2,4,6,8,10,12,14,64,66,68,70,72,74,76,78},{1,3,5,7,9,11,13,15,65,67,..., dimensions={0} | all-to-all | bytes 524288 | tf_op jit(solution)/shard_map/all_to_all | solution.py:49
  (63 shorter events, 10.2 us)
Async XLA Ops:
  0.6 1.2 copy-start
  1.9 3.4 %copy-start.4 = (s32[2,1]{0,1:T(1,128)S(1)}, s32[2,1]{0,1:T(1,128)}, u32[]{:S(2)}) copy-start(s32[2,1]{0,1:T(1,128)} %param.7) | copy-start | bytes 28
  1.9 3.7 %copy-start.3 = (s32[2,1,8,2]{2,3,1,0:T(2,128)S(1)}, s32[2,1,8,2]{2,3,1,0:T(2,128)}, u32[]{:S(2)}) copy-start(s32[2,1,8,2]{2,3,1,0:T(2,128)} %param.6) | copy-start | bytes 388
  1.9 3.9 %copy-start.2 = (f32[1,64,512]{2,1,0:T(8,128)S(1)}, f32[1,64,512]{2,1,0:T(8,128)}, u32[]{:S(2)}) copy-start(f32[1,64,512]{2,1,0:T(8,128)} %param.4) | copy-start | bytes 393220
  2.0 21.6 %collective-permute-start = (f32[8,128,128]{2,1,0:T(8,128)S(1)}, f32[8,128,128]{2,1,0:T(8,128)S(1)}, u32[]{:S(2)}, u32[]{:S(2)}) collective-permute-start(f32[8,128,128]{2,1,0:T(8,128)S(1)} %get-tuple-element.34.own0), channel_id=1, source_target_pairs={{0,8},{1,9},{2,10},{3,11},{4,12},{5,13},{6,14},{7,15},{8,64},{9,65... | collective-permute-start | bytes 1572872 | tf_op jit(solution)/shard_map/ppermute | solution.py:446
  3.7 19.9 %collective-permute-start.1 = (f32[8,128,128]{2,1,0:T(8,128)S(1)}, f32[8,128,128]{2,1,0:T(8,128)S(1)}, u32[]{:S(2)}, u32[]{:S(2)}) collective-permute-start(f32[8,128,128]{2,1,0:T(8,128)S(1)} %get-tuple-element.35.own1), channel_id=1, source_target_pairs={{0,72},{1,73},{2,74},{3,75},{4,76},{5,77},{6,78},{7,79},{8,0},{9,1... | collective-permute-start | bytes 1572872 | tf_op jit(solution)/shard_map/ppermute | solution.py:447
  24.9 27.5 %collective-permute-start.2 = (f32[16,128,128]{2,1,0:T(8,128)}, f32[16,128,128]{2,1,0:T(8,128)}, u32[]{:S(2)}, u32[]{:S(2)}) collective-permute-start(f32[16,128,128]{2,1,0:T(8,128)} %get-tuple-element.36), channel_id=1, source_target_pairs={{0,8},{1,9},{2,10},{3,11},{4,12},{5,13},{6,14},{7,15},{8,64},{9,65... | collective-permute-start | bytes 3145736 | tf_op jit(solution)/shard_map/ppermute | solution.py:469
  26.0 26.5 %collective-permute-start.3 = (f32[16,128,128]{2,1,0:T(8,128)}, f32[16,128,128]{2,1,0:T(8,128)}, u32[]{:S(2)}, u32[]{:S(2)}) collective-permute-start(f32[16,128,128]{2,1,0:T(8,128)} %get-tuple-element.37), channel_id=1, source_target_pairs={{0,72},{1,73},{2,74},{3,75},{4,76},{5,77},{6,78},{7,79},{8,0},{9,1... | collective-permute-start | bytes 3145736 | tf_op jit(solution)/shard_map/ppermute | solution.py:470
  28.3 1.0 copy-start.1
  29.3 20.9 %all-to-all-start.1 = ((f32[16,128,128]{2,1,0:T(8,128)}), f32[16,128,128]{2,1,0:T(8,128)S(1)}, u32[]{:S(2)}, u32[]{:S(2)}) async-start(f32[16,128,128]{2,1,0:T(8,128)} %copy-done.1), calls=%async_computation.1 | async-start | bytes 2097152 | tf_op jit(solution)/shard_map/all_to_all | solution.py:49
  52.4 6.2 %collective-permute-start.4 = (f32[16,64,128]{2,1,0:T(8,128)S(1)}, f32[16,64,128]{2,1,0:T(8,128)S(1)}, u32[]{:S(2)}, u32[]{:S(2)}) collective-permute-start(f32[16,64,128]{2,1,0:T(8,128)S(1)} %get-tuple-element.42), channel_id=1, source_target_pairs={{0,1},{1,0},{2,3},{3,2},{4,5},{5,4},{6,7},{7,6},{8,9},{9,8},{10,11... | collective-permute-start | bytes 1572872 | tf_op jit(solution)/shard_map/ppermute | solution.py:264
  57.3 4.5 %collective-permute-start.5 = (f32[1024,128]{1,0:T(8,128)S(1)}, f32[1024,128]{1,0:T(8,128)S(1)}, u32[]{:S(2)}, u32[]{:S(2)}) collective-permute-start(f32[1024,128]{1,0:T(8,128)S(1)} %mate.3.after), channel_id=1, source_target_pairs={{0,1},{1,0},{2,3},{3,2},{4,5},{5,4},{6,7},{7,6},{8,9},{9,8},{10,11... | collective-permute-start | bytes 1572872 | tf_op jit(solution)/shard_map/ppermute | solution.py:266
  60.6 1.2 collective-permute-start.6
  103.1 2.7 %collective-permute-start.7 = (f32[16,128,128]{2,1,0:T(8,128)S(1)}, f32[16,128,128]{2,1,0:T(8,128)S(1)}, u32[]{:S(2)}, u32[]{:S(2)}) collective-permute-start(f32[16,128,128]{2,1,0:T(8,128)S(1)} %all_to_all.42.recv), channel_id=1, source_target_pairs={{0,1},{1,0},{2,3},{3,2},{4,5},{5,4},{6,7},{7,6},{8,9},{9,8},{10,11... | collective-permute-start | bytes 3145736 | tf_op jit(solution)/shard_map/ppermute | solution.py:264
  104.4 4.3 %collective-permute-start.8 = (f32[1024,128]{1,0:T(8,128)S(1)}, f32[1024,128]{1,0:T(8,128)S(1)}, u32[]{:S(2)}, u32[]{:S(2)}) collective-permute-start(f32[1024,128]{1,0:T(8,128)S(1)} %mate.4.after), channel_id=1, source_target_pairs={{0,1},{1,0},{2,3},{3,2},{4,5},{5,4},{6,7},{7,6},{8,9},{9,8},{10,11... | collective-permute-start | bytes 1572872 | tf_op jit(solution)/shard_map/ppermute | solution.py:266
  107.7 1.2 collective-permute-start.9
  150.2 2.7 %collective-permute-start.10 = (f32[16,128,128]{2,1,0:T(8,128)S(1)}, f32[16,128,128]{2,1,0:T(8,128)S(1)}, u32[]{:S(2)}, u32[]{:S(2)}) collective-permute-start(f32[16,128,128]{2,1,0:T(8,128)S(1)} %all_to_all.44.recv), channel_id=1, source_target_pairs={{0,1},{1,0},{2,3},{3,2},{4,5},{5,4},{6,7},{7,6},{8,9},{9,8},{10,11... | collective-permute-start | bytes 3145736 | tf_op jit(solution)/shard_map/ppermute | solution.py:264
  151.5 4.3 %collective-permute-start.11 = (f32[1024,128]{1,0:T(8,128)S(1)}, f32[1024,128]{1,0:T(8,128)S(1)}, u32[]{:S(2)}, u32[]{:S(2)}) collective-permute-start(f32[1024,128]{1,0:T(8,128)S(1)} %mate.5.after), channel_id=1, source_target_pairs={{0,1},{1,0},{2,3},{3,2},{4,5},{5,4},{6,7},{7,6},{8,9},{9,8},{10,11... | collective-permute-start | bytes 1572872 | tf_op jit(solution)/shard_map/ppermute | solution.py:266
  154.8 1.2 collective-permute-start.12
